TPU v7x, 32 devices: a whole 2x2x4 slice. The times are simulated.
32 devices in a mesh: row: 8 (over y, x, core), col: 4 (over z).
Axes of the slice: x: 2, y: 2, z: 4, core: 2. Of those that a mesh axis runs over, the one named last changes fastest.
Arguments:
- probes: float32 [16384, 256], P(('row', 'col')), may hold values from -6 to 6
- spectrum: float32 [32, 512], P(('row', 'col')), may hold values from 0.5 to 4
Outputs:
- leaf_basis: float32 [16384, 256], P(('row', 'col'))
- leaf_transfer: float32 [8192, 256], P(('row', 'col'))
- pair_transfer: float32 [4096, 256], P(('row', 'col'))
- group_factor: float32 [2048, 256], P(('row', 'col'))
All inputs are finite; a program needn't handle non-finite values.
Results may differ from a plain program's by a relative error of at most 0.000076.
Values sent between devices are 32-bit elements; how exact they have to be, the bound alone decides.
No kernel may reach another device: no remote copies, remote signals or barrier semaphores. Data moves between devices by JAX's collectives and lax.ppermute only.
A program may use at most 64 MiB of HBM per device.

v0:
```python
import math

import jax
import jax.numpy as jnp
from jax import lax
from jax.sharding import PartitionSpec as P


def partner(value, axis, distance):
    mask = 2**distance
    pairs = [(source, source ^ mask) for source in range(lax.axis_size(axis))]
    return lax.ppermute(value, axis, pairs)


def circle(product, length):
    angle = 2.0 * math.pi / length * (product % length).astype(jnp.float32)
    return (jnp.cos(angle), jnp.sin(angle))


def lower_solve(low, rhs):
    return jax.scipy.linalg.solve_triangular(low, rhs, lower=True)


def matmul(left, right):
    return jnp.dot(left, right, precision=lax.Precision.HIGHEST)


def local(probes, spectrum):
    rows_dev, width = probes.shape
    n_row = lax.axis_size("row")
    n_col = lax.axis_size("col")
    devices = n_row * n_col
    slab = rows_dev // devices
    total = rows_dev * devices
    col_index = lax.axis_index("col")
    flat = lax.axis_index("row") * n_col + col_index
    highest = lax.Precision.HIGHEST
    spread = lax.all_to_all(
        probes.reshape(1, rows_dev, width), ("row", "col"), split_axis=1, concat_axis=0, tiled=True
    )
    small_index = jnp.arange(devices, dtype=jnp.int32)
    cos_small, sin_small = circle(small_index[:, None] * small_index[None, :], devices)
    real_first = jnp.einsum("ka,abr->kbr", cos_small, spread, precision=highest)
    imag_first = -jnp.einsum("ka,abr->kbr", sin_small, spread, precision=highest)
    local_rows = flat * slab + jnp.arange(slab, dtype=jnp.int32)
    cos_turn, sin_turn = circle(small_index[:, None] * local_rows[None, :], total)
    cos_turn = cos_turn[:, :, None]
    sin_turn = sin_turn[:, :, None]
    turned = jnp.stack(
        [
            real_first * cos_turn + imag_first * sin_turn,
            imag_first * cos_turn - real_first * sin_turn,
        ]
    )
    columns = lax.all_to_all(turned, ("row", "col"), split_axis=1, concat_axis=2, tiled=True)
    columns = columns.reshape(2, rows_dev, width)
    big_index = jnp.arange(rows_dev, dtype=jnp.int32)
    cos_big, sin_big = circle(big_index[:, None] * big_index[None, :], rows_dev)
    real_col, imag_col = (columns[0], columns[1])
    symbol = spectrum[0][:, None]
    real_spec = (matmul(cos_big, real_col) + matmul(sin_big, imag_col)) * symbol
    imag_spec = (matmul(cos_big, imag_col) - matmul(sin_big, real_col)) * symbol
    real_back = matmul(cos_big, real_spec) - matmul(sin_big, imag_spec)
    imag_back = matmul(cos_big, imag_spec) + matmul(sin_big, real_spec)
    cos_back, sin_back = circle(big_index * flat, total)
    cos_back = cos_back[:, None]
    sin_back = sin_back[:, None]
    returned = jnp.stack(
        [real_back * cos_back - imag_back * sin_back, imag_back * cos_back + real_back * sin_back]
    )
    spectra = lax.all_to_all(
        returned.reshape(2, 1, rows_dev, width),
        ("row", "col"),
        split_axis=2,
        concat_axis=1,
        tiled=True,
    )
    partial_sample = (
        jnp.einsum("ak,kbr->abr", cos_small, spectra[0], precision=highest)
        - jnp.einsum("ak,kbr->abr", sin_small, spectra[1], precision=highest)
    ) / total
    sample = lax.all_to_all(partial_sample, ("row", "col"), split_axis=0, concat_axis=1, tiled=True)
    sample = sample.reshape(rows_dev, width)
    leaf_gram = matmul(sample.T, sample) / rows_dev
    leaf_low = jnp.linalg.cholesky(leaf_gram)
    leaf_basis = lower_solve(leaf_low, sample.T).T
    pair_gram = leaf_gram + partner(leaf_gram, "col", 0)
    group_gram = pair_gram + partner(pair_gram, "col", 1)
    pair_low = jnp.linalg.cholesky(pair_gram)
    leaf_transfer = lower_solve(pair_low, leaf_low).T
    group_low = jnp.linalg.cholesky(group_gram)
    pair_whole = lower_solve(group_low, pair_low).T
    half = width // 2
    pair_transfer = lax.dynamic_slice_in_dim(pair_whole, col_index % 2 * half, half, 0)
    quarter = width // 4
    group_factor = lax.dynamic_slice_in_dim(group_low.T, col_index % 4 * quarter, quarter, 0)
    return (leaf_basis, leaf_transfer, pair_transfer, group_factor)


def solution(mesh):
    placed = (P(("row", "col"), None), P(("row", "col"), None))
    return jax.shard_map(
        local,
        mesh=mesh,
        in_specs=placed,
        out_specs=(
            P(("row", "col"), None),
            P(("row", "col"), None),
            P(("row", "col"), None),
            P(("row", "col"), None),
        ),
        check_vma=False,
    )
```

profile of v0, /device:TPU:0, one launch (start us, length us, event | category | flops | bytes accessed | tf_op | source)
XLA Modules:
  0.0 351.0 jit_solution(7423663234639681763)
XLA Ops:
  2.8 7.3 %all-to-all-start = ((f32[1,512,256]{2,0,1:T(1,128)}), f32[1,512,256]{2,0,1:T(1,128)S(1)}, u32[]{:S(2)}, u32[]{:S(2)}) async-start(f32[1,512,256]{2,0,1:T(1,128)} %reshape.142), calls=%async_computation | async-start | bytes 1048576 | tf_op jit(solution)/shard_map/all_to_all | solution.py:38
  10.3 14.2 %all-to-all-done = f32[1,512,256]{2,0,1:T(1,128)S(1)} async-done(((f32[1,512,256]{2,0,1:T(1,128)}), f32[1,512,256]{2,0,1:T(1,128)S(1)}, u32[]{:S(2)}, u32[]{:S(2)}) %all-to-all-start) | async-done | bytes 524320 | tf_op jit(solution)/shard_map/all_to_all | solution.py:38
  32.5 25.0 %all-to-all-done.1 = f32[2,32,16,256]{3,2,0,1:T(8,128)S(1)} async-done(((f32[2,32,16,256]{3,2,0,1:T(8,128)}), f32[2,32,16,256]{3,2,0,1:T(8,128)S(1)}, u32[]{:S(2)}, u32[]{:S(2)}) %all-to-all-start.1) | async-done | bytes 1048608 | tf_op jit(solution)/shard_map/all_to_all | solution.py:55
  57.6 5.6 %fusion.21 = f32[512,256]{1,0:T(8,128)S(1)} fusion(f32[512,256]{1,0:T(8,128)S(1)} %bitcast.154), kind=kOutput, calls=%fused_computation.45 | convolution fusion | flops 808976384 | bytes 1048576 | tf_op jit(solution)/shard_map/dot_general | solution.py:25
  63.2 5.6 %fusion.17 = f32[512,256]{1,0:T(8,128)S(1)} fusion(f32[512,256]{1,0:T(8,128)S(1)} %bitcast.156), kind=kOutput, calls=%fused_computation.43 | convolution fusion | flops 808976384 | bytes 1048576 | tf_op jit(solution)/shard_map/dot_general | solution.py:25
  68.8 5.6 %fusion = f32[512,256]{1,0:T(8,128)S(1)} fusion(f32[512,256]{1,0:T(8,128)S(1)} %fusion.21, f32[512,256]{1,0:T(8,128)S(1)} %bitcast.157, f32[512]{0:T(512)S(1)} %bitcast.158), kind=kOutput, calls=%fused_computation.13 | convolution fusion | flops 809238528 | bytes 1574912 | tf_op jit(solution)/shard_map/dot_general | solution.py:25
  74.5 5.6 %fusion.1 = f32[512,256]{1,0:T(8,128)S(1)} fusion(f32[512,256]{1,0:T(8,128)S(1)} %fusion.17, f32[512,256]{1,0:T(8,128)S(1)} %bitcast.155, f32[512]{0:T(512)S(1)} %bitcast.159), kind=kOutput, calls=%fused_computation.14 | convolution fusion | flops 809238528 | bytes 1574912 | tf_op jit(solution)/shard_map/dot_general | solution.py:25
  80.1 5.6 %fusion.15 = f32[512,256]{1,0:T(8,128)S(1)} fusion(f32[512,256]{1,0:T(8,128)S(1)} %fusion.1), kind=kOutput, calls=%fused_computation.42 | convolution fusion | flops 808976384 | bytes 1048576 | tf_op jit(solution)/shard_map/dot_general | solution.py:25
  91.4 5.6 %convolution_add_fusion = f32[512,256]{1,0:T(8,128)S(1)} fusion(f32[512,256]{1,0:T(8,128)S(1)} %fusion.15, f32[512,256]{1,0:T(8,128)S(1)} %fusion), kind=kOutput, calls=%fused_computation.9 | convolution fusion | flops 809107456 | bytes 1572864 | tf_op jit(solution)/shard_map/dot_general | solution.py:25
  97.0 7.2 %subtract_bitcast_fusion = (f32[1,512,256]{2,1,0:T(8,128)S(1)}, f32[1,512,256]{2,1,0:T(8,128)S(1)}) fusion(f32[512,256]{1,0:T(8,128)S(1)} %convolution_add_fusion, f32[512]{0:T(512)S(1)} %get-tuple-element.108, f32[512]{0:T(512)S(1)} %get-tuple-element.109, f32[512,256]{1,0:T(8,128)S(1)} %fusion.19, f32[512,256]{1,0:T(8,128)S(1)} %fusion.1), kind=kOutput, calls=%fused_computation.37 | convolution fusion | flops 809893888 | bytes 2625536 | tf_op jit(solution)/shard_map/dot_general | solution.py:25
  105.1 29.7 %all_to_all.19 = f32[2,1,512,256]{3,0,1,2:T(2,128)S(1)} all-to-all(f32[2,1,512,256]{3,0,1,2:T(2,128)S(1)} %copy.57), channel_id=1, replica_groups=mesh['row'=8,'col'=4] {'row','col'}, dimensions={2} | all-to-all | bytes 2097152 | tf_op jit(solution)/shard_map/all_to_all | solution.py:71
  143.1 14.3 %all-to-all-done.3 = f32[32,16,256]{2,1,0:T(8,128)S(1)} async-done(((f32[32,16,256]{2,1,0:T(8,128)}), f32[32,16,256]{2,1,0:T(8,128)S(1)}, u32[]{:S(2)}, u32[]{:S(2)}) %all-to-all-start.3) | async-done | bytes 524320 | tf_op jit(solution)/shard_map/all_to_all | solution.py:82
  161.3 11.7 %cholesky.172 = f32[128,128]{1,0:T(8,128)S(1)} custom-call(f32[128,128]{1,0:T(8,128)S(1)} %cholesky.270), custom_call_target="Cholesky" | custom-call | tf_op jit(solution)/shard_map/jit(cholesky)/cholesky | solution.py:85
  173.0 9.8 %custom-call.19 = f32[1,128,128]{1,2,0:T(8,128)S(1)} custom-call(f32[1,128,128]{2,1,0:T(8,128)S(1)} %get-tuple-element.101), custom_call_target="InvertDiagBlocksLowerTriangular" | custom-call | tf_op jit(solution)/shard_map/jit(cholesky)/cholesky | solution.py:85
  183.3 11.7 %cholesky.189 = f32[128,128]{1,0:T(8,128)S(1)} custom-call(f32[128,128]{1,0:T(8,128)S(1)} %convolution_subtract_fusion.6), custom_call_target="Cholesky" | custom-call | tf_op jit(solution)/shard_map/jit(cholesky)/cholesky | solution.py:85
  201.8 19.8 %custom-call.15 = f32[2,128,128]{1,2,0:T(8,128)S(1)} custom-call(f32[2,128,128]{2,1,0:T(8,128)S(1)} %get-tuple-element.21), custom_call_target="InvertDiagBlocksLowerTriangular" | custom-call | tf_op jit(solution)/shard_map/jit(_solve_triangular)/triangular_solve | solution.py:21
  225.3 11.7 %cholesky.206 = f32[128,128]{1,0:T(8,128)S(1)} custom-call(f32[128,128]{1,0:T(8,128)S(1)} %cholesky.273), custom_call_target="Cholesky" | custom-call | tf_op jit(solution)/shard_map/jit(cholesky)/cholesky | solution.py:89
  237.0 9.8 %custom-call.20 = f32[1,128,128]{1,2,0:T(8,128)S(1)} custom-call(f32[1,128,128]{2,1,0:T(8,128)S(1)} %get-tuple-element.97), custom_call_target="InvertDiagBlocksLowerTriangular" | custom-call | tf_op jit(solution)/shard_map/jit(cholesky)/cholesky | solution.py:89
  247.3 11.7 %cholesky.223 = f32[128,128]{1,0:T(8,128)S(1)} custom-call(f32[128,128]{1,0:T(8,128)S(1)} %slice_subtract_fusion.1), custom_call_target="Cholesky" | custom-call | tf_op jit(solution)/shard_map/jit(cholesky)/cholesky | solution.py:89
  265.7 19.9 %custom-call.21 = f32[2,128,128]{1,2,0:T(8,128)S(1)} custom-call(f32[2,128,128]{2,1,0:T(8,128)S(1)} %get-tuple-element.28), custom_call_target="InvertDiagBlocksLowerTriangular" | custom-call | tf_op jit(solution)/shard_map/jit(_solve_triangular)/triangular_solve | solution.py:21
  287.6 11.7 %cholesky.240 = f32[128,128]{1,0:T(8,128)S(1)} custom-call(f32[128,128]{1,0:T(8,128)S(1)} %cholesky.276), custom_call_target="Cholesky" | custom-call | tf_op jit(solution)/shard_map/jit(cholesky)/cholesky | solution.py:91
  299.4 9.8 %custom-call.22 = f32[1,128,128]{1,2,0:T(8,128)S(1)} custom-call(f32[1,128,128]{2,1,0:T(8,128)S(1)} %get-tuple-element.93), custom_call_target="InvertDiagBlocksLowerTriangular" | custom-call | tf_op jit(solution)/shard_map/jit(cholesky)/cholesky | solution.py:91
  309.9 11.7 %cholesky.257 = f32[128,128]{1,0:T(8,128)S(1)} custom-call(f32[128,128]{1,0:T(8,128)S(1)} %slice_subtract_fusion), custom_call_target="Cholesky" | custom-call | tf_op jit(solution)/shard_map/jit(cholesky)/cholesky | solution.py:91
  328.3 19.9 %custom-call.23 = f32[2,128,128]{1,2,0:T(8,128)S(1)} custom-call(f32[2,128,128]{2,1,0:T(8,128)S(1)} %get-tuple-element.29), custom_call_target="InvertDiagBlocksLowerTriangular" | custom-call | tf_op jit(solution)/shard_map/jit(_solve_triangular)/triangular_solve | solution.py:21
  (109 shorter events, 66.6 us)
Async XLA Ops:
  2.8 21.7 %all-to-all-start = ((f32[1,512,256]{2,0,1:T(1,128)}), f32[1,512,256]{2,0,1:T(1,128)S(1)}, u32[]{:S(2)}, u32[]{:S(2)}) async-start(f32[1,512,256]{2,0,1:T(1,128)} %reshape.142), calls=%async_computation | async-start | bytes 1048576 | tf_op jit(solution)/shard_map/all_to_all | solution.py:38
  28.2 29.3 %all-to-all-start.1 = ((f32[2,32,16,256]{3,2,0,1:T(8,128)}), f32[2,32,16,256]{3,2,0,1:T(8,128)S(1)}, u32[]{:S(2)}, u32[]{:S(2)}) async-start(f32[2,32,16,256]{3,2,0,1:T(8,128)} %copy.54), calls=%async_computation.1 | async-start | bytes 2097152 | tf_op jit(solution)/shard_map/all_to_all | solution.py:55
  63.2 5.6 %copy-start = (f32[1,512]{1,0:T(1,128)S(1)}, f32[1,512]{1,0:T(1,128)}, u32[]{:S(2)}) copy-start(f32[1,512]{1,0:T(1,128)} %param.6) | copy-start | bytes 6148
  138.6 18.8 %all-to-all-start.3 = ((f32[32,16,256]{2,1,0:T(8,128)}), f32[32,16,256]{2,1,0:T(8,128)S(1)}, u32[]{:S(2)}, u32[]{:S(2)}) async-start(f32[32,16,256]{2,1,0:T(8,128)} %copy.62), calls=%async_computation.3 | async-start | bytes 1048576 | tf_op jit(solution)/shard_map/all_to_all | solution.py:82
  158.5 65.7 %collective-permute-start = (f32[256,256]{0,1:T(8,128)S(1)}, f32[256,256]{0,1:T(8,128)S(1)}, u32[]{:S(2)}, u32[]{:S(2)}) collective-permute-start(f32[256,256]{0,1:T(8,128)S(1)} %fusion.3), channel_id=1, source_target_pairs={{0,1},{1,0},{2,3},{3,2},{4,5},{5,4},{6,7},{7,6},{8,9},{9,8},{10,11... | collective-permute-start | bytes 786440 | tf_op jit(solution)/shard_map/ppermute | solution.py:12
  224.2 63.2 %collective-permute-start.1 = (f32[256,256]{0,1:T(8,128)S(1)}, f32[256,256]{0,1:T(8,128)S(1)}, u32[]{:S(2)}, u32[]{:S(2)}) collective-permute-start(f32[256,256]{0,1:T(8,128)S(1)} %add.134), channel_id=1, source_target_pairs={{0,2},{1,3},{2,0},{3,1},{4,6},{5,7},{6,4},{7,5},{8,10},{9,11},{10,... | collective-permute-start | bytes 786440 | tf_op jit(solution)/shard_map/ppermute | solution.py:12
where the time goes:
time: 355 us; the launch traced here: 351 us
  other arithmetic  164 us (46%)
  matrix products  55.7 us (16%)
  waiting for transfers between devices  53.6 us (15%)
  blocking collectives  29.7 us (8%)
  local copies, waits for them, and re-layouts  22.8 us (6%)
  starting transfers between devices  19.5 us (5%)
  between operations  5.43 us (2%)
    another operation x7, other arithmetic, lower_solve(): return jax.scipy.linalg.solve_triangular(low, rhs, lower=True)  59.8 us
    dot_general x9, matrix products, matmul(): return jnp.dot(left, right, precision=lax.Precision.HIGHEST)  47.6 us
    another operation x7, other arithmetic, local(): pair_low = jnp.linalg.cholesky(pair_gram)  34.6 us
    another operation x7, other arithmetic, local(): leaf_low = jnp.linalg.cholesky(leaf_gram)  34.6 us
    another operation x7, other arithmetic, local(): group_low = jnp.linalg.cholesky(group_gram)  34.6 us
    all_to_all x1, blocking collectives, local(): lax.all_to_all(returned.reshape(2, 1, rows_dev, width), ('row', 'col'), s...  29.7 us
    all_to_all x1, waiting for transfers between devices, local(): lax.all_to_all(turned, ('row', 'col'), split_axis=1, concat_axis=2, tiled...  25 us
    all_to_all x1, waiting for transfers between devices, local(): lax.all_to_all(partial_sample, ('row', 'col'), split_axis=0, concat_axis=...  14.3 us
  transfers between devices with their start and end apart: 5, of which 3 were waited for; matrix products, arithmetic and copies ran while one was open for 35% of the time, Pallas kernels for 0%

commit v1 on v0

v1 whole, which is shorter than its diff:
```python
import math

import jax
import jax.numpy as jnp
import numpy as np
from jax import lax
from jax.experimental import pallas as pl
from jax.experimental.pallas import tpu as pltpu
from jax.sharding import PartitionSpec as P

LANES = 128
HIGHEST = lax.Precision.HIGHEST


def partner(value, axis, distance):
    mask = 2**distance
    pairs = [(source, source ^ mask) for source in range(lax.axis_size(axis))]
    return lax.ppermute(value, axis, pairs)


def matmul(left, right):
    return jnp.dot(left, right, precision=HIGHEST, preferred_element_type=jnp.float32)


def circle(product, length):
    angle = 2.0 * np.pi / length * (product % length)
    return np.cos(angle), np.sin(angle)


def tables(devices, split):
    major = devices * split
    total = major * LANES
    order = (np.arange(devices)[None, :] * split + np.arange(split)[:, None]).reshape(-1)
    freq = np.arange(major)
    cos, sin = circle(freq[:, None] * order[None, :], major)
    first = np.block([[cos, sin], [-sin, cos]])
    lane = np.arange(LANES)
    cos, sin = circle(lane[:, None] * lane[None, :], LANES)
    second = np.block([[cos, -sin], [sin, cos]])
    cos_turn, sin_turn = circle(freq[:, None] * lane[None, :], total)
    turn = np.stack([cos_turn, sin_turn])
    return [np.asarray(t, np.float32) for t in (first, first.T, second, second.T, turn)]


def circulant_kernel(devices, split, per_dev):
    major = devices * split
    pairs = per_dev // 2

    width = devices * per_dev

    def body(
        x_ref, lam_ref, first_ref, first_t_ref, second_ref, second_t_ref, turn_ref, o_ref, tile_ref
    ):
        cos = turn_ref[0]
        sin = turn_ref[1]
        for j in range(split):
            tile_ref[j * width : (j + 1) * width, :] = x_ref[:, j * LANES : (j + 1) * LANES]

        def column(c):
            return [
                tile_ref[pl.ds(j * width + c, devices, stride=per_dev), :] for j in range(split)
            ]

        packed = jnp.concatenate(
            [jnp.concatenate(column(2 * q) + column(2 * q + 1), 0) for q in range(pairs)], 1
        )
        mixed = matmul(first_ref[...], packed)
        turned = []
        for q in range(pairs):
            real = mixed[:major, q * LANES : (q + 1) * LANES]
            imag = mixed[major:, q * LANES : (q + 1) * LANES]
            turned.append(
                jnp.concatenate([real * cos + imag * sin, imag * cos - real * sin], 1)
            )
        spectra = matmul(jnp.concatenate(turned, 0), second_ref[...])
        lam = lam_ref[...]
        lam = jnp.concatenate([lam, lam], 1)
        spectra = jnp.concatenate(
            [spectra[q * major : (q + 1) * major] * lam for q in range(pairs)], 0
        )
        back = matmul(spectra, second_t_ref[...])
        turned = []
        for q in range(pairs):
            real = back[q * major : (q + 1) * major, :LANES]
            imag = back[q * major : (q + 1) * major, LANES:]
            turned.append(
                jnp.concatenate([real * cos - imag * sin, imag * cos + real * sin], 0)
            )
        sample = matmul(first_t_ref[...], jnp.concatenate(turned, 1))
        for c in range(per_dev):
            for j in range(split):
                row = (c % 2) * major + j * devices
                lane = (c // 2) * LANES
                tile_ref[pl.ds(j * width + c, devices, stride=per_dev), :] = sample[
                    row : row + devices, lane : lane + LANES
                ]
        for j in range(split):
            o_ref[:, j * LANES : (j + 1) * LANES] = tile_ref[j * width : (j + 1) * width, :]

    return body


def circulant(columns, lam, devices):
    width, rows_dev = columns.shape
    split = rows_dev // LANES
    return pl.pallas_call(
        circulant_kernel(devices, split, width // devices),
        out_shape=jax.ShapeDtypeStruct(columns.shape, jnp.float32),
        scratch_shapes=[pltpu.VMEM((split * width, LANES), jnp.float32)],
        compiler_params=pltpu.CompilerParams(vmem_limit_bytes=48 << 20),
        name="circulant",
    )(columns, lam, *tables(devices, split))


def symmetric_symbol(spectrum, devices):
    split = spectrum.shape[1] // LANES
    major = devices * split
    own = jnp.broadcast_to(spectrum.reshape(LANES, split).T[None], (devices, split, LANES))
    every = lax.all_to_all(own, ("row", "col"), split_axis=0, concat_axis=0, tiled=True)
    lam = every.swapaxes(0, 1).reshape(major, LANES)
    head = lam[:1]
    head = jnp.concatenate([head[:, :1], jnp.flip(head[:, 1:], 1)], 1)
    back = jnp.concatenate([head, jnp.flip(lam[1:], (0, 1))], 0)
    return (lam + back) * (0.5 / (major * LANES))


def factor_kernel(problems, width, block):
    tiles = width // LANES

    def body(gram_ref, upper_ref, inverse_ref, tile_ref):
        row = lax.broadcasted_iota(jnp.int32, (width, LANES), 0)
        lane = lax.broadcasted_iota(jnp.int32, (width, LANES), 1)
        for t in range(tiles):
            unit = jnp.where(row == lane + t * LANES, 1.0, 0.0).astype(jnp.float32)
            for p in range(problems):
                rows = slice(p * width, (p + 1) * width)
                tile_ref[t, rows, :] = gram_ref[p, :, t * LANES : (t + 1) * LANES]
                tile_ref[tiles + t, rows, :] = unit
        for base in range(0, width, block):
            own = base // LANES
            offset = base % LANES
            active = list(range(own, tiles)) + list(range(tiles, tiles + own + 1))
            panel = [
                [tile_ref[t, pl.ds(base + i, problems, stride=width), :] for t in active]
                for i in range(block)
            ]
            entry = {
                (i, j): jnp.broadcast_to(
                    panel[i][0][:, offset + j : offset + j + 1], (problems, LANES)
                )
                for i in range(block)
                for j in range(i, block)
            }
            for j in range(block):
                scale = lax.rsqrt(entry[j, j])
                factor = {i: entry[j, i] * scale for i in range(j + 1, block)}
                panel[j] = [x * scale for x in panel[j]]
                for i in range(j + 1, block):
                    for l in range(i, block):
                        entry[i, l] = entry[i, l] - factor[i] * factor[l]
                    panel[i] = [x - factor[i] * y for x, y in zip(panel[i], panel[j])]
                for x, t in zip(panel[j], active):
                    tile_ref[t, pl.ds(base + j, problems, stride=width), :] = x
            after = base + block
            if after < width:
                for p in range(problems):
                    done = jnp.concatenate(
                        [tile_ref[t, p * width + base : p * width + after, :] for t in active], 1
                    )
                    update = lax.dot_general(
                        done[:, : (tiles - own) * LANES],
                        done,
                        (((0,), (0,)), ((), ())),
                        precision=HIGHEST,
                        preferred_element_type=jnp.float32,
                    )
                    rows = slice(p * width + after, (p + 1) * width)
                    for q, t in enumerate(active):
                        tile_ref[t, rows, :] = (
                            tile_ref[t, rows, :]
                            - update[after - own * LANES :, q * LANES : (q + 1) * LANES]
                        )
        for t in range(tiles):
            lanes = slice(t * LANES, (t + 1) * LANES)
            for p in range(problems):
                rows = slice(p * width, (p + 1) * width)
                upper_ref[p, :, lanes] = jnp.where(
                    lane + t * LANES >= row, tile_ref[t, rows, :], 0.0
                )
                inverse_ref[p, :, lanes] = jnp.where(
                    lane + t * LANES <= row, tile_ref[tiles + t, rows, :], 0.0
                )

    return body


def factor(grams):
    problems, width, _ = grams.shape
    return pl.pallas_call(
        factor_kernel(problems, width, 16),
        out_shape=[jax.ShapeDtypeStruct(grams.shape, jnp.float32)] * 2,
        scratch_shapes=[pltpu.VMEM((2 * width // LANES, problems * width, LANES), jnp.float32)],
        compiler_params=pltpu.CompilerParams(vmem_limit_bytes=48 << 20),
        name="factor",
    )(grams)


def local(probes, spectrum):
    rows_dev, width = probes.shape
    devices = lax.axis_size("row") * lax.axis_size("col")
    col_index = lax.axis_index("col")
    axes = ("row", "col")
    lam = symmetric_symbol(spectrum, devices)
    columns = lax.all_to_all(probes.T, axes, split_axis=0, concat_axis=0, tiled=True)
    moved = circulant(columns, lam, devices)
    sample_t = lax.all_to_all(moved, axes, split_axis=0, concat_axis=0, tiled=True)
    leaf_gram = matmul(sample_t, sample_t.T) / rows_dev
    pair_gram = leaf_gram + partner(leaf_gram, "col", 0)
    group_gram = pair_gram + partner(pair_gram, "col", 1)
    upper, inverse = factor(jnp.stack([leaf_gram, pair_gram, group_gram]))
    half = width // 2
    quarter = width // 4
    pair_upper = lax.dynamic_slice_in_dim(upper[1], col_index % 2 * half, half, 0)
    group_factor = lax.dynamic_slice_in_dim(upper[2], col_index % 4 * quarter, quarter, 0)
    leaf_basis = matmul(sample_t.T, inverse[0].T)
    leaf_transfer = matmul(upper[0], inverse[1].T)
    pair_transfer = matmul(pair_upper, inverse[2].T)
    return (leaf_basis, leaf_transfer, pair_transfer, group_factor)


def solution(mesh):
    placed = P(("row", "col"), None)
    return jax.shard_map(
        local,
        mesh=mesh,
        in_specs=(placed, placed),
        out_specs=(placed, placed, placed, placed),
        check_vma=False,
    )
```

time: 355 us -> 107 us (0.30); the launches traced: 351 us -> 107 us
  other arithmetic: 164 us -> 2.2 us
  matrix products: 55.7 us -> 4.58 us
  Pallas kernels: 0 us -> 25 us
  local copies, waits for them, and re-layouts: 22.8 us -> 4.88 us
  waiting for transfers between devices: 53.6 us -> 37.4 us
  blocking collectives: 29.7 us -> 18.2 us
  starting transfers between devices: 19.5 us -> 13.9 us
  between operations: 5.43 us -> 0.76 us
    another operation x29 -> x2, other arithmetic: 164 us -> 0.09 us  [local(): upper, inverse = factor(jnp.stack([leaf_gram, pair_gram, group_gram]))]
    dot_general x13 -> x4, matrix products: 51.2 us -> 4.58 us  [matmul(): jnp.dot(left, right, precision=HIGHEST, preferred_element_type=jnp.float32)]
    all_to_all x3 -> x2, waiting for transfers between devices: 53.6 us -> 18.2 us  [the longest x1 12.8 us: local(): lax.all_to_all(probes.T, axes, split_axis=0, concat_axis=0, tiled=True)]
    pallas_call x0 -> x2, Pallas kernels: none -> 25 us  [the longest x1 21.9 us: factor(): pl.pallas_call(factor_kernel(problems, width, 16), out_shape=[jax.ShapeDt...]
    ppermute x2, waiting for transfers between devices: 0.01 us -> 19.1 us  [partner(): return lax.ppermute(value, axis, pairs)]
    another operation x28 -> x0, local copies, waits for them, and re-layouts: 13.7 us -> none  [the longest x13 7.97 us: lower_solve(): return jax.scipy.linalg.solve_triangular(low, rhs, lower=True)]
    all_to_all x1, blocking collectives: 29.7 us -> 18.2 us  [local(): lax.all_to_all(moved, axes, split_axis=0, concat_axis=0, tiled=True)]
    all_to_all x3 -> x2, starting transfers between devices: 16 us -> 10 us  [the longest x1 7.3 us: symmetric_symbol(): lax.all_to_all(own, ('row', 'col'), split_axis=0, concat_axis=0, tiled=True)]
  transfers between devices with their start and end apart: 5 -> 4, of which waited for: 3 -> 4; matrix products, arithmetic and copies ran while one was open for 35% -> 3% of each run, Pallas kernels for 0% -> 0%
where the time goes in v1:
time: 107 us
  waiting for transfers between devices  37.4 us (35%)
  Pallas kernels  25 us (23%)
  blocking collectives  18.2 us (17%)
  starting transfers between devices  13.9 us (13%)
  local copies, waits for them, and re-layouts  4.88 us (5%)
  matrix products  4.58 us (4%)
  other arithmetic  2.2 us (2%)
    pallas_call x1, Pallas kernels, factor(): pl.pallas_call(factor_kernel(problems, width, 16), out_shape=[jax.ShapeDt...  21.9 us
    ppermute x2, waiting for transfers between devices, partner(): return lax.ppermute(value, axis, pairs)  19.1 us
    all_to_all x1, blocking collectives, local(): lax.all_to_all(moved, axes, split_axis=0, concat_axis=0, tiled=True)  18.2 us
    all_to_all x1, waiting for transfers between devices, local(): lax.all_to_all(probes.T, axes, split_axis=0, concat_axis=0, tiled=True)  12.8 us
    all_to_all x1, starting transfers between devices, symmetric_symbol(): lax.all_to_all(own, ('row', 'col'), split_axis=0, concat_axis=0, tiled=True)  7.3 us
    all_to_all x1, waiting for transfers between devices, symmetric_symbol(): lax.all_to_all(own, ('row', 'col'), split_axis=0, concat_axis=0, tiled=True)  5.46 us
    dot_general x4, matrix products, matmul(): jnp.dot(left, right, precision=HIGHEST, preferred_element_type=jnp.float32)  4.58 us
    ppermute x2, starting transfers between devices, partner(): return lax.ppermute(value, axis, pairs)  3.88 us
  transfers between devices with their start and end apart: 4, of which 4 were waited for; matrix products, arithmetic and copies ran while one was open for 3% of the time, Pallas kernels for 0%

profile of v1, /device:TPU:0, one launch (start us, length us, event | category | flops | bytes accessed | tf_op | source)
XLA Modules:
  0.0 107.0 jit_solution(12234656662017037817)
XLA Ops:
  0.6 0.5 broadcast.7
  1.1 1.3 %reduce.3 = f32[512]{0:T(512)S(1)} reduce(f32[1,512]{1,0:T(1,128)} %param.8, f32[]{:T(128)} %broadcast.7), dimensions={0}, to_apply=%param.8.reduce_sub_computation.3 | reduce | bytes 4100 | tf_op args[1]
  2.5 0.1 reshape.21
  2.7 0.7 broadcast_in_dim.2
  3.3 7.3 %all-to-all-start.1 = ((f32[32,4,128]{2,1,0:T(4,128)}), f32[32,4,128]{2,1,0:T(4,128)S(1)}, u32[]{:S(2)}, u32[]{:S(2)}) async-start(f32[32,4,128]{2,1,0:T(4,128)} %broadcast_in_dim.2), calls=%async_computation.1 | async-start | bytes 131072 | tf_op jit(solution)/shard_map/all_to_all | solution.py:119
  10.6 2.0 %copy.15 = f32[512,256]{0,1:T(8,128)} copy(f32[512,256]{1,0:T(8,128)} %param.7) | data formatting | bytes 1048576 | tf_op args[0]
  12.7 5.5 %all-to-all-done.1 = f32[32,4,128]{2,1,0:T(4,128)S(1)} async-done(((f32[32,4,128]{2,1,0:T(4,128)}), f32[32,4,128]{2,1,0:T(4,128)S(1)}, u32[]{:S(2)}, u32[]{:S(2)}) %all-to-all-start.1) | async-done | bytes 65568 | tf_op jit(solution)/shard_map/all_to_all | solution.py:119
  18.1 2.7 %all-to-all-start = ((f32[32,8,512]{2,1,0:T(8,128)}), f32[32,8,512]{2,1,0:T(8,128)S(1)}, u32[]{:S(2)}, u32[]{:S(2)}) async-start(f32[32,8,512]{2,1,0:T(8,128)} %bitcast.1), calls=%async_computation | async-start | bytes 1048576 | tf_op jit(solution)/shard_map/all_to_all | solution.py:214
  21.0 0.5 slice.39
  21.5 0.1 rev.9
  21.7 0.7 fusion.15.lam_ref
  22.5 12.8 %all-to-all-done = f32[32,8,512]{2,1,0:T(8,128)S(1)} async-done(((f32[32,8,512]{2,1,0:T(8,128)}), f32[32,8,512]{2,1,0:T(8,128)S(1)}, u32[]{:S(2)}, u32[]{:S(2)}) %all-to-all-start) | async-done | bytes 524320 | tf_op jit(solution)/shard_map/all_to_all | solution.py:214
  35.3 3.1 %circulant.1 = f32[256,512]{1,0:T(8,128)S(1)} custom-call(f32[256,512]{1,0:T(8,128)S(1)} %bitcast.35, f32[128,128]{1,0:T(8,128)S(1)} %fusion.15.lam_ref, f32[256,256]{1,0:T(8,128)S(1)} %copy-done, f32[256,256]{1,0:T(8,128)S(1)} %copy-done.1, f32[256,256]{1,0:T(8,128)S(1)} %copy-done.2, f32[256,256]{1,0:T(8,128)S(1)} %copy-done.3, f32[2,128,128]{2,1,0:T(8,128)S(1)} %copy-done.4), custom_call_target="tpu_custom_call" | custom-call | tf_op jit(solution)/shard_map/circulant/pallas_call | solution.py:106
  38.4 18.2 %all_to_all.28 = f32[32,8,512]{2,1,0:T(8,128)S(1)} all-to-all(f32[32,8,512]{2,1,0:T(8,128)S(1)} %bitcast.36), channel_id=1, replica_groups=mesh['row'=8,'col'=4] {'row','col'}, dimensions={0} | all-to-all | bytes 1048576 | tf_op jit(solution)/shard_map/all_to_all | solution.py:216
  56.6 0.6 convolution_multiply_fusion
  57.3 2.6 %collective-permute-start = (f32[256,256]{1,0:T(8,128)S(1)}, f32[256,256]{1,0:T(8,128)S(1)}, u32[]{:S(2)}, u32[]{:S(2)}) collective-permute-start(f32[256,256]{1,0:T(8,128)S(1)} %convolution_multiply_fusion), channel_id=1, source_target_pairs={{0,1},{1,0},{2,3},{3,2},{4,5},{5,4},{6,7},{7,6},{8,9},{9,8},{10,11... | collective-permute-start | bytes 786440 | tf_op jit(solution)/shard_map/ppermute | solution.py:18
  59.9 6.8 %collective-permute-done = f32[256,256]{1,0:T(8,128)S(1)} collective-permute-done((f32[256,256]{1,0:T(8,128)S(1)}, f32[256,256]{1,0:T(8,128)S(1)}, u32[]{:S(2)}, u32[]{:S(2)}) %collective-permute-start) | collective-permute-done | bytes 262176 | tf_op jit(solution)/shard_map/ppermute | solution.py:18
  66.7 1.3 %collective-permute-start.1 = (f32[256,256]{1,0:T(8,128)S(1)}, f32[256,256]{1,0:T(8,128)S(1)}, u32[]{:S(2)}, u32[]{:S(2)}) collective-permute-start(f32[256,256]{1,0:T(8,128)S(1)} %add.23), channel_id=1, source_target_pairs={{0,2},{1,3},{2,0},{3,1},{4,6},{5,7},{6,4},{7,5},{8,10},{9,11},{10,... | collective-permute-start | bytes 786440 | tf_op jit(solution)/shard_map/ppermute | solution.py:18
  68.0 12.3 %collective-permute-done.1 = f32[256,256]{1,0:T(8,128)S(1)} collective-permute-done((f32[256,256]{1,0:T(8,128)S(1)}, f32[256,256]{1,0:T(8,128)S(1)}, u32[]{:S(2)}, u32[]{:S(2)}) %collective-permute-start.1) | collective-permute-done | bytes 262176 | tf_op jit(solution)/shard_map/ppermute | solution.py:18
  80.4 21.9 %factor.1 = (f32[3,256,256]{2,1,0:T(8,128)S(1)}, f32[3,256,256]{2,1,0:T(8,128)S(1)}) custom-call(f32[3,256,256]{2,1,0:T(8,128)S(1)} %pad_maximum_fusion.gram_ref), custom_call_target="tpu_custom_call" | custom-call | tf_op jit(solution)/shard_map/factor/pallas_call | solution.py:199
  102.4 1.1 %fusion.5 = f32[256,256]{1,0:T(8,128)} fusion(f32[3,256,256]{2,1,0:T(8,128)S(1)} %get-tuple-element.6, f32[3,256,256]{2,1,0:T(8,128)S(1)} %get-tuple-element.7), kind=kOutput, calls=%fused_computation.7 | convolution fusion | flops 201326592 | bytes 786432 | tf_op jit(solution)/shard_map/dot_general | solution.py:22
  103.5 1.1 fusion.3
  104.5 0.6 dynamic-slice_bitcast_fusion
  105.2 1.8 %fusion = f32[512,256]{1,0:T(8,128)} fusion(f32[32,8,512]{2,1,0:T(8,128)S(1)} %all_to_all.28, f32[3,256,256]{2,1,0:T(8,128)S(1)} %get-tuple-element.6), kind=kOutput, calls=%fused_computation.2 | convolution fusion | flops 402653184 | bytes 1310720 | tf_op jit(solution)/shard_map/dot_general | solution.py:22
  (19 shorter events, 0.4 us)
Async XLA Ops:
  3.3 14.8 %all-to-all-start.1 = ((f32[32,4,128]{2,1,0:T(4,128)}), f32[32,4,128]{2,1,0:T(4,128)S(1)}, u32[]{:S(2)}, u32[]{:S(2)}) async-start(f32[32,4,128]{2,1,0:T(4,128)} %broadcast_in_dim.2), calls=%async_computation.1 | async-start | bytes 131072 | tf_op jit(solution)/shard_map/all_to_all | solution.py:119
  18.1 17.1 %copy-start.2 = (f32[256,256]{1,0:T(8,128)S(1)}, f32[256,256]{1,0:T(8,128)}, u32[]{:S(2)}) copy-start(f32[256,256]{1,0:T(8,128)} %constant.53.clone.second_ref) | copy-start | bytes 786436
  18.1 17.1 %copy-start.3 = (f32[256,256]{1,0:T(8,128)S(1)}, f32[256,256]{1,0:T(8,128)}, u32[]{:S(2)}) copy-start(f32[256,256]{1,0:T(8,128)} %constant.54.clone.second_t_ref) | copy-start | bytes 786436
  18.1 17.1 %copy-start.4 = (f32[2,128,128]{2,1,0:T(8,128)S(1)}, f32[2,128,128]{2,1,0:T(8,128)}, u32[]{:S(2)}) copy-start(f32[2,128,128]{2,1,0:T(8,128)} %constant.55.clone.turn_ref) | copy-start | bytes 393220
  18.1 17.1 %all-to-all-start = ((f32[32,8,512]{2,1,0:T(8,128)}), f32[32,8,512]{2,1,0:T(8,128)S(1)}, u32[]{:S(2)}, u32[]{:S(2)}) async-start(f32[32,8,512]{2,1,0:T(8,128)} %bitcast.1), calls=%async_computation | async-start | bytes 1048576 | tf_op jit(solution)/shard_map/all_to_all | solution.py:214
  20.9 14.4 %copy-start.1 = (f32[256,256]{1,0:T(8,128)S(1)}, f32[256,256]{1,0:T(8,128)}, u32[]{:S(2)}) copy-start(f32[256,256]{1,0:T(8,128)} %constant.52.clone.first_t_ref) | copy-start | bytes 786436
  20.9 14.4 %copy-start = (f32[256,256]{1,0:T(8,128)S(1)}, f32[256,256]{1,0:T(8,128)}, u32[]{:S(2)}) copy-start(f32[256,256]{1,0:T(8,128)} %constant.51.clone.first_ref) | copy-start | bytes 786436
  57.3 9.5 %collective-permute-start = (f32[256,256]{1,0:T(8,128)S(1)}, f32[256,256]{1,0:T(8,128)S(1)}, u32[]{:S(2)}, u32[]{:S(2)}) collective-permute-start(f32[256,256]{1,0:T(8,128)S(1)} %convolution_multiply_fusion), channel_id=1, source_target_pairs={{0,1},{1,0},{2,3},{3,2},{4,5},{5,4},{6,7},{7,6},{8,9},{9,8},{10,11... | collective-permute-start | bytes 786440 | tf_op jit(solution)/shard_map/ppermute | solution.py:18
  66.7 13.6 %collective-permute-start.1 = (f32[256,256]{1,0:T(8,128)S(1)}, f32[256,256]{1,0:T(8,128)S(1)}, u32[]{:S(2)}, u32[]{:S(2)}) collective-permute-start(f32[256,256]{1,0:T(8,128)S(1)} %add.23), channel_id=1, source_target_pairs={{0,2},{1,3},{2,0},{3,1},{4,6},{5,7},{6,4},{7,5},{8,10},{9,11},{10,... | collective-permute-start | bytes 786440 | tf_op jit(solution)/shard_map/ppermute | solution.py:18

commit v2 on v1

v2 whole, which is shorter than its diff:
```python
import math

import jax
import jax.numpy as jnp
import numpy as np
from jax import lax
from jax.experimental import pallas as pl
from jax.experimental.pallas import tpu as pltpu
from jax.sharding import PartitionSpec as P

LANES = 128
HIGHEST = lax.Precision.HIGHEST


def partner(value, axis, distance):
    mask = 2**distance
    pairs = [(source, source ^ mask) for source in range(lax.axis_size(axis))]
    return lax.ppermute(value, axis, pairs)


def matmul(left, right):
    return jnp.dot(left, right, precision=HIGHEST, preferred_element_type=jnp.float32)


def circle(product, length):
    angle = 2.0 * np.pi / length * (product % length)
    return np.cos(angle), np.sin(angle)


def tables(devices, split):
    major = devices * split
    total = major * LANES
    order = (np.arange(devices)[None, :] * split + np.arange(split)[:, None]).reshape(-1)
    freq = np.arange(major)
    cos, sin = circle(freq[:, None] * order[None, :], major)
    first = np.block([[cos, sin], [-sin, cos]])
    lane = np.arange(LANES)
    cos, sin = circle(lane[:, None] * lane[None, :], LANES)
    second = np.block([[cos, -sin], [sin, cos]])
    cos_turn, sin_turn = circle(freq[:, None] * lane[None, :], total)
    turn = np.stack([cos_turn, sin_turn])
    return [np.asarray(t, np.float32) for t in (first, first.T, second, second.T, turn)]


def circulant_kernel(devices, split, per_dev):
    major = devices * split
    pairs = per_dev // 2

    width = devices * per_dev

    def body(
        x_ref, lam_ref, first_ref, first_t_ref, second_ref, second_t_ref, turn_ref, o_ref, tile_ref
    ):
        cos = turn_ref[0]
        sin = turn_ref[1]
        for j in range(split):
            tile_ref[j * width : (j + 1) * width, :] = x_ref[:, j * LANES : (j + 1) * LANES]

        def column(c):
            return [
                tile_ref[pl.ds(j * width + c, devices, stride=per_dev), :] for j in range(split)
            ]

        packed = jnp.concatenate(
            [jnp.concatenate(column(2 * q) + column(2 * q + 1), 0) for q in range(pairs)], 1
        )
        mixed = matmul(first_ref[...], packed)
        turned = []
        for q in range(pairs):
            real = mixed[:major, q * LANES : (q + 1) * LANES]
            imag = mixed[major:, q * LANES : (q + 1) * LANES]
            turned.append(
                jnp.concatenate([real * cos + imag * sin, imag * cos - real * sin], 1)
            )
        spectra = matmul(jnp.concatenate(turned, 0), second_ref[...])
        lam = lam_ref[...]
        lam = jnp.concatenate([lam, lam], 1)
        spectra = jnp.concatenate(
            [spectra[q * major : (q + 1) * major] * lam for q in range(pairs)], 0
        )
        back = matmul(spectra, second_t_ref[...])
        turned = []
        for q in range(pairs):
            real = back[q * major : (q + 1) * major, :LANES]
            imag = back[q * major : (q + 1) * major, LANES:]
            turned.append(
                jnp.concatenate([real * cos - imag * sin, imag * cos + real * sin], 0)
            )
        sample = matmul(first_t_ref[...], jnp.concatenate(turned, 1))
        for c in range(per_dev):
            for j in range(split):
                row = (c % 2) * major + j * devices
                lane = (c // 2) * LANES
                tile_ref[pl.ds(j * width + c, devices, stride=per_dev), :] = sample[
                    row : row + devices, lane : lane + LANES
                ]
        for j in range(split):
            o_ref[:, j * LANES : (j + 1) * LANES] = tile_ref[j * width : (j + 1) * width, :]

    return body


def circulant(columns, lam, devices):
    width, rows_dev = columns.shape
    split = rows_dev // LANES
    return pl.pallas_call(
        circulant_kernel(devices, split, width // devices),
        out_shape=jax.ShapeDtypeStruct(columns.shape, jnp.float32),
        scratch_shapes=[pltpu.VMEM((split * width, LANES), jnp.float32)],
        compiler_params=pltpu.CompilerParams(vmem_limit_bytes=48 << 20),
        name="circulant",
    )(columns, lam, *tables(devices, split))


def symmetric_symbol(every, devices):
    split = every.shape[1] // LANES
    major = devices * split
    lam = every.reshape(devices, LANES, split).transpose(2, 0, 1).reshape(major, LANES)
    head = lam[:1]
    head = jnp.concatenate([head[:, :1], jnp.flip(head[:, 1:], 1)], 1)
    back = jnp.concatenate([head, jnp.flip(lam[1:], (0, 1))], 0)
    return (lam + back) * (0.5 / (major * LANES))


def iota(shape, dim):
    return lax.broadcasted_iota(jnp.int32, shape, dim)


def times_transpose(left, right):
    return lax.dot_general(
        left,
        right,
        (((1,), (1,)), ((), ())),
        precision=HIGHEST,
        preferred_element_type=jnp.float32,
    )


def gram_kernel(sample_ref, packed_ref):
    width, rows = sample_ref.shape
    upper = times_transpose(sample_ref[:LANES, :], sample_ref[...]) * (1.0 / rows)
    last = sample_ref[LANES:, :]
    last = times_transpose(last, last) * (1.0 / rows)
    row = iota((LANES, LANES), 0)
    lane = iota((LANES, LANES), 1)
    packed_ref[:LANES, :] = jnp.where(lane >= row, upper[:, :LANES], last)
    packed_ref[LANES : 2 * LANES, :] = upper[:, LANES:]
    diagonal = jnp.sum(jnp.where(lane == row, last, 0.0), axis=0, keepdims=True)
    packed_ref[2 * LANES :, :] = jnp.broadcast_to(diagonal, (8, LANES))


def packed_gram(sample_t):
    return pl.pallas_call(
        gram_kernel,
        out_shape=jax.ShapeDtypeStruct((2 * LANES + 8, LANES), jnp.float32),
        name="gram",
    )(sample_t)


def parts(value):
    high = value.astype(jnp.bfloat16).astype(jnp.float32)
    rest = value - high
    middle = rest.astype(jnp.bfloat16).astype(jnp.float32)
    return high, middle, rest - middle


def eliminate(tile_ref, problems, width, block):
    tiles = width // LANES
    thin = iota((problems, LANES), 1)
    for base in range(0, width, block):
        own = base // LANES
        offset = base % LANES
        order = [own] + [t for t in range(tiles) if t != own]
        panel = [
            [tile_ref[t, pl.ds(base + i, problems, stride=width), :] for t in order]
            for i in range(block)
        ]
        entry = {
            (i, j): jnp.broadcast_to(
                panel[i][0][:, offset + j : offset + j + 1], (problems, LANES)
            )
            for i in range(block)
            for j in range(i, block)
        }
        for j in range(block):
            scale = lax.rsqrt(entry[j, j])
            factor = {i: entry[j, i] * scale for i in range(j + 1, block)}
            hot = thin == offset + j
            panel[j] = [jnp.where(hot, 1.0, panel[j][0]) * scale] + [
                x * scale for x in panel[j][1:]
            ]
            for i in range(j + 1, block):
                for l in range(i, block):
                    entry[i, l] = entry[i, l] - factor[i] * factor[l]
                kept = [jnp.where(hot, 0.0, panel[i][0])] + panel[i][1:]
                panel[i] = [x - factor[i] * y for x, y in zip(kept, panel[j])]
            for x, t in zip(panel[j], order):
                tile_ref[t, pl.ds(base + j, problems, stride=width), :] = x
        after = base + block
        if after == width:
            continue
        first = after // LANES * LANES
        lane = iota((block, LANES), 1) - offset
        inverse = (lane < 0) | (lane >= block) | (lane <= iota((block, LANES), 0))
        below = iota((width - after, LANES), 1) - offset
        below = (below >= 0) & (below < block)
        for p in range(problems):
            start = p * width
            rows = [parts(tile_ref[t, start + base : start + after, :]) for t in range(tiles)]
            left = jnp.concatenate(
                [
                    jnp.concatenate([rows[t][q] for q in (0, 0, 1, 1, 0, 2)], 0)
                    for t in range(first // LANES, tiles)
                ],
                1,
            ).astype(jnp.bfloat16)
            rows[own] = [jnp.where(inverse, x, 0.0) for x in rows[own]]
            right = jnp.concatenate(
                [
                    jnp.concatenate([rows[t][q] for q in (0, 1, 0, 1, 2, 0)], 0)
                    for t in range(tiles)
                ],
                1,
            ).astype(jnp.bfloat16)
            update = lax.dot_general(
                left, right, (((0,), (0,)), ((), ())), preferred_element_type=jnp.float32
            )
            for t in range(tiles):
                old = tile_ref[t, start + after : start + width, :]
                if t == own:
                    old = jnp.where(below, 0.0, old)
                tile_ref[t, start + after : start + width, :] = (
                    old - update[after - first :, t * LANES : (t + 1) * LANES]
                )


def finish_kernel(
    place_ref,
    sample_ref,
    leaf_ref,
    pair_ref,
    group_ref,
    basis_ref,
    leaf_transfer_ref,
    pair_transfer_ref,
    group_factor_ref,
    tile_ref,
    upper_ref,
):
    width = sample_ref.shape[0]
    row = iota((LANES, LANES), 0)
    lane = iota((LANES, LANES), 1)
    for p, packed_ref in enumerate((leaf_ref, pair_ref, group_ref)):
        start = p * width
        shared = packed_ref[:LANES, :]
        tile_ref[0, start : start + LANES, :] = shared
        tile_ref[0, start + LANES : start + width, :] = jnp.zeros((LANES, LANES), jnp.float32)
        tile_ref[1, start : start + LANES, :] = packed_ref[LANES : 2 * LANES, :]
        diagonal = jnp.broadcast_to(packed_ref[2 * LANES : 2 * LANES + 1, :], (LANES, LANES))
        tile_ref[1, start + LANES : start + width, :] = jnp.where(
            lane == row, diagonal, shared.T
        )
    eliminate(tile_ref, 3, width, 16)
    row = iota((width, width), 0)
    lane = iota((width, width), 1)
    inverse = []
    for p in range(3):
        start = p * width
        whole = jnp.concatenate([tile_ref[t, start : start + width, :] for t in range(2)], 1)
        inverse.append(jnp.where(lane <= row, whole, 0.0))
        upper_ref[p] = jnp.where(
            lane > row, whole, jnp.where(lane == row, 1.0 / whole, 0.0)
        )
    basis_ref[...] = times_transpose(sample_ref[...].T, inverse[0])
    leaf_transfer_ref[...] = times_transpose(upper_ref[0], inverse[1])
    half = width // 2
    quarter = width // 4
    place = place_ref[0]
    pair_upper = upper_ref[1, pl.ds(pl.multiple_of(place % 2 * half, half), half), :]
    pair_transfer_ref[...] = times_transpose(pair_upper, inverse[2])
    group_factor_ref[...] = upper_ref[
        2, pl.ds(pl.multiple_of(place % 4 * quarter, quarter), quarter), :
    ]


def finish(place, sample_t, leaf, pair, group):
    width, rows = sample_t.shape
    shapes = [(rows, width), (width, width), (width // 2, width), (width // 4, width)]
    return pl.pallas_call(
        finish_kernel,
        out_shape=[jax.ShapeDtypeStruct(shape, jnp.float32) for shape in shapes],
        in_specs=[pl.BlockSpec(memory_space=pltpu.SMEM)]
        + [pl.BlockSpec(memory_space=pltpu.VMEM)] * 4,
        scratch_shapes=[
            pltpu.VMEM((width // LANES, 3 * width, LANES), jnp.float32),
            pltpu.VMEM((3, width, width), jnp.float32),
        ],
        compiler_params=pltpu.CompilerParams(vmem_limit_bytes=48 << 20),
        name="finish",
    )(place, sample_t, leaf, pair, group)


def local(probes, spectrum):
    devices = lax.axis_size("row") * lax.axis_size("col")
    axes = ("row", "col")
    turned, spectrum = lax.optimization_barrier((probes.T, spectrum))
    columns = lax.all_to_all(turned, axes, split_axis=0, concat_axis=0, tiled=True)
    every = lax.all_to_all(
        jnp.broadcast_to(spectrum, (devices, spectrum.shape[1])),
        axes,
        split_axis=0,
        concat_axis=0,
        tiled=True,
    )
    moved = circulant(columns, symmetric_symbol(every, devices), devices)
    sample_t = lax.all_to_all(moved, axes, split_axis=0, concat_axis=0, tiled=True)
    leaf = packed_gram(sample_t)
    pair = leaf + partner(leaf, "col", 0)
    group = pair + partner(pair, "col", 1)
    place = lax.axis_index("col").reshape(1).astype(jnp.int32)
    return tuple(finish(place, sample_t, leaf, pair, group))


def solution(mesh):
    placed = P(("row", "col"), None)
    return jax.shard_map(
        local,
        mesh=mesh,
        in_specs=(placed, placed),
        out_specs=(placed, placed, placed, placed),
        check_vma=False,
    )
```

time: 107 us -> 87.9 us (0.82)
  blocking collectives: 18.2 us -> 32.9 us
  waiting for transfers between devices: 37.4 us -> 23.8 us
  starting transfers between devices: 13.9 us -> 6.55 us
  Pallas kernels: 25 us -> 18 us
  matrix products: 4.58 us -> 0 us
    all_to_all x0 -> x1, blocking collectives: none -> 14.6 us  [local(): lax.all_to_all(jnp.broadcast_to(spectrum, (devices, spectrum.shape[1])),...]
    ppermute x2, waiting for transfers between devices: 19.1 us -> 11.3 us  [partner(): return lax.ppermute(value, axis, pairs)]
    all_to_all x2 -> x1, starting transfers between devices: 10 us -> 2.74 us  [local(): lax.all_to_all(turned, axes, split_axis=0, concat_axis=0, tiled=True)]
    pallas_call x1 -> x2, Pallas kernels: 21.9 us -> 14.8 us  [the longest x1 12.3 us: finish(): pl.pallas_call(finish_kernel, out_shape=[jax.ShapeDtypeStruct(shape, jnp....]
    all_to_all x2 -> x1, waiting for transfers between devices: 18.2 us -> 12.5 us  [local(): lax.all_to_all(turned, axes, split_axis=0, concat_axis=0, tiled=True)]
    dot_general x4 -> x0, matrix products: 4.58 us -> none  [matmul(): jnp.dot(left, right, precision=HIGHEST, preferred_element_type=jnp.float32)]
    unnamed x1 -> x0, other arithmetic: 1.34 us -> none
    unnamed x12 -> x17, local copies, waits for them, and re-layouts: 2.58 us -> 2.75 us
  transfers between devices with their start and end apart: 4 -> 3, of which waited for: 4 -> 3; matrix products, arithmetic and copies ran while one was open for 3% -> 2% of each run, Pallas kernels for 0% -> 0%
where the time goes in v2:
time: 87.9 us; the launch traced here: 87.5 us
  blocking collectives  32.9 us (37%)
  waiting for transfers between devices  23.8 us (27%)
  Pallas kernels  18 us (20%)
  starting transfers between devices  6.55 us (7%)
  local copies, waits for them, and re-layouts  3.83 us (4%)
  other arithmetic  1.68 us (2%)
    all_to_all x1, blocking collectives, local(): lax.all_to_all(moved, axes, split_axis=0, concat_axis=0, tiled=True)  18.3 us
    all_to_all x1, blocking collectives, local(): lax.all_to_all(jnp.broadcast_to(spectrum, (devices, spectrum.shape[1])),...  14.6 us
    all_to_all x1, waiting for transfers between devices, local(): lax.all_to_all(turned, axes, split_axis=0, concat_axis=0, tiled=True)  12.5 us
    pallas_call x1, Pallas kernels, finish(): pl.pallas_call(finish_kernel, out_shape=[jax.ShapeDtypeStruct(shape, jnp....  12.3 us
    ppermute x2, waiting for transfers between devices, partner(): return lax.ppermute(value, axis, pairs)  11.3 us
    ppermute x2, starting transfers between devices, partner(): return lax.ppermute(value, axis, pairs)  3.81 us
    pallas_call x1, Pallas kernels, circulant(): pl.pallas_call(circulant_kernel(devices, split, width // devices), out_sh...  3.13 us
    unnamed x17, local copies, waits for them, and re-layouts  2.75 us
  transfers between devices with their start and end apart: 3, of which 3 were waited for; matrix products, arithmetic and copies ran while one was open for 2% of the time, Pallas kernels for 0%

profile of v2, /device:TPU:0, one launch (start us, length us, event | category | flops | bytes accessed | tf_op | source)
XLA Modules:
  0.0 87.5 jit_solution(3723930541048248426)
XLA Ops:
  0.6 2.0 %copy.14 = f32[512,256]{0,1:T(8,128)} copy(f32[512,256]{1,0:T(8,128)} %param.7) | data formatting | bytes 1048576 | tf_op args[0]
  2.7 0.7 copy-done.7
  3.4 14.6 %all_to_all.28 = f32[32,1,512]{2,1,0:T(1,128)S(1)} all-to-all(f32[32,1,512]{2,1,0:T(1,128)S(1)} %broadcast_in_dim.2), channel_id=1, replica_groups=mesh['row'=8,'col'=4] {'row','col'}, dimensions={0} | all-to-all | bytes 131072 | tf_op jit(solution)/shard_map/all_to_all | solution.py:308
  18.0 2.7 %all-to-all-start = ((f32[32,8,512]{2,1,0:T(8,128)}), f32[32,8,512]{2,1,0:T(8,128)S(1)}, u32[]{:S(2)}, u32[]{:S(2)}) async-start(f32[32,8,512]{2,1,0:T(8,128)} %bitcast.2), calls=%async_computation | async-start | bytes 1048576 | tf_op jit(solution)/shard_map/all_to_all | solution.py:307
  20.7 0.0 copy-start.5
  20.7 0.1 copy.15
  20.9 0.0 copy-start.3
  20.9 0.0 copy-start.4
  20.9 0.1 copy.16
  21.0 0.5 slice.15
  21.5 0.1 slice.16
  21.6 0.1 rev.8
  21.7 0.1 rev.9
  21.8 0.7 fusion.lam_ref
  22.6 12.5 %all-to-all-done = f32[32,8,512]{2,1,0:T(8,128)S(1)} async-done(((f32[32,8,512]{2,1,0:T(8,128)}), f32[32,8,512]{2,1,0:T(8,128)S(1)}, u32[]{:S(2)}, u32[]{:S(2)}) %all-to-all-start) | async-done | bytes 524320 | tf_op jit(solution)/shard_map/all_to_all | solution.py:307
  35.1 3.1 %circulant.1 = f32[256,512]{1,0:T(8,128)S(1)} custom-call(f32[256,512]{1,0:T(8,128)S(1)} %bitcast.14, f32[128,128]{1,0:T(8,128)S(1)} %fusion.lam_ref, f32[256,256]{1,0:T(8,128)S(1)} %copy-done.5, f32[256,256]{1,0:T(8,128)S(1)} %copy-done.4, f32[256,256]{1,0:T(8,128)S(1)} %copy-done.3, f32[256,256]{1,0:T(8,128)S(1)} %copy-done.2, f32[2,128,128]{2,1,0:T(8,128)S(1)} %copy-done.6), custom_call_target="tpu_custom_call" | custom-call | tf_op jit(solution)/shard_map/circulant/pallas_call | solution.py:106
  38.3 18.3 %all_to_all.29 = f32[32,8,512]{2,1,0:T(8,128)} all-to-all(f32[32,8,512]{2,1,0:T(8,128)S(1)} %bitcast.15), channel_id=1, replica_groups=mesh['row'=8,'col'=4] {'row','col'}, dimensions={0} | all-to-all | bytes 1048576 | tf_op jit(solution)/shard_map/all_to_all | solution.py:316
  56.6 2.5 %gram.1.leaf_ref = f32[264,128]{1,0:T(8,128)} custom-call(f32[256,512]{1,0:T(8,128)} %bitcast.12), custom_call_target="tpu_custom_call" | custom-call | tf_op jit(solution)/shard_map/gram/pallas_call | solution.py:153
  59.1 2.5 %collective-permute-start = (f32[264,128]{1,0:T(8,128)}, f32[264,128]{1,0:T(8,128)S(1)}, u32[]{:S(2)}, u32[]{:S(2)}) collective-permute-start(f32[264,128]{1,0:T(8,128)} %gram.1.leaf_ref), channel_id=1, source_target_pairs={{0,1},{1,0},{2,3},{3,2},{4,5},{5,4},{6,7},{7,6},{8,9},{9,8},{10,11... | collective-permute-start | bytes 405512 | tf_op jit(solution)/shard_map/ppermute | solution.py:18
  61.7 4.3 %collective-permute-done = f32[264,128]{1,0:T(8,128)S(1)} collective-permute-done((f32[264,128]{1,0:T(8,128)}, f32[264,128]{1,0:T(8,128)S(1)}, u32[]{:S(2)}, u32[]{:S(2)}) %collective-permute-start) | collective-permute-done | bytes 135200 | tf_op jit(solution)/shard_map/ppermute | solution.py:18
  66.0 0.9 %add.10.pair_ref = f32[264,128]{1,0:T(8,128)S(1)} add(f32[264,128]{1,0:T(8,128)} %gram.1.leaf_ref, f32[264,128]{1,0:T(8,128)S(1)} %collective-permute-done) | non-fusion elementwise | flops 33792 | bytes 405504 | tf_op jit(solution)/shard_map/add | solution.py:318
  66.9 1.3 %collective-permute-start.1 = (f32[264,128]{1,0:T(8,128)S(1)}, f32[264,128]{1,0:T(8,128)S(1)}, u32[]{:S(2)}, u32[]{:S(2)}) collective-permute-start(f32[264,128]{1,0:T(8,128)S(1)} %add.10.pair_ref), channel_id=1, source_target_pairs={{0,2},{1,3},{2,0},{3,1},{4,6},{5,7},{6,4},{7,5},{8,10},{9,11},{10,... | collective-permute-start | bytes 405512 | tf_op jit(solution)/shard_map/ppermute | solution.py:18
  68.2 7.0 %collective-permute-done.1 = f32[264,128]{1,0:T(8,128)S(1)} collective-permute-done((f32[264,128]{1,0:T(8,128)S(1)}, f32[264,128]{1,0:T(8,128)S(1)}, u32[]{:S(2)}, u32[]{:S(2)}) %collective-permute-start.1) | collective-permute-done | bytes 135200 | tf_op jit(solution)/shard_map/ppermute | solution.py:18
  75.2 12.3 %finish.1 = (f32[512,256]{1,0:T(8,128)}, f32[256,256]{1,0:T(8,128)}, f32[128,256]{1,0:T(8,128)}, f32[64,256]{1,0:T(8,128)}) custom-call(s32[1]{0:T(128)} %bitcast.place_ref, f32[256,512]{1,0:T(8,128)S(1)} %bitcast.13, f32[264,128]{1,0:T(8,128)S(1)} %copy-done.1, f32[264,128]{1,0:T(8,128)S(1)} %add.10.pair_ref, f32[264,128]{1,0:T(8,128)S(1)} %add.11.group_ref), custom_call_target="tpu_custom_call" | custom-call | tf_op jit(solution)/shard_map/finish/pallas_call | solution.py:289
  (15 shorter events, 0.1 us)
Async XLA Ops:
  2.7 0.7 copy-start.7
  18.0 17.1 %copy-start.6 = (f32[2,128,128]{2,1,0:T(8,128)S(1)}, f32[2,128,128]{2,1,0:T(8,128)}, u32[]{:S(2)}) copy-start(f32[2,128,128]{2,1,0:T(8,128)} %constant.20.clone.turn_ref) | copy-start | bytes 393220
  18.0 17.1 %all-to-all-start = ((f32[32,8,512]{2,1,0:T(8,128)}), f32[32,8,512]{2,1,0:T(8,128)S(1)}, u32[]{:S(2)}, u32[]{:S(2)}) async-start(f32[32,8,512]{2,1,0:T(8,128)} %bitcast.2), calls=%async_computation | async-start | bytes 1048576 | tf_op jit(solution)/shard_map/all_to_all | solution.py:307
  20.7 14.4 %copy-start.5 = (f32[256,256]{1,0:T(8,128)S(1)}, f32[256,256]{1,0:T(8,128)}, u32[]{:S(2)}) copy-start(f32[256,256]{1,0:T(8,128)} %constant.16.clone.first_ref) | copy-start | bytes 786436
  20.9 14.2 %copy-start.3 = (f32[256,256]{1,0:T(8,128)S(1)}, f32[256,256]{1,0:T(8,128)}, u32[]{:S(2)}) copy-start(f32[256,256]{1,0:T(8,128)} %constant.18.clone.second_ref) | copy-start | bytes 786436
  20.9 14.2 %copy-start.4 = (f32[256,256]{1,0:T(8,128)S(1)}, f32[256,256]{1,0:T(8,128)}, u32[]{:S(2)}) copy-start(f32[256,256]{1,0:T(8,128)} %constant.17.clone.first_t_ref) | copy-start | bytes 786436
  21.0 14.1 %copy-start.2 = (f32[256,256]{1,0:T(8,128)S(1)}, f32[256,256]{1,0:T(8,128)}, u32[]{:S(2)}) copy-start(f32[256,256]{1,0:T(8,128)} %constant.19.clone.second_t_ref) | copy-start | bytes 786436
  59.1 16.1 %copy-start = (f32[32,8,512]{2,1,0:T(8,128)S(1)}, f32[32,8,512]{2,1,0:T(8,128)}, u32[]{:S(2)}) copy-start(f32[32,8,512]{2,1,0:T(8,128)} %all_to_all.29) | copy-start | bytes 1572868
  59.1 6.9 %collective-permute-start = (f32[264,128]{1,0:T(8,128)}, f32[264,128]{1,0:T(8,128)S(1)}, u32[]{:S(2)}, u32[]{:S(2)}) collective-permute-start(f32[264,128]{1,0:T(8,128)} %gram.1.leaf_ref), channel_id=1, source_target_pairs={{0,1},{1,0},{2,3},{3,2},{4,5},{5,4},{6,7},{7,6},{8,9},{9,8},{10,11... | collective-permute-start | bytes 405512 | tf_op jit(solution)/shard_map/ppermute | solution.py:18
  66.9 8.2 %collective-permute-start.1 = (f32[264,128]{1,0:T(8,128)S(1)}, f32[264,128]{1,0:T(8,128)S(1)}, u32[]{:S(2)}, u32[]{:S(2)}) collective-permute-start(f32[264,128]{1,0:T(8,128)S(1)} %add.10.pair_ref), channel_id=1, source_target_pairs={{0,2},{1,3},{2,0},{3,1},{4,6},{5,7},{6,4},{7,5},{8,10},{9,11},{10,... | collective-permute-start | bytes 405512 | tf_op jit(solution)/shard_map/ppermute | solution.py:18
  68.2 7.0 %copy-start.1 = (f32[264,128]{1,0:T(8,128)S(1)}, f32[264,128]{1,0:T(8,128)}, u32[]{:S(2)}) copy-start(f32[264,128]{1,0:T(8,128)} %gram.1.leaf_ref) | copy-start | bytes 405508

commit v3 on v2

--- a/solution.py
+++ b/solution.py
@@ -42,19 +42,84 @@
     return [np.asarray(t, np.float32) for t in (first, first.T, second, second.T, turn)]
 
 
-def circulant_kernel(devices, split, per_dev):
+def iota(shape, dim):
+    return lax.broadcasted_iota(jnp.int32, shape, dim)
+
+
+def times_transpose(left, right):
+    return lax.dot_general(
+        left,
+        right,
+        (((1,), (1,)), ((), ())),
+        precision=HIGHEST,
+        preferred_element_type=jnp.float32,
+    )
+
+
+def spread_kernel(per_dev, extra):
+    def body(probes_ref, spectrum_ref, o_ref):
+        rows, width = probes_ref.shape
+        split = rows // LANES
+        for j in range(split):
+            lanes = slice(j * LANES, (j + 1) * LANES)
+            o_ref[:, lanes] = probes_ref[lanes, :].T
+        place = iota((LANES, rows), 1)
+        own = jnp.where(place // split == iota((LANES, rows), 0), spectrum_ref[...], 0.0)
+        for t in range(extra):
+            part = iota((8, rows), 0) % per_dev + t * per_dev
+            pick = jnp.where(iota((8, rows), 1) % split == part, 1.0, 0.0)
+            symbol = times_transpose(pick, own)
+            for r in range(0, width, 8):
+                o_ref[r : r + 8, rows + t * LANES : rows + (t + 1) * LANES] = symbol
+
+    return body
+
+
+def spread(probes, spectrum, devices):
+    rows, width = probes.shape
+    per_dev = width // devices
+    extra = pl.cdiv(rows // LANES, per_dev)
+    return pl.pallas_call(
+        spread_kernel(per_dev, extra),
+        out_shape=jax.ShapeDtypeStruct((width, rows + extra * LANES), jnp.float32),
+        name="spread",
+    )(probes, spectrum)
+
+
+def circulant_kernel(devices, split, per_dev, extra):
     major = devices * split
     pairs = per_dev // 2
-
     width = devices * per_dev
 
-    def body(
-        x_ref, lam_ref, first_ref, first_t_ref, second_ref, second_t_ref, turn_ref, o_ref, tile_ref
-    ):
+    def symmetric_symbol(tile_ref):
+        lam = jnp.concatenate(
+            [
+                tile_ref[
+                    pl.ds((split + h // per_dev) * width + h % per_dev, devices, stride=per_dev), :
+                ]
+                for h in range(split)
+            ],
+            0,
+        )
+        row = iota((LANES, LANES), 0)
+        lane = iota((LANES, LANES), 1)
+        flip = jnp.where(row + lane == LANES - 1, 1.0, 0.0)
+        head_flip = jnp.where((row + lane) % LANES == 0, 1.0, 0.0)
+        back = matmul(lam, jnp.concatenate([flip, head_flip], 1))
+        row = iota((major, major), 0)
+        lane = iota((major, major), 1)
+        turn = jnp.where(row + lane == major, 1.0, 0.0)
+        other = jnp.where(
+            iota((major, LANES), 0) == 0, back[:, LANES:], matmul(turn, back[:, :LANES])
+        )
+        return (lam + other) * (0.5 / (major * LANES))
+
+    def body(x_ref, first_ref, first_t_ref, second_ref, second_t_ref, turn_ref, o_ref, tile_ref):
         cos = turn_ref[0]
         sin = turn_ref[1]
-        for j in range(split):
+        for j in range(split + extra):
             tile_ref[j * width : (j + 1) * width, :] = x_ref[:, j * LANES : (j + 1) * LANES]
+        lam = symmetric_symbol(tile_ref)
 
         def column(c):
             return [
@@ -73,7 +138,6 @@
                 jnp.concatenate([real * cos + imag * sin, imag * cos - real * sin], 1)
             )
         spectra = matmul(jnp.concatenate(turned, 0), second_ref[...])
-        lam = lam_ref[...]
         lam = jnp.concatenate([lam, lam], 1)
         spectra = jnp.concatenate(
             [spectra[q * major : (q + 1) * major] * lam for q in range(pairs)], 0
@@ -100,40 +164,17 @@
     return body
 
 
-def circulant(columns, lam, devices):
-    width, rows_dev = columns.shape
-    split = rows_dev // LANES
+def circulant(columns, rows, devices):
+    width = columns.shape[0]
+    split = rows // LANES
+    tiles = columns.shape[1] // LANES
     return pl.pallas_call(
-        circulant_kernel(devices, split, width // devices),
-        out_shape=jax.ShapeDtypeStruct(columns.shape, jnp.float32),
-        scratch_shapes=[pltpu.VMEM((split * width, LANES), jnp.float32)],
+        circulant_kernel(devices, split, width // devices, tiles - split),
+        out_shape=jax.ShapeDtypeStruct((width, rows), jnp.float32),
+        scratch_shapes=[pltpu.VMEM((tiles * width, LANES), jnp.float32)],
         compiler_params=pltpu.CompilerParams(vmem_limit_bytes=48 << 20),
         name="circulant",
-    )(columns, lam, *tables(devices, split))
-
-
-def symmetric_symbol(every, devices):
-    split = every.shape[1] // LANES
-    major = devices * split
-    lam = every.reshape(devices, LANES, split).transpose(2, 0, 1).reshape(major, LANES)
-    head = lam[:1]
-    head = jnp.concatenate([head[:, :1], jnp.flip(head[:, 1:], 1)], 1)
-    back = jnp.concatenate([head, jnp.flip(lam[1:], (0, 1))], 0)
-    return (lam + back) * (0.5 / (major * LANES))
-
-
-def iota(shape, dim):
-    return lax.broadcasted_iota(jnp.int32, shape, dim)
-
-
-def times_transpose(left, right):
-    return lax.dot_general(
-        left,
-        right,
-        (((1,), (1,)), ((), ())),
-        precision=HIGHEST,
-        preferred_element_type=jnp.float32,
-    )
+    )(columns, *tables(devices, split))
 
 
 def gram_kernel(sample_ref, packed_ref):
@@ -303,16 +344,10 @@
 def local(probes, spectrum):
     devices = lax.axis_size("row") * lax.axis_size("col")
     axes = ("row", "col")
-    turned, spectrum = lax.optimization_barrier((probes.T, spectrum))
-    columns = lax.all_to_all(turned, axes, split_axis=0, concat_axis=0, tiled=True)
-    every = lax.all_to_all(
-        jnp.broadcast_to(spectrum, (devices, spectrum.shape[1])),
-        axes,
-        split_axis=0,
-        concat_axis=0,
-        tiled=True,
+    columns = lax.all_to_all(
+        spread(probes, spectrum, devices), axes, split_axis=0, concat_axis=0, tiled=True
     )
-    moved = circulant(columns, symmetric_symbol(every, devices), devices)
+    moved = circulant(columns, probes.shape[0], devices)
     sample_t = lax.all_to_all(moved, axes, split_axis=0, concat_axis=0, tiled=True)
     leaf = packed_gram(sample_t)
     pair = leaf + partner(leaf, "col", 0)

time: 87.9 us -> 80.3 us (0.914)
  waiting for transfers between devices: 23.8 us -> 11.3 us
  blocking collectives: 32.9 us -> 42.8 us
  local copies, waits for them, and re-layouts: 3.83 us -> 0.03 us
  starting transfers between devices: 6.55 us -> 3.81 us
  Pallas kernels: 18 us -> 20.4 us
    all_to_all x1 -> x0, waiting for transfers between devices: 12.5 us -> none  [local(): lax.all_to_all(turned, axes, split_axis=0, concat_axis=0, tiled=True)]
    all_to_all x1, blocking collectives: 14.6 us -> 24.2 us  [local(): lax.all_to_all(spread(probes, spectrum, devices), axes, split_axis=0, con...]
    all_to_all x1 -> x0, starting transfers between devices: 2.74 us -> none  [local(): lax.all_to_all(turned, axes, split_axis=0, concat_axis=0, tiled=True)]
    unnamed x17 -> x14, local copies, waits for them, and re-layouts: 2.75 us -> 0.03 us
    pallas_call x1 -> x2, Pallas kernels: 3.13 us -> 5.6 us  [the longest x1 3.38 us: circulant(): pl.pallas_call(circulant_kernel(devices, split, width // devices, tiles -...]
  transfers between devices with their start and end apart: 3 -> 2, of which waited for: 3 -> 2; matrix products, arithmetic and copies ran while one was open for 2% -> 0% of each run, Pallas kernels for 0% -> 0%
where the time goes in v3:
time: 80.3 us; the launch traced here: 80 us
  blocking collectives  42.8 us (53%)
  Pallas kernels  20.4 us (25%)
  waiting for transfers between devices  11.3 us (14%)
  starting transfers between devices  3.81 us (5%)
  other arithmetic  0.95 us (1%)
    all_to_all x1, blocking collectives, local(): lax.all_to_all(spread(probes, spectrum, devices), axes, split_axis=0, con...  24.2 us
    all_to_all x1, blocking collectives, local(): lax.all_to_all(moved, axes, split_axis=0, concat_axis=0, tiled=True)  18.6 us
    pallas_call x1, Pallas kernels, finish(): pl.pallas_call(finish_kernel, out_shape=[jax.ShapeDtypeStruct(shape, jnp....  12.3 us
    ppermute x2, waiting for transfers between devices, partner(): return lax.ppermute(value, axis, pairs)  11.3 us
    ppermute x2, starting transfers between devices, partner(): return lax.ppermute(value, axis, pairs)  3.81 us
    pallas_call x1, Pallas kernels, circulant(): pl.pallas_call(circulant_kernel(devices, split, width // devices, tiles -...  3.38 us
    pallas_call x1, Pallas kernels, packed_gram(): pl.pallas_call(gram_kernel, out_shape=jax.ShapeDtypeStruct((2 * LANES + 8...  2.53 us
    pallas_call x1, Pallas kernels, spread(): pl.pallas_call(spread_kernel(per_dev, extra), out_shape=jax.ShapeDtypeStr...  2.22 us
  transfers between devices with their start and end apart: 2, of which 2 were waited for; matrix products, arithmetic and copies ran while one was open for 0% of the time, Pallas kernels for 0%

profile of v3, /device:TPU:0, one launch (start us, length us, event | category | flops | bytes accessed | tf_op | source)
XLA Modules:
  0.0 80.0 jit_solution(16588022788549950924)
XLA Ops:
  0.6 2.2 %spread.1 = f32[256,640]{1,0:T(8,128)} custom-call(f32[512,256]{1,0:T(8,128)} %probes_ref.1, f32[1,512]{1,0:T(1,128)} %spectrum_ref.1), custom_call_target="tpu_custom_call" | custom-call | tf_op jit(solution)/shard_map/spread/pallas_call | solution.py:82
  2.8 0.0 copy-start.2
  2.8 0.0 copy-start.3
  2.9 0.0 copy-start.4
  2.9 0.0 copy-start.5
  2.9 0.0 copy-start.6
  2.9 24.2 %all_to_all.22 = f32[32,8,640]{2,1,0:T(8,128)S(1)} all-to-all(f32[32,8,640]{2,1,0:T(8,128)} %bitcast.9), channel_id=1, replica_groups=mesh['row'=8,'col'=4] {'row','col'}, dimensions={0} | all-to-all | bytes 1310720 | tf_op jit(solution)/shard_map/all_to_all | solution.py:347
  27.1 0.0 copy-done.2
  27.1 0.0 copy-done.3
  27.1 0.0 copy-done.4
  27.1 0.0 copy-done.5
  27.1 0.0 copy-done.6
  27.1 3.4 %circulant.1 = f32[256,512]{1,0:T(8,128)S(1)} custom-call(f32[256,640]{1,0:T(8,128)S(1)} %bitcast.7, f32[256,256]{1,0:T(8,128)S(1)} %copy-done.5, f32[256,256]{1,0:T(8,128)S(1)} %copy-done.4, f32[256,256]{1,0:T(8,128)S(1)} %copy-done.3, f32[256,256]{1,0:T(8,128)S(1)} %copy-done.2, f32[2,128,128]{2,1,0:T(8,128)S(1)} %copy-done.6), custom_call_target="tpu_custom_call" | custom-call | tf_op jit(solution)/shard_map/circulant/pallas_call | solution.py:171
  30.5 18.6 %all_to_all.23 = f32[32,8,512]{2,1,0:T(8,128)} all-to-all(f32[32,8,512]{2,1,0:T(8,128)S(1)} %bitcast.8), channel_id=1, replica_groups=mesh['row'=8,'col'=4] {'row','col'}, dimensions={0} | all-to-all | bytes 1048576 | tf_op jit(solution)/shard_map/all_to_all | solution.py:351
  49.1 2.5 %gram.1.leaf_ref = f32[264,128]{1,0:T(8,128)} custom-call(f32[256,512]{1,0:T(8,128)} %bitcast.5), custom_call_target="tpu_custom_call" | custom-call | tf_op jit(solution)/shard_map/gram/pallas_call | solution.py:194
  51.6 0.0 copy-start
  51.6 2.5 %collective-permute-start = (f32[264,128]{1,0:T(8,128)}, f32[264,128]{1,0:T(8,128)S(1)}, u32[]{:S(2)}, u32[]{:S(2)}) collective-permute-start(f32[264,128]{1,0:T(8,128)} %gram.1.leaf_ref), channel_id=1, source_target_pairs={{0,1},{1,0},{2,3},{3,2},{4,5},{5,4},{6,7},{7,6},{8,9},{9,8},{10,11... | collective-permute-start | bytes 405512 | tf_op jit(solution)/shard_map/ppermute | solution.py:18
  54.2 4.3 %collective-permute-done = f32[264,128]{1,0:T(8,128)S(1)} collective-permute-done((f32[264,128]{1,0:T(8,128)}, f32[264,128]{1,0:T(8,128)S(1)}, u32[]{:S(2)}, u32[]{:S(2)}) %collective-permute-start) | collective-permute-done | bytes 135200 | tf_op jit(solution)/shard_map/ppermute | solution.py:18
  58.5 0.9 %add.6.pair_ref = f32[264,128]{1,0:T(8,128)S(1)} add(f32[264,128]{1,0:T(8,128)} %gram.1.leaf_ref, f32[264,128]{1,0:T(8,128)S(1)} %collective-permute-done) | non-fusion elementwise | flops 33792 | bytes 405504 | tf_op jit(solution)/shard_map/add | solution.py:353
  59.4 1.3 %collective-permute-start.1 = (f32[264,128]{1,0:T(8,128)S(1)}, f32[264,128]{1,0:T(8,128)S(1)}, u32[]{:S(2)}, u32[]{:S(2)}) collective-permute-start(f32[264,128]{1,0:T(8,128)S(1)} %add.6.pair_ref), channel_id=1, source_target_pairs={{0,2},{1,3},{2,0},{3,1},{4,6},{5,7},{6,4},{7,5},{8,10},{9,11},{10,... | collective-permute-start | bytes 405512 | tf_op jit(solution)/shard_map/ppermute | solution.py:18
  60.7 7.0 %collective-permute-done.1 = f32[264,128]{1,0:T(8,128)S(1)} collective-permute-done((f32[264,128]{1,0:T(8,128)S(1)}, f32[264,128]{1,0:T(8,128)S(1)}, u32[]{:S(2)}, u32[]{:S(2)}) %collective-permute-start.1) | collective-permute-done | bytes 135200 | tf_op jit(solution)/shard_map/ppermute | solution.py:18
  67.7 0.0 copy-done
  67.7 0.0 copy-done.1
  67.7 12.3 %finish.1 = (f32[512,256]{1,0:T(8,128)}, f32[256,256]{1,0:T(8,128)}, f32[128,256]{1,0:T(8,128)}, f32[64,256]{1,0:T(8,128)}) custom-call(s32[1]{0:T(128)} %bitcast.place_ref, f32[256,512]{1,0:T(8,128)S(1)} %bitcast.6, f32[264,128]{1,0:T(8,128)S(1)} %copy-done.1, f32[264,128]{1,0:T(8,128)S(1)} %add.6.pair_ref, f32[264,128]{1,0:T(8,128)S(1)} %add.7.group_ref), custom_call_target="tpu_custom_call" | custom-call | tf_op jit(solution)/shard_map/finish/pallas_call | solution.py:330
  (2 shorter events, 0.0 us)
Async XLA Ops:
  2.8 24.3 %copy-start.2 = (f32[256,256]{1,0:T(8,128)S(1)}, f32[256,256]{1,0:T(8,128)}, u32[]{:S(2)}) copy-start(f32[256,256]{1,0:T(8,128)} %constant.17.clone.second_t_ref) | copy-start | bytes 786436
  2.8 24.3 %copy-start.3 = (f32[256,256]{1,0:T(8,128)S(1)}, f32[256,256]{1,0:T(8,128)}, u32[]{:S(2)}) copy-start(f32[256,256]{1,0:T(8,128)} %constant.16.clone.second_ref) | copy-start | bytes 786436
  2.9 24.3 %copy-start.4 = (f32[256,256]{1,0:T(8,128)S(1)}, f32[256,256]{1,0:T(8,128)}, u32[]{:S(2)}) copy-start(f32[256,256]{1,0:T(8,128)} %constant.15.clone.first_t_ref) | copy-start | bytes 786436
  2.9 24.3 %copy-start.5 = (f32[256,256]{1,0:T(8,128)S(1)}, f32[256,256]{1,0:T(8,128)}, u32[]{:S(2)}) copy-start(f32[256,256]{1,0:T(8,128)} %constant.14.clone.first_ref) | copy-start | bytes 786436
  2.9 24.3 %copy-start.6 = (f32[2,128,128]{2,1,0:T(8,128)S(1)}, f32[2,128,128]{2,1,0:T(8,128)}, u32[]{:S(2)}) copy-start(f32[2,128,128]{2,1,0:T(8,128)} %constant.18.clone.turn_ref) | copy-start | bytes 393220
  51.6 16.1 %copy-start = (f32[32,8,512]{2,1,0:T(8,128)S(1)}, f32[32,8,512]{2,1,0:T(8,128)}, u32[]{:S(2)}) copy-start(f32[32,8,512]{2,1,0:T(8,128)} %all_to_all.23) | copy-start | bytes 1572868
  51.6 6.9 %collective-permute-start = (f32[264,128]{1,0:T(8,128)}, f32[264,128]{1,0:T(8,128)S(1)}, u32[]{:S(2)}, u32[]{:S(2)}) collective-permute-start(f32[264,128]{1,0:T(8,128)} %gram.1.leaf_ref), channel_id=1, source_target_pairs={{0,1},{1,0},{2,3},{3,2},{4,5},{5,4},{6,7},{7,6},{8,9},{9,8},{10,11... | collective-permute-start | bytes 405512 | tf_op jit(solution)/shard_map/ppermute | solution.py:18
  59.4 8.2 %collective-permute-start.1 = (f32[264,128]{1,0:T(8,128)S(1)}, f32[264,128]{1,0:T(8,128)S(1)}, u32[]{:S(2)}, u32[]{:S(2)}) collective-permute-start(f32[264,128]{1,0:T(8,128)S(1)} %add.6.pair_ref), channel_id=1, source_target_pairs={{0,2},{1,3},{2,0},{3,1},{4,6},{5,7},{6,4},{7,5},{8,10},{9,11},{10,... | collective-permute-start | bytes 405512 | tf_op jit(solution)/shard_map/ppermute | solution.py:18
  60.7 7.0 %copy-start.1 = (f32[264,128]{1,0:T(8,128)S(1)}, f32[264,128]{1,0:T(8,128)}, u32[]{:S(2)}) copy-start(f32[264,128]{1,0:T(8,128)} %gram.1.leaf_ref) | copy-start | bytes 405508

commit v4 on v3

--- a/solution.py
+++ b/solution.py
@@ -205,21 +205,24 @@
     return high, middle, rest - middle
 
 
-def eliminate(tile_ref, problems, width, block):
+def eliminate(tile_ref, done_ref, problems, width, block):
     tiles = width // LANES
     thin = iota((problems, LANES), 1)
-    for base in range(0, width, block):
-        own = base // LANES
-        offset = base % LANES
-        order = [own] + [t for t in range(tiles) if t != own]
-        panel = [
-            [tile_ref[t, pl.ds(base + i, problems, stride=width), :] for t in order]
+
+    def across(value, lane):
+        return jnp.broadcast_to(value[:, lane : lane + 1], (problems, LANES))
+
+    def load(base):
+        return [
+            [tile_ref[t, pl.ds(base + i, problems, stride=width), :] for t in range(tiles)]
             for i in range(block)
         ]
+
+    panel = load(0)
+    for base in range(0, width, block):
+        own, offset = divmod(base, LANES)
         entry = {
-            (i, j): jnp.broadcast_to(
-                panel[i][0][:, offset + j : offset + j + 1], (problems, LANES)
-            )
+            (i, j): across(panel[i][own], offset + j)
             for i in range(block)
             for j in range(i, block)
         }
@@ -227,31 +230,44 @@
             scale = lax.rsqrt(entry[j, j])
             factor = {i: entry[j, i] * scale for i in range(j + 1, block)}
             hot = thin == offset + j
-            panel[j] = [jnp.where(hot, 1.0, panel[j][0]) * scale] + [
-                x * scale for x in panel[j][1:]
-            ]
+            panel[j][own] = jnp.where(hot, 1.0, panel[j][own])
+            panel[j] = [x * scale for x in panel[j]]
             for i in range(j + 1, block):
                 for l in range(i, block):
                     entry[i, l] = entry[i, l] - factor[i] * factor[l]
-                kept = [jnp.where(hot, 0.0, panel[i][0])] + panel[i][1:]
-                panel[i] = [x - factor[i] * y for x, y in zip(kept, panel[j])]
-            for x, t in zip(panel[j], order):
-                tile_ref[t, pl.ds(base + j, problems, stride=width), :] = x
+                panel[i][own] = jnp.where(hot, 0.0, panel[i][own])
+                panel[i] = [x - factor[i] * y for x, y in zip(panel[i], panel[j])]
+            for t in range(tiles):
+                done_ref[t, pl.ds(base + j, problems, stride=width), :] = panel[j][t]
         after = base + block
         if after == width:
+            break
+        inside = (thin >= offset) & (thin < offset + block)
+        clean = [list(rows) for rows in panel]
+        for j in range(block):
+            clean[j][own] = jnp.where(inside & (thin > offset + j), 0.0, panel[j][own])
+        ahead = load(after)
+        for i in range(block):
+            ahead[i][own] = jnp.where(inside, 0.0, ahead[i][own])
+            for j in range(block):
+                weight = across(panel[j][after // LANES], after % LANES + i)
+                ahead[i] = [x - weight * y for x, y in zip(ahead[i], clean[j])]
+        panel = ahead
+        past = after + block
+        if past == width:
             continue
-        first = after // LANES * LANES
+        first = past // LANES
         lane = iota((block, LANES), 1) - offset
         inverse = (lane < 0) | (lane >= block) | (lane <= iota((block, LANES), 0))
-        below = iota((width - after, LANES), 1) - offset
+        below = iota((width - past, LANES), 1) - offset
         below = (below >= 0) & (below < block)
         for p in range(problems):
             start = p * width
-            rows = [parts(tile_ref[t, start + base : start + after, :]) for t in range(tiles)]
+            rows = [parts(done_ref[t, start + base : start + after, :]) for t in range(tiles)]
             left = jnp.concatenate(
                 [
                     jnp.concatenate([rows[t][q] for q in (0, 0, 1, 1, 0, 2)], 0)
-                    for t in range(first // LANES, tiles)
+                    for t in range(first, tiles)
                 ],
                 1,
             ).astype(jnp.bfloat16)
@@ -267,11 +283,11 @@
                 left, right, (((0,), (0,)), ((), ())), preferred_element_type=jnp.float32
             )
             for t in range(tiles):
-                old = tile_ref[t, start + after : start + width, :]
+                old = tile_ref[t, start + past : start + width, :]
                 if t == own:
                     old = jnp.where(below, 0.0, old)
-                tile_ref[t, start + after : start + width, :] = (
-                    old - update[after - first :, t * LANES : (t + 1) * LANES]
+                tile_ref[t, start + past : start + width, :] = (
+                    old - update[past - first * LANES :, t * LANES : (t + 1) * LANES]
                 )
 
 
@@ -286,6 +302,7 @@
     pair_transfer_ref,
     group_factor_ref,
     tile_ref,
+    done_ref,
     upper_ref,
 ):
     width = sample_ref.shape[0]
@@ -301,13 +318,13 @@
         tile_ref[1, start + LANES : start + width, :] = jnp.where(
             lane == row, diagonal, shared.T
         )
-    eliminate(tile_ref, 3, width, 16)
+    eliminate(tile_ref, done_ref, 3, width, 8)
     row = iota((width, width), 0)
     lane = iota((width, width), 1)
     inverse = []
     for p in range(3):
         start = p * width
-        whole = jnp.concatenate([tile_ref[t, start : start + width, :] for t in range(2)], 1)
+        whole = jnp.concatenate([done_ref[t, start : start + width, :] for t in range(2)], 1)
         inverse.append(jnp.where(lane <= row, whole, 0.0))
         upper_ref[p] = jnp.where(
             lane > row, whole, jnp.where(lane == row, 1.0 / whole, 0.0)
@@ -333,6 +350,7 @@
         in_specs=[pl.BlockSpec(memory_space=pltpu.SMEM)]
         + [pl.BlockSpec(memory_space=pltpu.VMEM)] * 4,
         scratch_shapes=[
+            pltpu.VMEM((width // LANES, 3 * width, LANES), jnp.float32),
             pltpu.VMEM((width // LANES, 3 * width, LANES), jnp.float32),
             pltpu.VMEM((3, width, width), jnp.float32),
         ],

time: 80.3 us -> 79.4 us (0.989)
  Pallas kernels: 20.4 us -> 19.5 us
    pallas_call x1, Pallas kernels: 12.3 us -> 11.4 us  [finish(): pl.pallas_call(finish_kernel, out_shape=[jax.ShapeDtypeStruct(shape, jnp....]
where the time goes in v4:
time: 79.4 us; the launch traced here: 79.1 us
  blocking collectives  42.8 us (54%)
  Pallas kernels  19.5 us (25%)
  waiting for transfers between devices  11.3 us (14%)
  starting transfers between devices  3.81 us (5%)
  other arithmetic  0.95 us (1%)
    all_to_all x1, blocking collectives, local(): lax.all_to_all(spread(probes, spectrum, devices), axes, split_axis=0, con...  24.2 us
    all_to_all x1, blocking collectives, local(): lax.all_to_all(moved, axes, split_axis=0, concat_axis=0, tiled=True)  18.6 us
    pallas_call x1, Pallas kernels, finish(): pl.pallas_call(finish_kernel, out_shape=[jax.ShapeDtypeStruct(shape, jnp....  11.4 us
    ppermute x2, waiting for transfers between devices, partner(): return lax.ppermute(value, axis, pairs)  11.3 us
    ppermute x2, starting transfers between devices, partner(): return lax.ppermute(value, axis, pairs)  3.81 us
    pallas_call x1, Pallas kernels, circulant(): pl.pallas_call(circulant_kernel(devices, split, width // devices, tiles -...  3.38 us
    pallas_call x1, Pallas kernels, packed_gram(): pl.pallas_call(gram_kernel, out_shape=jax.ShapeDtypeStruct((2 * LANES + 8...  2.53 us
    pallas_call x1, Pallas kernels, spread(): pl.pallas_call(spread_kernel(per_dev, extra), out_shape=jax.ShapeDtypeStr...  2.22 us
  transfers between devices with their start and end apart: 2, of which 2 were waited for; matrix products, arithmetic and copies ran while one was open for 0% of the time, Pallas kernels for 0%

profile of v4, /device:TPU:0, one launch (start us, length us, event | category | flops | bytes accessed | tf_op | source)
XLA Modules:
  0.0 79.1 jit_solution(11036350295210118498)
XLA Ops:
  0.6 2.2 %spread.1 = f32[256,640]{1,0:T(8,128)} custom-call(f32[512,256]{1,0:T(8,128)} %probes_ref.1, f32[1,512]{1,0:T(1,128)} %spectrum_ref.1), custom_call_target="tpu_custom_call" | custom-call | tf_op jit(solution)/shard_map/spread/pallas_call | solution.py:82
  2.8 0.0 copy-start.2
  2.8 0.0 copy-start.3
  2.9 0.0 copy-start.4
  2.9 0.0 copy-start.5
  2.9 0.0 copy-start.6
  2.9 24.2 %all_to_all.22 = f32[32,8,640]{2,1,0:T(8,128)S(1)} all-to-all(f32[32,8,640]{2,1,0:T(8,128)} %bitcast.9), channel_id=1, replica_groups=mesh['row'=8,'col'=4] {'row','col'}, dimensions={0} | all-to-all | bytes 1310720 | tf_op jit(solution)/shard_map/all_to_all | solution.py:365
  27.1 0.0 copy-done.2
  27.1 0.0 copy-done.3
  27.1 0.0 copy-done.4
  27.1 0.0 copy-done.5
  27.1 0.0 copy-done.6
  27.1 3.4 %circulant.1 = f32[256,512]{1,0:T(8,128)S(1)} custom-call(f32[256,640]{1,0:T(8,128)S(1)} %bitcast.7, f32[256,256]{1,0:T(8,128)S(1)} %copy-done.5, f32[256,256]{1,0:T(8,128)S(1)} %copy-done.4, f32[256,256]{1,0:T(8,128)S(1)} %copy-done.3, f32[256,256]{1,0:T(8,128)S(1)} %copy-done.2, f32[2,128,128]{2,1,0:T(8,128)S(1)} %copy-done.6), custom_call_target="tpu_custom_call" | custom-call | tf_op jit(solution)/shard_map/circulant/pallas_call | solution.py:171
  30.5 18.6 %all_to_all.23 = f32[32,8,512]{2,1,0:T(8,128)} all-to-all(f32[32,8,512]{2,1,0:T(8,128)S(1)} %bitcast.8), channel_id=1, replica_groups=mesh['row'=8,'col'=4] {'row','col'}, dimensions={0} | all-to-all | bytes 1048576 | tf_op jit(solution)/shard_map/all_to_all | solution.py:369
  49.1 2.5 %gram.1.leaf_ref = f32[264,128]{1,0:T(8,128)} custom-call(f32[256,512]{1,0:T(8,128)} %bitcast.5), custom_call_target="tpu_custom_call" | custom-call | tf_op jit(solution)/shard_map/gram/pallas_call | solution.py:194
  51.6 0.0 copy-start
  51.6 2.5 %collective-permute-start = (f32[264,128]{1,0:T(8,128)}, f32[264,128]{1,0:T(8,128)S(1)}, u32[]{:S(2)}, u32[]{:S(2)}) collective-permute-start(f32[264,128]{1,0:T(8,128)} %gram.1.leaf_ref), channel_id=1, source_target_pairs={{0,1},{1,0},{2,3},{3,2},{4,5},{5,4},{6,7},{7,6},{8,9},{9,8},{10,11... | collective-permute-start | bytes 405512 | tf_op jit(solution)/shard_map/ppermute | solution.py:18
  54.2 4.3 %collective-permute-done = f32[264,128]{1,0:T(8,128)S(1)} collective-permute-done((f32[264,128]{1,0:T(8,128)}, f32[264,128]{1,0:T(8,128)S(1)}, u32[]{:S(2)}, u32[]{:S(2)}) %collective-permute-start) | collective-permute-done | bytes 135200 | tf_op jit(solution)/shard_map/ppermute | solution.py:18
  58.5 0.9 %add.6.pair_ref = f32[264,128]{1,0:T(8,128)S(1)} add(f32[264,128]{1,0:T(8,128)} %gram.1.leaf_ref, f32[264,128]{1,0:T(8,128)S(1)} %collective-permute-done) | non-fusion elementwise | flops 33792 | bytes 405504 | tf_op jit(solution)/shard_map/add | solution.py:371
  59.4 1.3 %collective-permute-start.1 = (f32[264,128]{1,0:T(8,128)S(1)}, f32[264,128]{1,0:T(8,128)S(1)}, u32[]{:S(2)}, u32[]{:S(2)}) collective-permute-start(f32[264,128]{1,0:T(8,128)S(1)} %add.6.pair_ref), channel_id=1, source_target_pairs={{0,2},{1,3},{2,0},{3,1},{4,6},{5,7},{6,4},{7,5},{8,10},{9,11},{10,... | collective-permute-start | bytes 405512 | tf_op jit(solution)/shard_map/ppermute | solution.py:18
  60.7 7.0 %collective-permute-done.1 = f32[264,128]{1,0:T(8,128)S(1)} collective-permute-done((f32[264,128]{1,0:T(8,128)S(1)}, f32[264,128]{1,0:T(8,128)S(1)}, u32[]{:S(2)}, u32[]{:S(2)}) %collective-permute-start.1) | collective-permute-done | bytes 135200 | tf_op jit(solution)/shard_map/ppermute | solution.py:18
  67.7 0.0 copy-done
  67.7 0.0 copy-done.1
  67.7 11.4 %finish.1 = (f32[512,256]{1,0:T(8,128)}, f32[256,256]{1,0:T(8,128)}, f32[128,256]{1,0:T(8,128)}, f32[64,256]{1,0:T(8,128)}) custom-call(s32[1]{0:T(128)} %bitcast.place_ref, f32[256,512]{1,0:T(8,128)S(1)} %bitcast.6, f32[264,128]{1,0:T(8,128)S(1)} %copy-done.1, f32[264,128]{1,0:T(8,128)S(1)} %add.6.pair_ref, f32[264,128]{1,0:T(8,128)S(1)} %add.7.group_ref), custom_call_target="tpu_custom_call" | custom-call | tf_op jit(solution)/shard_map/finish/pallas_call | solution.py:347
  (2 shorter events, 0.0 us)
Async XLA Ops:
  2.8 24.3 %copy-start.2 = (f32[256,256]{1,0:T(8,128)S(1)}, f32[256,256]{1,0:T(8,128)}, u32[]{:S(2)}) copy-start(f32[256,256]{1,0:T(8,128)} %constant.17.clone.second_t_ref) | copy-start | bytes 786436
  2.8 24.3 %copy-start.3 = (f32[256,256]{1,0:T(8,128)S(1)}, f32[256,256]{1,0:T(8,128)}, u32[]{:S(2)}) copy-start(f32[256,256]{1,0:T(8,128)} %constant.16.clone.second_ref) | copy-start | bytes 786436
  2.9 24.3 %copy-start.4 = (f32[256,256]{1,0:T(8,128)S(1)}, f32[256,256]{1,0:T(8,128)}, u32[]{:S(2)}) copy-start(f32[256,256]{1,0:T(8,128)} %constant.15.clone.first_t_ref) | copy-start | bytes 786436
  2.9 24.3 %copy-start.5 = (f32[256,256]{1,0:T(8,128)S(1)}, f32[256,256]{1,0:T(8,128)}, u32[]{:S(2)}) copy-start(f32[256,256]{1,0:T(8,128)} %constant.14.clone.first_ref) | copy-start | bytes 786436
  2.9 24.3 %copy-start.6 = (f32[2,128,128]{2,1,0:T(8,128)S(1)}, f32[2,128,128]{2,1,0:T(8,128)}, u32[]{:S(2)}) copy-start(f32[2,128,128]{2,1,0:T(8,128)} %constant.18.clone.turn_ref) | copy-start | bytes 393220
  51.6 16.1 %copy-start = (f32[32,8,512]{2,1,0:T(8,128)S(1)}, f32[32,8,512]{2,1,0:T(8,128)}, u32[]{:S(2)}) copy-start(f32[32,8,512]{2,1,0:T(8,128)} %all_to_all.23) | copy-start | bytes 1572868
  51.6 6.9 %collective-permute-start = (f32[264,128]{1,0:T(8,128)}, f32[264,128]{1,0:T(8,128)S(1)}, u32[]{:S(2)}, u32[]{:S(2)}) collective-permute-start(f32[264,128]{1,0:T(8,128)} %gram.1.leaf_ref), channel_id=1, source_target_pairs={{0,1},{1,0},{2,3},{3,2},{4,5},{5,4},{6,7},{7,6},{8,9},{9,8},{10,11... | collective-permute-start | bytes 405512 | tf_op jit(solution)/shard_map/ppermute | solution.py:18
  59.4 8.2 %collective-permute-start.1 = (f32[264,128]{1,0:T(8,128)S(1)}, f32[264,128]{1,0:T(8,128)S(1)}, u32[]{:S(2)}, u32[]{:S(2)}) collective-permute-start(f32[264,128]{1,0:T(8,128)S(1)} %add.6.pair_ref), channel_id=1, source_target_pairs={{0,2},{1,3},{2,0},{3,1},{4,6},{5,7},{6,4},{7,5},{8,10},{9,11},{10,... | collective-permute-start | bytes 405512 | tf_op jit(solution)/shard_map/ppermute | solution.py:18
  60.7 7.0 %copy-start.1 = (f32[264,128]{1,0:T(8,128)S(1)}, f32[264,128]{1,0:T(8,128)}, u32[]{:S(2)}) copy-start(f32[264,128]{1,0:T(8,128)} %gram.1.leaf_ref) | copy-start | bytes 405508

commit v5 on v4

--- a/solution.py
+++ b/solution.py
@@ -12,8 +12,7 @@
 HIGHEST = lax.Precision.HIGHEST
 
 
-def partner(value, axis, distance):
-    mask = 2**distance
+def partner(value, axis, mask):
     pairs = [(source, source ^ mask) for source in range(lax.axis_size(axis))]
     return lax.ppermute(value, axis, pairs)
 
@@ -177,25 +176,16 @@
     )(columns, *tables(devices, split))
 
 
-def gram_kernel(sample_ref, packed_ref):
-    width, rows = sample_ref.shape
-    upper = times_transpose(sample_ref[:LANES, :], sample_ref[...]) * (1.0 / rows)
-    last = sample_ref[LANES:, :]
-    last = times_transpose(last, last) * (1.0 / rows)
+def packed_gram(sample_t):
+    gram = times_transpose(sample_t, sample_t) * (1.0 / sample_t.shape[1])
     row = iota((LANES, LANES), 0)
     lane = iota((LANES, LANES), 1)
-    packed_ref[:LANES, :] = jnp.where(lane >= row, upper[:, :LANES], last)
-    packed_ref[LANES : 2 * LANES, :] = upper[:, LANES:]
+    last = gram[LANES:, LANES:]
+    shared = jnp.where(lane >= row, gram[:LANES, :LANES], last)
     diagonal = jnp.sum(jnp.where(lane == row, last, 0.0), axis=0, keepdims=True)
-    packed_ref[2 * LANES :, :] = jnp.broadcast_to(diagonal, (8, LANES))
-
-
-def packed_gram(sample_t):
-    return pl.pallas_call(
-        gram_kernel,
-        out_shape=jax.ShapeDtypeStruct((2 * LANES + 8, LANES), jnp.float32),
-        name="gram",
-    )(sample_t)
+    return jnp.concatenate(
+        [shared, gram[:LANES, LANES:], jnp.broadcast_to(diagonal, (8, LANES))], 0
+    )
 
 
 def parts(value):
@@ -291,13 +281,41 @@
                 )
 
 
-def finish_kernel(
+def unpack(packed, tile_ref, start, width):
+    row = iota((LANES, LANES), 0)
+    lane = iota((LANES, LANES), 1)
+    shared = packed[:LANES, :]
+    tile_ref[0, start : start + LANES, :] = shared
+    tile_ref[0, start + LANES : start + width, :] = jnp.zeros((LANES, LANES), jnp.float32)
+    tile_ref[1, start : start + LANES, :] = packed[LANES : 2 * LANES, :]
+    diagonal = jnp.broadcast_to(packed[2 * LANES : 2 * LANES + 1, :], (LANES, LANES))
+    tile_ref[1, start + LANES : start + width, :] = jnp.where(lane == row, diagonal, shared.T)
+
+
+def factors(done_ref, start, width):
+    row = iota((width, width), 0)
+    lane = iota((width, width), 1)
+    whole = jnp.concatenate([done_ref[t, start : start + width, :] for t in range(2)], 1)
+    upper = jnp.where(lane > row, whole, jnp.where(lane == row, 1.0 / whole, 0.0))
+    return upper, jnp.where(lane <= row, whole, 0.0)
+
+
+def leaf_kernel(sample_ref, packed_ref, basis_ref, upper_ref, tile_ref, done_ref):
+    width = sample_ref.shape[0]
+    unpack(packed_ref[...], tile_ref, 0, width)
+    eliminate(tile_ref, done_ref, 1, width, 8)
+    upper, inverse = factors(done_ref, 0, width)
+    upper_ref[...] = upper
+    basis_ref[...] = times_transpose(sample_ref[...].T, inverse)
+
+
+def group_kernel(
     place_ref,
-    sample_ref,
     leaf_ref,
-    pair_ref,
-    group_ref,
-    basis_ref,
+    near_ref,
+    far_ref,
+    last_ref,
+    leaf_upper_ref,
     leaf_transfer_ref,
     pair_transfer_ref,
     group_factor_ref,
@@ -305,58 +323,52 @@
     done_ref,
     upper_ref,
 ):
-    width = sample_ref.shape[0]
-    row = iota((LANES, LANES), 0)
-    lane = iota((LANES, LANES), 1)
-    for p, packed_ref in enumerate((leaf_ref, pair_ref, group_ref)):
-        start = p * width
-        shared = packed_ref[:LANES, :]
-        tile_ref[0, start : start + LANES, :] = shared
-        tile_ref[0, start + LANES : start + width, :] = jnp.zeros((LANES, LANES), jnp.float32)
-        tile_ref[1, start : start + LANES, :] = packed_ref[LANES : 2 * LANES, :]
-        diagonal = jnp.broadcast_to(packed_ref[2 * LANES : 2 * LANES + 1, :], (LANES, LANES))
-        tile_ref[1, start + LANES : start + width, :] = jnp.where(
-            lane == row, diagonal, shared.T
-        )
-    eliminate(tile_ref, done_ref, 3, width, 8)
-    row = iota((width, width), 0)
-    lane = iota((width, width), 1)
-    inverse = []
-    for p in range(3):
-        start = p * width
-        whole = jnp.concatenate([done_ref[t, start : start + width, :] for t in range(2)], 1)
-        inverse.append(jnp.where(lane <= row, whole, 0.0))
-        upper_ref[p] = jnp.where(
-            lane > row, whole, jnp.where(lane == row, 1.0 / whole, 0.0)
-        )
-    basis_ref[...] = times_transpose(sample_ref[...].T, inverse[0])
-    leaf_transfer_ref[...] = times_transpose(upper_ref[0], inverse[1])
+    width = leaf_upper_ref.shape[0]
+    pair = leaf_ref[...] + near_ref[...]
+    unpack(pair, tile_ref, 0, width)
+    unpack(pair + (far_ref[...] + last_ref[...]), tile_ref, width, width)
+    eliminate(tile_ref, done_ref, 2, width, 8)
+    upper_ref[0], pair_inverse = factors(done_ref, 0, width)
+    upper_ref[1], group_inverse = factors(done_ref, width, width)
+    leaf_transfer_ref[...] = times_transpose(leaf_upper_ref[...], pair_inverse)
     half = width // 2
     quarter = width // 4
     place = place_ref[0]
-    pair_upper = upper_ref[1, pl.ds(pl.multiple_of(place % 2 * half, half), half), :]
-    pair_transfer_ref[...] = times_transpose(pair_upper, inverse[2])
+    pair_upper = upper_ref[0, pl.ds(pl.multiple_of(place % 2 * half, half), half), :]
+    pair_transfer_ref[...] = times_transpose(pair_upper, group_inverse)
     group_factor_ref[...] = upper_ref[
-        2, pl.ds(pl.multiple_of(place % 4 * quarter, quarter), quarter), :
+        1, pl.ds(pl.multiple_of(place % 4 * quarter, quarter), quarter), :
     ]
 
 
-def finish(place, sample_t, leaf, pair, group):
+def scratch(problems, width):
+    tiles = width // LANES
+    return [pltpu.VMEM((tiles, problems * width, LANES), jnp.float32)] * 2
+
+
+def leaf_factor(sample_t, leaf):
     width, rows = sample_t.shape
-    shapes = [(rows, width), (width, width), (width // 2, width), (width // 4, width)]
     return pl.pallas_call(
-        finish_kernel,
+        leaf_kernel,
+        out_shape=[jax.ShapeDtypeStruct(shape, jnp.float32) for shape in ((rows, width), (width, width))],
+        scratch_shapes=scratch(1, width),
+        compiler_params=pltpu.CompilerParams(vmem_limit_bytes=24 << 20),
+        name="leaf",
+    )(sample_t, leaf)
+
+
+def group_factors(place, leaf, near, far, last, leaf_upper):
+    width = leaf_upper.shape[0]
+    shapes = [(width, width), (width // 2, width), (width // 4, width)]
+    return pl.pallas_call(
+        group_kernel,
         out_shape=[jax.ShapeDtypeStruct(shape, jnp.float32) for shape in shapes],
         in_specs=[pl.BlockSpec(memory_space=pltpu.SMEM)]
-        + [pl.BlockSpec(memory_space=pltpu.VMEM)] * 4,
-        scratch_shapes=[
-            pltpu.VMEM((width // LANES, 3 * width, LANES), jnp.float32),
-            pltpu.VMEM((width // LANES, 3 * width, LANES), jnp.float32),
-            pltpu.VMEM((3, width, width), jnp.float32),
-        ],
-        compiler_params=pltpu.CompilerParams(vmem_limit_bytes=48 << 20),
-        name="finish",
-    )(place, sample_t, leaf, pair, group)
+        + [pl.BlockSpec(memory_space=pltpu.VMEM)] * 5,
+        scratch_shapes=scratch(2, width) + [pltpu.VMEM((2, width, width), jnp.float32)],
+        compiler_params=pltpu.CompilerParams(vmem_limit_bytes=24 << 20),
+        name="group",
+    )(place, leaf, near, far, last, leaf_upper)
 
 
 def local(probes, spectrum):
@@ -368,10 +380,10 @@
     moved = circulant(columns, probes.shape[0], devices)
     sample_t = lax.all_to_all(moved, axes, split_axis=0, concat_axis=0, tiled=True)
     leaf = packed_gram(sample_t)
-    pair = leaf + partner(leaf, "col", 0)
-    group = pair + partner(pair, "col", 1)
+    near, far, last = (partner(leaf, "col", mask) for mask in (1, 2, 3))
+    leaf_basis, leaf_upper = leaf_factor(sample_t, leaf)
     place = lax.axis_index("col").reshape(1).astype(jnp.int32)
-    return tuple(finish(place, sample_t, leaf, pair, group))
+    return (leaf_basis, *group_factors(place, leaf, near, far, last, leaf_upper))
 
 
 def solution(mesh):

time: 79.4 us -> 75.1 us (0.946)
  waiting for transfers between devices: 11.3 us -> 0.56 us
  Pallas kernels: 19.5 us -> 25.2 us
  starting transfers between devices: 3.81 us -> 5.05 us
  other arithmetic: 0.95 us -> 0.05 us
    ppermute x2 -> x3, waiting for transfers between devices: 11.3 us -> 0.56 us  [partner(): return lax.ppermute(value, axis, pairs)]
    pallas_call x2, Pallas kernels: 13.9 us -> 19.6 us  [the longest x1 10.2 us: group_factors(): pl.pallas_call(group_kernel, out_shape=[jax.ShapeDtypeStruct(shape, jnp.f...]
    ppermute x2 -> x3, starting transfers between devices: 3.81 us -> 5.05 us  [partner(): return lax.ppermute(value, axis, pairs)]
    add x2 -> x0, other arithmetic: 0.95 us -> none  [the longest x1 0.93 us: local(): pair = leaf + partner(leaf, 'col', 0)]
  transfers between devices with their start and end apart: 2 -> 3, of which waited for: 2 -> 1; matrix products, arithmetic and copies ran while one was open for 0% -> 0% of each run, Pallas kernels for 0% -> 13%
where the time goes in v5:
time: 75.1 us; the launch traced here: 74.9 us
  blocking collectives  42.7 us (57%)
  Pallas kernels  25.2 us (34%)
  starting transfers between devices  5.05 us (7%)
    all_to_all x1, blocking collectives, local(): lax.all_to_all(spread(probes, spectrum, devices), axes, split_axis=0, con...  24.2 us
    all_to_all x1, blocking collectives, local(): lax.all_to_all(moved, axes, split_axis=0, concat_axis=0, tiled=True)  18.5 us
    pallas_call x1, Pallas kernels, group_factors(): pl.pallas_call(group_kernel, out_shape=[jax.ShapeDtypeStruct(shape, jnp.f...  10.2 us
    pallas_call x1, Pallas kernels, leaf_factor(): pl.pallas_call(leaf_kernel, out_shape=[jax.ShapeDtypeStruct(shape, jnp.fl...  9.38 us
    ppermute x3, starting transfers between devices, partner(): return lax.ppermute(value, axis, pairs)  5.05 us
    pallas_call x1, Pallas kernels, circulant(): pl.pallas_call(circulant_kernel(devices, split, width // devices, tiles -...  3.38 us
    pallas_call x1, Pallas kernels, spread(): pl.pallas_call(spread_kernel(per_dev, extra), out_shape=jax.ShapeDtypeStr...  2.22 us
  transfers between devices with their start and end apart: 3, of which 1 were waited for; matrix products, arithmetic and copies ran while one was open for 0% of the time, Pallas kernels for 13%

profile of v5, /device:TPU:0, one launch (start us, length us, event | category | flops | bytes accessed | tf_op | source)
XLA Modules:
  0.0 74.9 jit_solution(12100829902144982080)
XLA Ops:
  0.6 2.2 %spread.1 = f32[256,640]{1,0:T(8,128)} custom-call(f32[512,256]{1,0:T(8,128)} %probes_ref.1, f32[1,512]{1,0:T(1,128)} %spectrum_ref.1), custom_call_target="tpu_custom_call" | custom-call | tf_op jit(solution)/shard_map/spread/pallas_call | solution.py:81
  2.8 0.0 copy-start
  2.8 0.0 copy-start.1
  2.9 0.0 copy-start.2
  2.9 0.0 copy-start.3
  2.9 0.0 copy-start.4
  2.9 24.2 %all_to_all.22 = f32[32,8,640]{2,1,0:T(8,128)S(1)} all-to-all(f32[32,8,640]{2,1,0:T(8,128)} %bitcast.10), channel_id=1, replica_groups=mesh['row'=8,'col'=4] {'row','col'}, dimensions={0} | all-to-all | bytes 1310720 | tf_op jit(solution)/shard_map/all_to_all | solution.py:377
  27.1 0.0 copy-done
  27.1 0.0 copy-done.1
  27.1 0.0 copy-done.2
  27.1 0.0 copy-done.3
  27.1 0.0 copy-done.4
  27.1 3.4 %circulant.1 = f32[256,512]{1,0:T(8,128)S(1)} custom-call(f32[256,640]{1,0:T(8,128)S(1)} %bitcast.8, f32[256,256]{1,0:T(8,128)S(1)} %copy-done, f32[256,256]{1,0:T(8,128)S(1)} %copy-done.1, f32[256,256]{1,0:T(8,128)S(1)} %copy-done.2, f32[256,256]{1,0:T(8,128)S(1)} %copy-done.3, f32[2,128,128]{2,1,0:T(8,128)S(1)} %copy-done.4), custom_call_target="tpu_custom_call" | custom-call | tf_op jit(solution)/shard_map/circulant/pallas_call | solution.py:170
  30.5 18.5 %all_to_all.23 = f32[32,8,512]{2,1,0:T(8,128)S(1)} all-to-all(f32[32,8,512]{2,1,0:T(8,128)S(1)} %bitcast.9), channel_id=1, replica_groups=mesh['row'=8,'col'=4] {'row','col'}, dimensions={0} | all-to-all | bytes 1048576 | tf_op jit(solution)/shard_map/all_to_all | solution.py:381
  49.0 0.6 convolution_multiply_fusion
  49.7 2.6 %collective-permute-start = (f32[264,128]{1,0:T(8,128)S(1)}, f32[264,128]{1,0:T(8,128)S(1)}, u32[]{:S(2)}, u32[]{:S(2)}) collective-permute-start(f32[264,128]{1,0:T(8,128)S(1)} %pad_maximum_fusion.packed_ref.leaf_ref), channel_id=1, source_target_pairs={{0,1},{1,0},{2,3},{3,2},{4,5},{5,4},{6,7},{7,6},{8,9},{9,8},{10,11... | collective-permute-start | bytes 405512 | tf_op jit(solution)/shard_map/ppermute | solution.py:17
  52.3 0.8 %collective-permute-start.1 = (f32[264,128]{1,0:T(8,128)S(1)}, f32[264,128]{1,0:T(8,128)S(1)}, u32[]{:S(2)}, u32[]{:S(2)}) collective-permute-start(f32[264,128]{1,0:T(8,128)S(1)} %pad_maximum_fusion.packed_ref.leaf_ref), channel_id=1, source_target_pairs={{0,2},{1,3},{2,0},{3,1},{4,6},{5,7},{6,4},{7,5},{8,10},{9,11},{10,... | collective-permute-start | bytes 405512 | tf_op jit(solution)/shard_map/ppermute | solution.py:17
  53.1 1.6 %collective-permute-start.2 = (f32[264,128]{1,0:T(8,128)S(1)}, f32[264,128]{1,0:T(8,128)S(1)}, u32[]{:S(2)}, u32[]{:S(2)}) collective-permute-start(f32[264,128]{1,0:T(8,128)S(1)} %pad_maximum_fusion.packed_ref.leaf_ref), channel_id=1, source_target_pairs={{0,3},{1,2},{2,1},{3,0},{4,7},{5,6},{6,5},{7,4},{8,11},{9,10},{10,... | collective-permute-start | bytes 405512 | tf_op jit(solution)/shard_map/ppermute | solution.py:17
  54.7 9.4 %leaf.1 = (f32[512,256]{1,0:T(8,128)}, f32[256,256]{1,0:T(8,128)S(1)}) custom-call(f32[256,512]{1,0:T(8,128)S(1)} %bitcast.7, f32[264,128]{1,0:T(8,128)S(1)} %pad_maximum_fusion.packed_ref.leaf_ref), custom_call_target="tpu_custom_call" | custom-call | tf_op jit(solution)/shard_map/leaf/pallas_call | solution.py:351
  64.1 0.0 collective-permute-done.near_ref
  64.1 0.6 collective-permute-done.1.far_ref
  64.7 0.0 collective-permute-done.2.last_ref
  64.7 10.2 %group.1 = (f32[256,256]{1,0:T(8,128)}, f32[128,256]{1,0:T(8,128)}, f32[64,256]{1,0:T(8,128)}) custom-call(s32[1]{0:T(128)} %bitcast.4.place_ref, f32[264,128]{1,0:T(8,128)S(1)} %pad_maximum_fusion.packed_ref.leaf_ref, f32[264,128]{1,0:T(8,128)S(1)} %collective-permute-done.near_ref, f32[264,128]{1,0:T(8,128)S(1)} %collective-permute-done.1.far_ref, ...), custom_call_target="tpu_custom_call" | custom-call | tf_op jit(solution)/shard_map/group/pallas_call | solution.py:363
  (3 shorter events, 0.1 us)
Async XLA Ops:
  2.8 24.3 %copy-start = (f32[256,256]{1,0:T(8,128)S(1)}, f32[256,256]{1,0:T(8,128)}, u32[]{:S(2)}) copy-start(f32[256,256]{1,0:T(8,128)} %constant.18.clone.first_ref) | copy-start | bytes 786436
  2.8 24.3 %copy-start.1 = (f32[256,256]{1,0:T(8,128)S(1)}, f32[256,256]{1,0:T(8,128)}, u32[]{:S(2)}) copy-start(f32[256,256]{1,0:T(8,128)} %constant.19.clone.first_t_ref) | copy-start | bytes 786436
  2.9 24.3 %copy-start.2 = (f32[256,256]{1,0:T(8,128)S(1)}, f32[256,256]{1,0:T(8,128)}, u32[]{:S(2)}) copy-start(f32[256,256]{1,0:T(8,128)} %constant.20.clone.second_ref) | copy-start | bytes 786436
  2.9 24.3 %copy-start.3 = (f32[256,256]{1,0:T(8,128)S(1)}, f32[256,256]{1,0:T(8,128)}, u32[]{:S(2)}) copy-start(f32[256,256]{1,0:T(8,128)} %constant.21.clone.second_t_ref) | copy-start | bytes 786436
  2.9 24.3 %copy-start.4 = (f32[2,128,128]{2,1,0:T(8,128)S(1)}, f32[2,128,128]{2,1,0:T(8,128)}, u32[]{:S(2)}) copy-start(f32[2,128,128]{2,1,0:T(8,128)} %constant.22.clone.turn_ref) | copy-start | bytes 393220
  49.7 14.4 %collective-permute-start = (f32[264,128]{1,0:T(8,128)S(1)}, f32[264,128]{1,0:T(8,128)S(1)}, u32[]{:S(2)}, u32[]{:S(2)}) collective-permute-start(f32[264,128]{1,0:T(8,128)S(1)} %pad_maximum_fusion.packed_ref.leaf_ref), channel_id=1, source_target_pairs={{0,1},{1,0},{2,3},{3,2},{4,5},{5,4},{6,7},{7,6},{8,9},{9,8},{10,11... | collective-permute-start | bytes 405512 | tf_op jit(solution)/shard_map/ppermute | solution.py:17
  52.3 12.4 %collective-permute-start.1 = (f32[264,128]{1,0:T(8,128)S(1)}, f32[264,128]{1,0:T(8,128)S(1)}, u32[]{:S(2)}, u32[]{:S(2)}) collective-permute-start(f32[264,128]{1,0:T(8,128)S(1)} %pad_maximum_fusion.packed_ref.leaf_ref), channel_id=1, source_target_pairs={{0,2},{1,3},{2,0},{3,1},{4,6},{5,7},{6,4},{7,5},{8,10},{9,11},{10,... | collective-permute-start | bytes 405512 | tf_op jit(solution)/shard_map/ppermute | solution.py:17
  53.1 11.6 %collective-permute-start.2 = (f32[264,128]{1,0:T(8,128)S(1)}, f32[264,128]{1,0:T(8,128)S(1)}, u32[]{:S(2)}, u32[]{:S(2)}) collective-permute-start(f32[264,128]{1,0:T(8,128)S(1)} %pad_maximum_fusion.packed_ref.leaf_ref), channel_id=1, source_target_pairs={{0,3},{1,2},{2,1},{3,0},{4,7},{5,6},{6,5},{7,4},{8,11},{9,10},{10,... | collective-permute-start | bytes 405512 | tf_op jit(solution)/shard_map/ppermute | solution.py:17

commit v6 on v5

--- a/solution.py
+++ b/solution.py
@@ -195,65 +195,83 @@
     return high, middle, rest - middle
 
 
-def eliminate(tile_ref, done_ref, problems, width, block):
+def eliminate(tile_ref, done_ref, problems, width):
     tiles = width // LANES
-    thin = iota((problems, LANES), 1)
-
-    def across(value, lane):
-        return jnp.broadcast_to(value[:, lane : lane + 1], (problems, LANES))
+    block = 8
+    shape = (block, LANES)
+    sub = iota(shape, 0)
+    lane = iota(shape, 1)
+
+    def row_of(value, i):
+        return jnp.broadcast_to(value[i : i + 1, :], shape)
+
+    def lane_of(value, l):
+        return jnp.broadcast_to(value[:, l : l + 1], shape)
+
+    def turned(value, l):
+        only = jnp.sum(jnp.where(lane == sub + l, value, 0.0), axis=1, keepdims=True)
+        return jnp.broadcast_to(only, shape)
 
     def load(base):
         return [
-            [tile_ref[t, pl.ds(base + i, problems, stride=width), :] for t in range(tiles)]
-            for i in range(block)
+            [
+                tile_ref[t, p * width + base : p * width + base + block, :]
+                for t in range(tiles)
+            ]
+            for p in range(problems)
         ]
 
     panel = load(0)
     for base in range(0, width, block):
         own, offset = divmod(base, LANES)
-        entry = {
-            (i, j): across(panel[i][own], offset + j)
-            for i in range(block)
-            for j in range(i, block)
-        }
+        after = base + block
+        more = after < width
+        column = [[lane_of(x[own], offset + l) for l in range(block)] for x in panel]
+        inside = (lane >= offset) & (lane < offset + block)
+        if more:
+            near, shift = divmod(after, LANES)
+            cross = [[turned(row_of(x[near], i), shift) for i in range(block)] for x in panel]
+            ahead = load(after)
+            for x in ahead:
+                x[own] = jnp.where(inside, 0.0, x[own])
         for j in range(block):
-            scale = lax.rsqrt(entry[j, j])
-            factor = {i: entry[j, i] * scale for i in range(j + 1, block)}
-            hot = thin == offset + j
-            panel[j][own] = jnp.where(hot, 1.0, panel[j][own])
-            panel[j] = [x * scale for x in panel[j]]
-            for i in range(j + 1, block):
-                for l in range(i, block):
-                    entry[i, l] = entry[i, l] - factor[i] * factor[l]
-                panel[i][own] = jnp.where(hot, 0.0, panel[i][own])
-                panel[i] = [x - factor[i] * y for x, y in zip(panel[i], panel[j])]
+            hot = (lane == offset + j) & (sub >= j)
+            unit = jnp.where(sub == j, 1.0, 0.0)
+            for p in range(problems):
+                x, c = panel[p], column[p]
+                scale = lax.rsqrt(row_of(c[j], j))
+                factor = c[j] * scale
+                each = {l: row_of(factor, l) for l in range(j + 1, block)}
+                for l in range(j + 1, block):
+                    c[l] = c[l] - factor * each[l]
+                lower = jnp.where(sub > j, factor, 0.0)
+                x[own] = jnp.where(hot, unit, x[own])
+                pivot = [row_of(y, j) * scale for y in x]
+                panel[p] = [
+                    jnp.where(sub == j, v, y - lower * v) for v, y in zip(pivot, x)
+                ]
+                if more:
+                    weight = cross[p][j] * scale
+                    for i in range(j + 1, block):
+                        cross[p][i] = cross[p][i] - each[i] * weight
+                    pivot[own] = jnp.where(inside & (lane > offset + j), 0.0, pivot[own])
+                    ahead[p] = [y - weight * v for v, y in zip(pivot, ahead[p])]
+        for p in range(problems):
             for t in range(tiles):
-                done_ref[t, pl.ds(base + j, problems, stride=width), :] = panel[j][t]
-        after = base + block
-        if after == width:
+                done_ref[t, p * width + base : p * width + after, :] = panel[p][t]
+        if not more:
             break
-        inside = (thin >= offset) & (thin < offset + block)
-        clean = [list(rows) for rows in panel]
-        for j in range(block):
-            clean[j][own] = jnp.where(inside & (thin > offset + j), 0.0, panel[j][own])
-        ahead = load(after)
-        for i in range(block):
-            ahead[i][own] = jnp.where(inside, 0.0, ahead[i][own])
-            for j in range(block):
-                weight = across(panel[j][after // LANES], after % LANES + i)
-                ahead[i] = [x - weight * y for x, y in zip(ahead[i], clean[j])]
-        panel = ahead
+        done, panel = panel, ahead
         past = after + block
         if past == width:
             continue
         first = past // LANES
-        lane = iota((block, LANES), 1) - offset
-        inverse = (lane < 0) | (lane >= block) | (lane <= iota((block, LANES), 0))
+        inverse = ~inside | (lane - offset <= sub)
         below = iota((width - past, LANES), 1) - offset
         below = (below >= 0) & (below < block)
         for p in range(problems):
             start = p * width
-            rows = [parts(done_ref[t, start + base : start + after, :]) for t in range(tiles)]
+            rows = [parts(x) for x in done[p]]
             left = jnp.concatenate(
                 [
                     jnp.concatenate([rows[t][q] for q in (0, 0, 1, 1, 0, 2)], 0)
@@ -285,11 +303,14 @@
     row = iota((LANES, LANES), 0)
     lane = iota((LANES, LANES), 1)
     shared = packed[:LANES, :]
-    tile_ref[0, start : start + LANES, :] = shared
+    other = shared.T
+    tile_ref[0, start : start + LANES, :] = jnp.where(lane >= row, shared, other)
     tile_ref[0, start + LANES : start + width, :] = jnp.zeros((LANES, LANES), jnp.float32)
     tile_ref[1, start : start + LANES, :] = packed[LANES : 2 * LANES, :]
     diagonal = jnp.broadcast_to(packed[2 * LANES : 2 * LANES + 1, :], (LANES, LANES))
-    tile_ref[1, start + LANES : start + width, :] = jnp.where(lane == row, diagonal, shared.T)
+    tile_ref[1, start + LANES : start + width, :] = jnp.where(
+        lane < row, shared, jnp.where(lane == row, diagonal, other)
+    )
 
 
 def factors(done_ref, start, width):
@@ -300,44 +321,53 @@
     return upper, jnp.where(lane <= row, whole, 0.0)
 
 
-def leaf_kernel(sample_ref, packed_ref, basis_ref, upper_ref, tile_ref, done_ref):
+def pair_kernel(
+    sample_ref,
+    leaf_ref,
+    near_ref,
+    basis_ref,
+    transfer_ref,
+    upper_ref,
+    pair_ref,
+    tile_ref,
+    done_ref,
+):
     width = sample_ref.shape[0]
-    unpack(packed_ref[...], tile_ref, 0, width)
-    eliminate(tile_ref, done_ref, 1, width, 8)
-    upper, inverse = factors(done_ref, 0, width)
-    upper_ref[...] = upper
-    basis_ref[...] = times_transpose(sample_ref[...].T, inverse)
+    leaf = leaf_ref[...]
+    pair = leaf + near_ref[...]
+    pair_ref[...] = pair
+    unpack(leaf, tile_ref, 0, width)
+    unpack(pair, tile_ref, width, width)
+    eliminate(tile_ref, done_ref, 2, width)
+    leaf_upper, leaf_inverse = factors(done_ref, 0, width)
+    upper_ref[...], pair_inverse = factors(done_ref, width, width)
+    basis_ref[...] = times_transpose(sample_ref[...].T, leaf_inverse)
+    transfer_ref[...] = times_transpose(leaf_upper, pair_inverse)
 
 
 def group_kernel(
     place_ref,
-    leaf_ref,
-    near_ref,
+    pair_ref,
     far_ref,
     last_ref,
-    leaf_upper_ref,
-    leaf_transfer_ref,
-    pair_transfer_ref,
-    group_factor_ref,
+    pair_upper_ref,
+    transfer_ref,
+    factor_ref,
     tile_ref,
     done_ref,
     upper_ref,
 ):
-    width = leaf_upper_ref.shape[0]
-    pair = leaf_ref[...] + near_ref[...]
-    unpack(pair, tile_ref, 0, width)
-    unpack(pair + (far_ref[...] + last_ref[...]), tile_ref, width, width)
-    eliminate(tile_ref, done_ref, 2, width, 8)
-    upper_ref[0], pair_inverse = factors(done_ref, 0, width)
-    upper_ref[1], group_inverse = factors(done_ref, width, width)
-    leaf_transfer_ref[...] = times_transpose(leaf_upper_ref[...], pair_inverse)
+    width = pair_upper_ref.shape[0]
+    unpack(pair_ref[...] + (far_ref[...] + last_ref[...]), tile_ref, 0, width)
+    eliminate(tile_ref, done_ref, 1, width)
+    upper_ref[...], inverse = factors(done_ref, 0, width)
     half = width // 2
     quarter = width // 4
     place = place_ref[0]
-    pair_upper = upper_ref[0, pl.ds(pl.multiple_of(place % 2 * half, half), half), :]
-    pair_transfer_ref[...] = times_transpose(pair_upper, group_inverse)
-    group_factor_ref[...] = upper_ref[
-        1, pl.ds(pl.multiple_of(place % 4 * quarter, quarter), quarter), :
+    pair_upper = pair_upper_ref[pl.ds(pl.multiple_of(place % 2 * half, half), half), :]
+    transfer_ref[...] = times_transpose(pair_upper, inverse)
+    factor_ref[...] = upper_ref[
+        pl.ds(pl.multiple_of(place % 4 * quarter, quarter), quarter), :
     ]
 
 
@@ -346,29 +376,30 @@
     return [pltpu.VMEM((tiles, problems * width, LANES), jnp.float32)] * 2
 
 
-def leaf_factor(sample_t, leaf):
+def pair_factors(sample_t, leaf, near):
     width, rows = sample_t.shape
+    shapes = [(rows, width), (width, width), (width, width), leaf.shape]
     return pl.pallas_call(
-        leaf_kernel,
-        out_shape=[jax.ShapeDtypeStruct(shape, jnp.float32) for shape in ((rows, width), (width, width))],
-        scratch_shapes=scratch(1, width),
+        pair_kernel,
+        out_shape=[jax.ShapeDtypeStruct(shape, jnp.float32) for shape in shapes],
+        scratch_shapes=scratch(2, width),
         compiler_params=pltpu.CompilerParams(vmem_limit_bytes=24 << 20),
-        name="leaf",
-    )(sample_t, leaf)
-
-
-def group_factors(place, leaf, near, far, last, leaf_upper):
-    width = leaf_upper.shape[0]
-    shapes = [(width, width), (width // 2, width), (width // 4, width)]
+        name="pair",
+    )(sample_t, leaf, near)
+
+
+def group_factors(place, pair, far, last, pair_upper):
+    width = pair_upper.shape[0]
+    shapes = [(width // 2, width), (width // 4, width)]
     return pl.pallas_call(
         group_kernel,
         out_shape=[jax.ShapeDtypeStruct(shape, jnp.float32) for shape in shapes],
         in_specs=[pl.BlockSpec(memory_space=pltpu.SMEM)]
-        + [pl.BlockSpec(memory_space=pltpu.VMEM)] * 5,
-        scratch_shapes=scratch(2, width) + [pltpu.VMEM((2, width, width), jnp.float32)],
+        + [pl.BlockSpec(memory_space=pltpu.VMEM)] * 4,
+        scratch_shapes=scratch(1, width) + [pltpu.VMEM((width, width), jnp.float32)],
         compiler_params=pltpu.CompilerParams(vmem_limit_bytes=24 << 20),
         name="group",
-    )(place, leaf, near, far, last, leaf_upper)
+    )(place, pair, far, last, pair_upper)
 
 
 def local(probes, spectrum):
@@ -381,9 +412,10 @@
     sample_t = lax.all_to_all(moved, axes, split_axis=0, concat_axis=0, tiled=True)
     leaf = packed_gram(sample_t)
     near, far, last = (partner(leaf, "col", mask) for mask in (1, 2, 3))
-    leaf_basis, leaf_upper = leaf_factor(sample_t, leaf)
+    leaf_basis, leaf_transfer, pair_upper, pair = pair_factors(sample_t, leaf, near)
     place = lax.axis_index("col").reshape(1).astype(jnp.int32)
-    return (leaf_basis, *group_factors(place, leaf, near, far, last, leaf_upper))
+    pair_transfer, group_factor = group_factors(place, pair, far, last, pair_upper)
+    return leaf_basis, leaf_transfer, pair_transfer, group_factor
 
 
 def solution(mesh):

time: 75.1 us -> 76.6 us (1.020)
  waiting for transfers between devices: 0.56 us -> 3.3 us
  Pallas kernels: 25.2 us -> 24 us
    ppermute x3, waiting for transfers between devices: 0.56 us -> 3.3 us  [partner(): return lax.ppermute(value, axis, pairs)]
    pallas_call x1, Pallas kernels: 10.2 us -> 7.89 us  [group_factors(): pl.pallas_call(group_kernel, out_shape=[jax.ShapeDtypeStruct(shape, jnp.f...]
    pallas_call x1, Pallas kernels: 9.38 us -> 10.5 us  [pair_factors(): pl.pallas_call(pair_kernel, out_shape=[jax.ShapeDtypeStruct(shape, jnp.fl...]
  transfers between devices with their start and end apart: 3 -> 3, of which waited for: 1 -> 1; matrix products, arithmetic and copies ran while one was open for 0% -> 0% of each run, Pallas kernels for 13% -> 14%
where the time goes in v6:
time: 76.6 us; the launch traced here: 76.4 us
  blocking collectives  42.7 us (56%)
  Pallas kernels  24 us (31%)
  starting transfers between devices  5.05 us (7%)
  waiting for transfers between devices  3.3 us (4%)
    all_to_all x1, blocking collectives, local(): lax.all_to_all(spread(probes, spectrum, devices), axes, split_axis=0, con...  24.2 us
    all_to_all x1, blocking collectives, local(): lax.all_to_all(moved, axes, split_axis=0, concat_axis=0, tiled=True)  18.5 us
    pallas_call x1, Pallas kernels, pair_factors(): pl.pallas_call(pair_kernel, out_shape=[jax.ShapeDtypeStruct(shape, jnp.fl...  10.5 us
    pallas_call x1, Pallas kernels, group_factors(): pl.pallas_call(group_kernel, out_shape=[jax.ShapeDtypeStruct(shape, jnp.f...  7.89 us
    ppermute x3, starting transfers between devices, partner(): return lax.ppermute(value, axis, pairs)  5.05 us
    pallas_call x1, Pallas kernels, circulant(): pl.pallas_call(circulant_kernel(devices, split, width // devices, tiles -...  3.38 us
    ppermute x3, waiting for transfers between devices, partner(): return lax.ppermute(value, axis, pairs)  3.3 us
    pallas_call x1, Pallas kernels, spread(): pl.pallas_call(spread_kernel(per_dev, extra), out_shape=jax.ShapeDtypeStr...  2.22 us
  transfers between devices with their start and end apart: 3, of which 1 were waited for; matrix products, arithmetic and copies ran while one was open for 0% of the time, Pallas kernels for 14%

profile of v6, /device:TPU:0, one launch (start us, length us, event | category | flops | bytes accessed | tf_op | source)
XLA Modules:
  0.0 76.4 jit_solution(5335677441271438526)
XLA Ops:
  0.6 2.2 %spread.1 = f32[256,640]{1,0:T(8,128)} custom-call(f32[512,256]{1,0:T(8,128)} %probes_ref.1, f32[1,512]{1,0:T(1,128)} %spectrum_ref.1), custom_call_target="tpu_custom_call" | custom-call | tf_op jit(solution)/shard_map/spread/pallas_call | solution.py:81
  2.8 0.0 copy-start
  2.8 0.0 copy-start.1
  2.9 0.0 copy-start.2
  2.9 0.0 copy-start.3
  2.9 0.0 copy-start.4
  2.9 24.2 %all_to_all.22 = f32[32,8,640]{2,1,0:T(8,128)S(1)} all-to-all(f32[32,8,640]{2,1,0:T(8,128)} %bitcast.10), channel_id=1, replica_groups=mesh['row'=8,'col'=4] {'row','col'}, dimensions={0} | all-to-all | bytes 1310720 | tf_op jit(solution)/shard_map/all_to_all | solution.py:408
  27.1 0.0 copy-done
  27.1 0.0 copy-done.1
  27.1 0.0 copy-done.2
  27.1 0.0 copy-done.3
  27.1 0.0 copy-done.4
  27.1 3.4 %circulant.1 = f32[256,512]{1,0:T(8,128)S(1)} custom-call(f32[256,640]{1,0:T(8,128)S(1)} %bitcast.8, f32[256,256]{1,0:T(8,128)S(1)} %copy-done, f32[256,256]{1,0:T(8,128)S(1)} %copy-done.1, f32[256,256]{1,0:T(8,128)S(1)} %copy-done.2, f32[256,256]{1,0:T(8,128)S(1)} %copy-done.3, f32[2,128,128]{2,1,0:T(8,128)S(1)} %copy-done.4), custom_call_target="tpu_custom_call" | custom-call | tf_op jit(solution)/shard_map/circulant/pallas_call | solution.py:170
  30.5 18.5 %all_to_all.23 = f32[32,8,512]{2,1,0:T(8,128)S(1)} all-to-all(f32[32,8,512]{2,1,0:T(8,128)S(1)} %bitcast.9), channel_id=1, replica_groups=mesh['row'=8,'col'=4] {'row','col'}, dimensions={0} | all-to-all | bytes 1048576 | tf_op jit(solution)/shard_map/all_to_all | solution.py:412
  49.0 0.6 convolution_multiply_fusion
  49.7 2.6 %collective-permute-start = (f32[264,128]{1,0:T(8,128)S(1)}, f32[264,128]{1,0:T(8,128)S(1)}, u32[]{:S(2)}, u32[]{:S(2)}) collective-permute-start(f32[264,128]{1,0:T(8,128)S(1)} %pad_maximum_fusion.leaf_ref), channel_id=1, source_target_pairs={{0,1},{1,0},{2,3},{3,2},{4,5},{5,4},{6,7},{7,6},{8,9},{9,8},{10,11... | collective-permute-start | bytes 405512 | tf_op jit(solution)/shard_map/ppermute | solution.py:17
  52.3 0.8 %collective-permute-start.1 = (f32[264,128]{1,0:T(8,128)S(1)}, f32[264,128]{1,0:T(8,128)S(1)}, u32[]{:S(2)}, u32[]{:S(2)}) collective-permute-start(f32[264,128]{1,0:T(8,128)S(1)} %pad_maximum_fusion.leaf_ref), channel_id=1, source_target_pairs={{0,2},{1,3},{2,0},{3,1},{4,6},{5,7},{6,4},{7,5},{8,10},{9,11},{10,... | collective-permute-start | bytes 405512 | tf_op jit(solution)/shard_map/ppermute | solution.py:17
  53.1 1.6 %collective-permute-start.2 = (f32[264,128]{1,0:T(8,128)S(1)}, f32[264,128]{1,0:T(8,128)S(1)}, u32[]{:S(2)}, u32[]{:S(2)}) collective-permute-start(f32[264,128]{1,0:T(8,128)S(1)} %pad_maximum_fusion.leaf_ref), channel_id=1, source_target_pairs={{0,3},{1,2},{2,1},{3,0},{4,7},{5,6},{6,5},{7,4},{8,11},{9,10},{10,... | collective-permute-start | bytes 405512 | tf_op jit(solution)/shard_map/ppermute | solution.py:17
  54.7 3.3 %collective-permute-done.near_ref = f32[264,128]{1,0:T(8,128)S(1)} collective-permute-done((f32[264,128]{1,0:T(8,128)S(1)}, f32[264,128]{1,0:T(8,128)S(1)}, u32[]{:S(2)}, u32[]{:S(2)}) %collective-permute-start) | collective-permute-done | bytes 135200 | tf_op jit(solution)/shard_map/ppermute | solution.py:17
  58.0 10.5 %pair.1 = (f32[512,256]{1,0:T(8,128)}, f32[256,256]{1,0:T(8,128)}, f32[256,256]{1,0:T(8,128)S(1)}, f32[264,128]{1,0:T(8,128)S(1)}) custom-call(f32[256,512]{1,0:T(8,128)S(1)} %bitcast.7, f32[264,128]{1,0:T(8,128)S(1)} %pad_maximum_fusion.leaf_ref, f32[264,128]{1,0:T(8,128)S(1)} %collective-permute-done.near_ref), custom_call_target="tpu_custom_call" | custom-call | tf_op jit(solution)/shard_map/pair/pallas_call | solution.py:382
  68.5 0.0 collective-permute-done.1.far_ref
  68.5 0.0 collective-permute-done.2.last_ref
  68.5 7.9 %group.1 = (f32[128,256]{1,0:T(8,128)}, f32[64,256]{1,0:T(8,128)}) custom-call(s32[1]{0:T(128)} %bitcast.4.place_ref, f32[264,128]{1,0:T(8,128)S(1)} %get-tuple-element.12.pair_ref, f32[264,128]{1,0:T(8,128)S(1)} %collective-permute-done.1.far_ref, f32[264,128]{1,0:T(8,128)S(1)} %collective-permute-done.2.last_ref, ...), custom_call_target="tpu_custom_call" | custom-call | tf_op jit(solution)/shard_map/group/pallas_call | solution.py:394
  (3 shorter events, 0.1 us)
Async XLA Ops:
  2.8 24.3 %copy-start = (f32[256,256]{1,0:T(8,128)S(1)}, f32[256,256]{1,0:T(8,128)}, u32[]{:S(2)}) copy-start(f32[256,256]{1,0:T(8,128)} %constant.18.clone.first_ref) | copy-start | bytes 786436
  2.8 24.3 %copy-start.1 = (f32[256,256]{1,0:T(8,128)S(1)}, f32[256,256]{1,0:T(8,128)}, u32[]{:S(2)}) copy-start(f32[256,256]{1,0:T(8,128)} %constant.19.clone.first_t_ref) | copy-start | bytes 786436
  2.9 24.3 %copy-start.2 = (f32[256,256]{1,0:T(8,128)S(1)}, f32[256,256]{1,0:T(8,128)}, u32[]{:S(2)}) copy-start(f32[256,256]{1,0:T(8,128)} %constant.20.clone.second_ref) | copy-start | bytes 786436
  2.9 24.3 %copy-start.3 = (f32[256,256]{1,0:T(8,128)S(1)}, f32[256,256]{1,0:T(8,128)}, u32[]{:S(2)}) copy-start(f32[256,256]{1,0:T(8,128)} %constant.21.clone.second_t_ref) | copy-start | bytes 786436
  2.9 24.3 %copy-start.4 = (f32[2,128,128]{2,1,0:T(8,128)S(1)}, f32[2,128,128]{2,1,0:T(8,128)}, u32[]{:S(2)}) copy-start(f32[2,128,128]{2,1,0:T(8,128)} %constant.22.clone.turn_ref) | copy-start | bytes 393220
  49.7 8.3 %collective-permute-start = (f32[264,128]{1,0:T(8,128)S(1)}, f32[264,128]{1,0:T(8,128)S(1)}, u32[]{:S(2)}, u32[]{:S(2)}) collective-permute-start(f32[264,128]{1,0:T(8,128)S(1)} %pad_maximum_fusion.leaf_ref), channel_id=1, source_target_pairs={{0,1},{1,0},{2,3},{3,2},{4,5},{5,4},{6,7},{7,6},{8,9},{9,8},{10,11... | collective-permute-start | bytes 405512 | tf_op jit(solution)/shard_map/ppermute | solution.py:17
  52.3 16.2 %collective-permute-start.1 = (f32[264,128]{1,0:T(8,128)S(1)}, f32[264,128]{1,0:T(8,128)S(1)}, u32[]{:S(2)}, u32[]{:S(2)}) collective-permute-start(f32[264,128]{1,0:T(8,128)S(1)} %pad_maximum_fusion.leaf_ref), channel_id=1, source_target_pairs={{0,2},{1,3},{2,0},{3,1},{4,6},{5,7},{6,4},{7,5},{8,10},{9,11},{10,... | collective-permute-start | bytes 405512 | tf_op jit(solution)/shard_map/ppermute | solution.py:17
  53.1 15.4 %collective-permute-start.2 = (f32[264,128]{1,0:T(8,128)S(1)}, f32[264,128]{1,0:T(8,128)S(1)}, u32[]{:S(2)}, u32[]{:S(2)}) collective-permute-start(f32[264,128]{1,0:T(8,128)S(1)} %pad_maximum_fusion.leaf_ref), channel_id=1, source_target_pairs={{0,3},{1,2},{2,1},{3,0},{4,7},{5,6},{6,5},{7,4},{8,11},{9,10},{10,... | collective-permute-start | bytes 405512 | tf_op jit(solution)/shard_map/ppermute | solution.py:17

commit v7 on v6

--- a/solution.py
+++ b/solution.py
@@ -24,6 +24,23 @@
 def circle(product, length):
     angle = 2.0 * np.pi / length * (product % length)
     return np.cos(angle), np.sin(angle)
+
+
+def halves(table):
+    high = table.astype(jnp.bfloat16)
+    return np.stack([high, (table - high.astype(np.float64)).astype(jnp.bfloat16)])
+
+
+def split2(value):
+    high = value.astype(jnp.bfloat16)
+    return high, (value - high.astype(jnp.float32)).astype(jnp.bfloat16)
+
+
+def product(left, right):
+    def dot(i, j):
+        return jnp.dot(left[i], right[j], preferred_element_type=jnp.float32)
+
+    return dot(0, 0) + (dot(0, 1) + dot(1, 0))
 
 
 def tables(devices, split):
@@ -38,7 +55,7 @@
     second = np.block([[cos, -sin], [sin, cos]])
     cos_turn, sin_turn = circle(freq[:, None] * lane[None, :], total)
     turn = np.stack([cos_turn, sin_turn])
-    return [np.asarray(t, np.float32) for t in (first, first.T, second, second.T, turn)]
+    return [halves(t) for t in (first, first.T, second, second.T)] + [turn.astype(np.float32)]
 
 
 def iota(shape, dim):
@@ -128,7 +145,7 @@
         packed = jnp.concatenate(
             [jnp.concatenate(column(2 * q) + column(2 * q + 1), 0) for q in range(pairs)], 1
         )
-        mixed = matmul(first_ref[...], packed)
+        mixed = product(first_ref, split2(packed))
         turned = []
         for q in range(pairs):
             real = mixed[:major, q * LANES : (q + 1) * LANES]
@@ -136,12 +153,12 @@
             turned.append(
                 jnp.concatenate([real * cos + imag * sin, imag * cos - real * sin], 1)
             )
-        spectra = matmul(jnp.concatenate(turned, 0), second_ref[...])
+        spectra = product(split2(jnp.concatenate(turned, 0)), second_ref)
         lam = jnp.concatenate([lam, lam], 1)
         spectra = jnp.concatenate(
             [spectra[q * major : (q + 1) * major] * lam for q in range(pairs)], 0
         )
-        back = matmul(spectra, second_t_ref[...])
+        back = product(split2(spectra), second_t_ref)
         turned = []
         for q in range(pairs):
             real = back[q * major : (q + 1) * major, :LANES]
@@ -149,7 +166,7 @@
             turned.append(
                 jnp.concatenate([real * cos - imag * sin, imag * cos + real * sin], 0)
             )
-        sample = matmul(first_t_ref[...], jnp.concatenate(turned, 1))
+        sample = product(first_t_ref, split2(jnp.concatenate(turned, 1)))
         for c in range(per_dev):
             for j in range(split):
                 row = (c % 2) * major + j * devices
@@ -321,53 +338,44 @@
     return upper, jnp.where(lane <= row, whole, 0.0)
 
 
-def pair_kernel(
-    sample_ref,
+def leaf_kernel(sample_ref, packed_ref, basis_ref, upper_ref, tile_ref, done_ref):
+    width = sample_ref.shape[0]
+    unpack(packed_ref[...], tile_ref, 0, width)
+    eliminate(tile_ref, done_ref, 1, width)
+    upper, inverse = factors(done_ref, 0, width)
+    upper_ref[...] = upper
+    basis_ref[...] = times_transpose(sample_ref[...].T, inverse)
+
+
+def group_kernel(
+    place_ref,
     leaf_ref,
     near_ref,
-    basis_ref,
-    transfer_ref,
-    upper_ref,
-    pair_ref,
-    tile_ref,
-    done_ref,
-):
-    width = sample_ref.shape[0]
-    leaf = leaf_ref[...]
-    pair = leaf + near_ref[...]
-    pair_ref[...] = pair
-    unpack(leaf, tile_ref, 0, width)
-    unpack(pair, tile_ref, width, width)
-    eliminate(tile_ref, done_ref, 2, width)
-    leaf_upper, leaf_inverse = factors(done_ref, 0, width)
-    upper_ref[...], pair_inverse = factors(done_ref, width, width)
-    basis_ref[...] = times_transpose(sample_ref[...].T, leaf_inverse)
-    transfer_ref[...] = times_transpose(leaf_upper, pair_inverse)
-
-
-def group_kernel(
-    place_ref,
-    pair_ref,
     far_ref,
     last_ref,
-    pair_upper_ref,
-    transfer_ref,
-    factor_ref,
+    leaf_upper_ref,
+    leaf_transfer_ref,
+    pair_transfer_ref,
+    group_factor_ref,
     tile_ref,
     done_ref,
     upper_ref,
 ):
-    width = pair_upper_ref.shape[0]
-    unpack(pair_ref[...] + (far_ref[...] + last_ref[...]), tile_ref, 0, width)
-    eliminate(tile_ref, done_ref, 1, width)
-    upper_ref[...], inverse = factors(done_ref, 0, width)
+    width = leaf_upper_ref.shape[0]
+    pair = leaf_ref[...] + near_ref[...]
+    unpack(pair, tile_ref, 0, width)
+    unpack(pair + (far_ref[...] + last_ref[...]), tile_ref, width, width)
+    eliminate(tile_ref, done_ref, 2, width)
+    upper_ref[0], pair_inverse = factors(done_ref, 0, width)
+    upper_ref[1], group_inverse = factors(done_ref, width, width)
+    leaf_transfer_ref[...] = times_transpose(leaf_upper_ref[...], pair_inverse)
     half = width // 2
     quarter = width // 4
     place = place_ref[0]
-    pair_upper = pair_upper_ref[pl.ds(pl.multiple_of(place % 2 * half, half), half), :]
-    transfer_ref[...] = times_transpose(pair_upper, inverse)
-    factor_ref[...] = upper_ref[
-        pl.ds(pl.multiple_of(place % 4 * quarter, quarter), quarter), :
+    pair_upper = upper_ref[0, pl.ds(pl.multiple_of(place % 2 * half, half), half), :]
+    pair_transfer_ref[...] = times_transpose(pair_upper, group_inverse)
+    group_factor_ref[...] = upper_ref[
+        1, pl.ds(pl.multiple_of(place % 4 * quarter, quarter), quarter), :
     ]
 
 
@@ -376,30 +384,29 @@
     return [pltpu.VMEM((tiles, problems * width, LANES), jnp.float32)] * 2
 
 
-def pair_factors(sample_t, leaf, near):
+def leaf_factor(sample_t, leaf):
     width, rows = sample_t.shape
-    shapes = [(rows, width), (width, width), (width, width), leaf.shape]
     return pl.pallas_call(
-        pair_kernel,
-        out_shape=[jax.ShapeDtypeStruct(shape, jnp.float32) for shape in shapes],
-        scratch_shapes=scratch(2, width),
+        leaf_kernel,
+        out_shape=[jax.ShapeDtypeStruct(shape, jnp.float32) for shape in ((rows, width), (width, width))],
+        scratch_shapes=scratch(1, width),
         compiler_params=pltpu.CompilerParams(vmem_limit_bytes=24 << 20),
-        name="pair",
-    )(sample_t, leaf, near)
-
-
-def group_factors(place, pair, far, last, pair_upper):
-    width = pair_upper.shape[0]
-    shapes = [(width // 2, width), (width // 4, width)]
+        name="leaf",
+    )(sample_t, leaf)
+
+
+def group_factors(place, leaf, near, far, last, leaf_upper):
+    width = leaf_upper.shape[0]
+    shapes = [(width, width), (width // 2, width), (width // 4, width)]
     return pl.pallas_call(
         group_kernel,
         out_shape=[jax.ShapeDtypeStruct(shape, jnp.float32) for shape in shapes],
         in_specs=[pl.BlockSpec(memory_space=pltpu.SMEM)]
-        + [pl.BlockSpec(memory_space=pltpu.VMEM)] * 4,
-        scratch_shapes=scratch(1, width) + [pltpu.VMEM((width, width), jnp.float32)],
+        + [pl.BlockSpec(memory_space=pltpu.VMEM)] * 5,
+        scratch_shapes=scratch(2, width) + [pltpu.VMEM((2, width, width), jnp.float32)],
         compiler_params=pltpu.CompilerParams(vmem_limit_bytes=24 << 20),
         name="group",
-    )(place, pair, far, last, pair_upper)
+    )(place, leaf, near, far, last, leaf_upper)
 
 
 def local(probes, spectrum):
@@ -411,11 +418,10 @@
     moved = circulant(columns, probes.shape[0], devices)
     sample_t = lax.all_to_all(moved, axes, split_axis=0, concat_axis=0, tiled=True)
     leaf = packed_gram(sample_t)
-    near, far, last = (partner(leaf, "col", mask) for mask in (1, 2, 3))
-    leaf_basis, leaf_transfer, pair_upper, pair = pair_factors(sample_t, leaf, near)
+    far, last, near = (partner(leaf, "col", mask) for mask in (2, 3, 1))
+    leaf_basis, leaf_upper = leaf_factor(sample_t, leaf)
     place = lax.axis_index("col").reshape(1).astype(jnp.int32)
-    pair_transfer, group_factor = group_factors(place, pair, far, last, pair_upper)
-    return leaf_basis, leaf_transfer, pair_transfer, group_factor
+    return (leaf_basis, *group_factors(place, leaf, near, far, last, leaf_upper))
 
 
 def solution(mesh):

time: 76.6 us -> 73.7 us (0.962)
  Pallas kernels: 24 us -> 22.4 us
  waiting for transfers between devices: 3.3 us -> 1.91 us
    pallas_call x1, Pallas kernels: 10.5 us -> 8.04 us  [leaf_factor(): pl.pallas_call(leaf_kernel, out_shape=[jax.ShapeDtypeStruct(shape, jnp.fl...]
    pallas_call x1, Pallas kernels: 7.89 us -> 9.83 us  [group_factors(): pl.pallas_call(group_kernel, out_shape=[jax.ShapeDtypeStruct(shape, jnp.f...]
    ppermute x3, waiting for transfers between devices: 3.3 us -> 1.91 us  [partner(): return lax.ppermute(value, axis, pairs)]
    pallas_call x1, Pallas kernels: 3.38 us -> 2.32 us  [circulant(): pl.pallas_call(circulant_kernel(devices, split, width // devices, tiles -...]
  transfers between devices with their start and end apart: 3 -> 3, of which waited for: 1 -> 1; matrix products, arithmetic and copies ran while one was open for 0% -> 0% of each run, Pallas kernels for 14% -> 11%
where the time goes in v7:
time: 73.7 us; the launch traced here: 73.4 us
  blocking collectives  42.7 us (58%)
  Pallas kernels  22.4 us (30%)
  starting transfers between devices  5.05 us (7%)
  waiting for transfers between devices  1.91 us (3%)
    all_to_all x1, blocking collectives, local(): lax.all_to_all(spread(probes, spectrum, devices), axes, split_axis=0, con...  24.2 us
    all_to_all x1, blocking collectives, local(): lax.all_to_all(moved, axes, split_axis=0, concat_axis=0, tiled=True)  18.5 us
    pallas_call x1, Pallas kernels, group_factors(): pl.pallas_call(group_kernel, out_shape=[jax.ShapeDtypeStruct(shape, jnp.f...  9.83 us
    pallas_call x1, Pallas kernels, leaf_factor(): pl.pallas_call(leaf_kernel, out_shape=[jax.ShapeDtypeStruct(shape, jnp.fl...  8.04 us
    ppermute x3, starting transfers between devices, partner(): return lax.ppermute(value, axis, pairs)  5.05 us
    pallas_call x1, Pallas kernels, circulant(): pl.pallas_call(circulant_kernel(devices, split, width // devices, tiles -...  2.32 us
    pallas_call x1, Pallas kernels, spread(): pl.pallas_call(spread_kernel(per_dev, extra), out_shape=jax.ShapeDtypeStr...  2.22 us
    ppermute x3, waiting for transfers between devices, partner(): return lax.ppermute(value, axis, pairs)  1.91 us
  transfers between devices with their start and end apart: 3, of which 1 were waited for; matrix products, arithmetic and copies ran while one was open for 0% of the time, Pallas kernels for 11%

profile of v7, /device:TPU:0, one launch (start us, length us, event | category | flops | bytes accessed | tf_op | source)
XLA Modules:
  0.0 73.4 jit_solution(13994206826841200728)
XLA Ops:
  0.6 2.2 %spread.1 = f32[256,640]{1,0:T(8,128)} custom-call(f32[512,256]{1,0:T(8,128)} %probes_ref.1, f32[1,512]{1,0:T(1,128)} %spectrum_ref.1), custom_call_target="tpu_custom_call" | custom-call | tf_op jit(solution)/shard_map/spread/pallas_call | solution.py:98
  2.8 0.0 copy-start
  2.8 0.0 copy-start.1
  2.9 0.0 copy-start.2
  2.9 0.0 copy-start.3
  2.9 0.0 copy-start.4
  2.9 24.2 %all_to_all.22 = f32[32,8,640]{2,1,0:T(8,128)S(1)} all-to-all(f32[32,8,640]{2,1,0:T(8,128)} %bitcast.10), channel_id=1, replica_groups=mesh['row'=8,'col'=4] {'row','col'}, dimensions={0} | all-to-all | bytes 1310720 | tf_op jit(solution)/shard_map/all_to_all | solution.py:415
  27.1 0.0 copy-done
  27.1 0.0 copy-done.1
  27.1 0.0 copy-done.2
  27.1 0.0 copy-done.3
  27.1 0.0 copy-done.4
  27.1 2.3 %circulant.1 = f32[256,512]{1,0:T(8,128)S(1)} custom-call(f32[256,640]{1,0:T(8,128)S(1)} %bitcast.8, bf16[2,256,256]{2,1,0:T(8,128)(2,1)S(1)} %copy-done, bf16[2,256,256]{2,1,0:T(8,128)(2,1)S(1)} %copy-done.1, bf16[2,256,256]{2,1,0:T(8,128)(2,1)S(1)} %copy-done.2, bf16[2,256,256]{2,1,0:T(8,128)(2,1)S(1)} %copy-done.3, f32[2,128,128]{2,1,0:T(8,128)S(1)} %copy-done.4), custom_call_target="tpu_custom_call" | custom-call | tf_op jit(solution)/shard_map/circulant/pallas_call | solution.py:187
  29.5 18.5 %all_to_all.23 = f32[32,8,512]{2,1,0:T(8,128)S(1)} all-to-all(f32[32,8,512]{2,1,0:T(8,128)S(1)} %bitcast.9), channel_id=1, replica_groups=mesh['row'=8,'col'=4] {'row','col'}, dimensions={0} | all-to-all | bytes 1048576 | tf_op jit(solution)/shard_map/all_to_all | solution.py:419
  47.9 0.6 convolution_multiply_fusion
  48.6 2.6 %collective-permute-start = (f32[264,128]{1,0:T(8,128)S(1)}, f32[264,128]{1,0:T(8,128)S(1)}, u32[]{:S(2)}, u32[]{:S(2)}) collective-permute-start(f32[264,128]{1,0:T(8,128)S(1)} %pad_maximum_fusion.packed_ref.leaf_ref), channel_id=1, source_target_pairs={{0,1},{1,0},{2,3},{3,2},{4,5},{5,4},{6,7},{7,6},{8,9},{9,8},{10,11... | collective-permute-start | bytes 405512 | tf_op jit(solution)/shard_map/ppermute | solution.py:17
  51.2 0.8 %collective-permute-start.1 = (f32[264,128]{1,0:T(8,128)S(1)}, f32[264,128]{1,0:T(8,128)S(1)}, u32[]{:S(2)}, u32[]{:S(2)}) collective-permute-start(f32[264,128]{1,0:T(8,128)S(1)} %pad_maximum_fusion.packed_ref.leaf_ref), channel_id=1, source_target_pairs={{0,2},{1,3},{2,0},{3,1},{4,6},{5,7},{6,4},{7,5},{8,10},{9,11},{10,... | collective-permute-start | bytes 405512 | tf_op jit(solution)/shard_map/ppermute | solution.py:17
  52.1 1.6 %collective-permute-start.2 = (f32[264,128]{1,0:T(8,128)S(1)}, f32[264,128]{1,0:T(8,128)S(1)}, u32[]{:S(2)}, u32[]{:S(2)}) collective-permute-start(f32[264,128]{1,0:T(8,128)S(1)} %pad_maximum_fusion.packed_ref.leaf_ref), channel_id=1, source_target_pairs={{0,3},{1,2},{2,1},{3,0},{4,7},{5,6},{6,5},{7,4},{8,11},{9,10},{10,... | collective-permute-start | bytes 405512 | tf_op jit(solution)/shard_map/ppermute | solution.py:17
  53.7 8.0 %leaf.1 = (f32[512,256]{1,0:T(8,128)}, f32[256,256]{1,0:T(8,128)S(1)}) custom-call(f32[256,512]{1,0:T(8,128)S(1)} %bitcast.7, f32[264,128]{1,0:T(8,128)S(1)} %pad_maximum_fusion.packed_ref.leaf_ref), custom_call_target="tpu_custom_call" | custom-call | tf_op jit(solution)/shard_map/leaf/pallas_call | solution.py:389
  61.7 0.0 collective-permute-done.near_ref
  61.7 1.9 %collective-permute-done.1.far_ref = f32[264,128]{1,0:T(8,128)S(1)} collective-permute-done((f32[264,128]{1,0:T(8,128)S(1)}, f32[264,128]{1,0:T(8,128)S(1)}, u32[]{:S(2)}, u32[]{:S(2)}) %collective-permute-start.1) | collective-permute-done | bytes 135200 | tf_op jit(solution)/shard_map/ppermute | solution.py:17
  63.6 0.0 collective-permute-done.2.last_ref
  63.6 9.8 %group.1 = (f32[256,256]{1,0:T(8,128)}, f32[128,256]{1,0:T(8,128)}, f32[64,256]{1,0:T(8,128)}) custom-call(s32[1]{0:T(128)} %bitcast.4.place_ref, f32[264,128]{1,0:T(8,128)S(1)} %pad_maximum_fusion.packed_ref.leaf_ref, f32[264,128]{1,0:T(8,128)S(1)} %collective-permute-done.near_ref, f32[264,128]{1,0:T(8,128)S(1)} %collective-permute-done.1.far_ref, ...), custom_call_target="tpu_custom_call" | custom-call | tf_op jit(solution)/shard_map/group/pallas_call | solution.py:401
  (3 shorter events, 0.1 us)
Async XLA Ops:
  2.8 24.3 %copy-start = (bf16[2,256,256]{2,1,0:T(8,128)(2,1)S(1)}, bf16[2,256,256]{2,1,0:T(8,128)(2,1)}, u32[]{:S(2)}) copy-start(bf16[2,256,256]{2,1,0:T(8,128)(2,1)} %constant.18.clone.first_ref) | copy-start | bytes 786436
  2.8 24.3 %copy-start.1 = (bf16[2,256,256]{2,1,0:T(8,128)(2,1)S(1)}, bf16[2,256,256]{2,1,0:T(8,128)(2,1)}, u32[]{:S(2)}) copy-start(bf16[2,256,256]{2,1,0:T(8,128)(2,1)} %constant.19.clone.first_t_ref) | copy-start | bytes 786436
  2.9 24.3 %copy-start.2 = (bf16[2,256,256]{2,1,0:T(8,128)(2,1)S(1)}, bf16[2,256,256]{2,1,0:T(8,128)(2,1)}, u32[]{:S(2)}) copy-start(bf16[2,256,256]{2,1,0:T(8,128)(2,1)} %constant.20.clone.second_ref) | copy-start | bytes 786436
  2.9 24.3 %copy-start.3 = (bf16[2,256,256]{2,1,0:T(8,128)(2,1)S(1)}, bf16[2,256,256]{2,1,0:T(8,128)(2,1)}, u32[]{:S(2)}) copy-start(bf16[2,256,256]{2,1,0:T(8,128)(2,1)} %constant.21.clone.second_t_ref) | copy-start | bytes 786436
  2.9 24.3 %copy-start.4 = (f32[2,128,128]{2,1,0:T(8,128)S(1)}, f32[2,128,128]{2,1,0:T(8,128)}, u32[]{:S(2)}) copy-start(f32[2,128,128]{2,1,0:T(8,128)} %constant.22.clone.turn_ref) | copy-start | bytes 393220
  48.6 13.1 %collective-permute-start = (f32[264,128]{1,0:T(8,128)S(1)}, f32[264,128]{1,0:T(8,128)S(1)}, u32[]{:S(2)}, u32[]{:S(2)}) collective-permute-start(f32[264,128]{1,0:T(8,128)S(1)} %pad_maximum_fusion.packed_ref.leaf_ref), channel_id=1, source_target_pairs={{0,1},{1,0},{2,3},{3,2},{4,5},{5,4},{6,7},{7,6},{8,9},{9,8},{10,11... | collective-permute-start | bytes 405512 | tf_op jit(solution)/shard_map/ppermute | solution.py:17
  51.2 12.4 %collective-permute-start.1 = (f32[264,128]{1,0:T(8,128)S(1)}, f32[264,128]{1,0:T(8,128)S(1)}, u32[]{:S(2)}, u32[]{:S(2)}) collective-permute-start(f32[264,128]{1,0:T(8,128)S(1)} %pad_maximum_fusion.packed_ref.leaf_ref), channel_id=1, source_target_pairs={{0,2},{1,3},{2,0},{3,1},{4,6},{5,7},{6,4},{7,5},{8,10},{9,11},{10,... | collective-permute-start | bytes 405512 | tf_op jit(solution)/shard_map/ppermute | solution.py:17
  52.1 11.6 %collective-permute-start.2 = (f32[264,128]{1,0:T(8,128)S(1)}, f32[264,128]{1,0:T(8,128)S(1)}, u32[]{:S(2)}, u32[]{:S(2)}) collective-permute-start(f32[264,128]{1,0:T(8,128)S(1)} %pad_maximum_fusion.packed_ref.leaf_ref), channel_id=1, source_target_pairs={{0,3},{1,2},{2,1},{3,0},{4,7},{5,6},{6,5},{7,4},{8,11},{9,10},{10,... | collective-permute-start | bytes 405512 | tf_op jit(solution)/shard_map/ppermute | solution.py:17

commit v8 on v7

--- a/solution.py
+++ b/solution.py
@@ -237,6 +237,30 @@
             ]
             for p in range(problems)
         ]
+
+    def stack(rows, order):
+        return jnp.concatenate(
+            [jnp.concatenate([row[q] for q in order], 0) for row in rows], 1
+        ).astype(jnp.bfloat16)
+
+    def outer(left, right):
+        return lax.dot_general(
+            left, right, (((0,), (0,)), ((), ())), preferred_element_type=jnp.float32
+        )
+
+    def defer(begin, end):
+        keep = iota((end - begin, LANES), 1) <= iota((end - begin, LANES), 0) + begin
+        for p in range(problems):
+            start = p * width
+            rows = [parts(done_ref[t, start + begin : start + end, :]) for t in range(tiles)]
+            left = stack(rows[1:], (0, 0, 1, 1, 0, 2))
+            rows[0] = [jnp.where(keep, x, 0.0) for x in rows[0]]
+            update = outer(left, stack(rows, (0, 1, 0, 1, 2, 0)))
+            for t in range(tiles):
+                tile_ref[t, start + LANES : start + width, :] = (
+                    tile_ref[t, start + LANES : start + width, :]
+                    - update[:, t * LANES : (t + 1) * LANES]
+                )
 
     panel = load(0)
     for base in range(0, width, block):
@@ -279,40 +303,31 @@
         if not more:
             break
         done, panel = panel, ahead
+        if base == LANES // 2 - block:
+            defer(0, LANES // 2)
+        if base == LANES - 2 * block:
+            defer(LANES // 2, LANES - block)
         past = after + block
-        if past == width:
+        stop = LANES if after < LANES else width
+        if past >= stop:
             continue
         first = past // LANES
         inverse = ~inside | (lane - offset <= sub)
-        below = iota((width - past, LANES), 1) - offset
+        below = iota((stop - past, LANES), 1) - offset
         below = (below >= 0) & (below < block)
         for p in range(problems):
             start = p * width
             rows = [parts(x) for x in done[p]]
-            left = jnp.concatenate(
-                [
-                    jnp.concatenate([rows[t][q] for q in (0, 0, 1, 1, 0, 2)], 0)
-                    for t in range(first, tiles)
-                ],
-                1,
-            ).astype(jnp.bfloat16)
+            left = stack(rows[first : pl.cdiv(stop, LANES)], (0, 0, 1, 1, 0, 2))
             rows[own] = [jnp.where(inverse, x, 0.0) for x in rows[own]]
-            right = jnp.concatenate(
-                [
-                    jnp.concatenate([rows[t][q] for q in (0, 1, 0, 1, 2, 0)], 0)
-                    for t in range(tiles)
-                ],
-                1,
-            ).astype(jnp.bfloat16)
-            update = lax.dot_general(
-                left, right, (((0,), (0,)), ((), ())), preferred_element_type=jnp.float32
-            )
+            update = outer(left, stack(rows, (0, 1, 0, 1, 2, 0)))
             for t in range(tiles):
-                old = tile_ref[t, start + past : start + width, :]
+                old = tile_ref[t, start + past : start + stop, :]
                 if t == own:
                     old = jnp.where(below, 0.0, old)
-                tile_ref[t, start + past : start + width, :] = (
-                    old - update[past - first * LANES :, t * LANES : (t + 1) * LANES]
+                tile_ref[t, start + past : start + stop, :] = (
+                    old
+                    - update[past - first * LANES : stop - first * LANES, t * LANES : (t + 1) * LANES]
                 )
 
 

time: 73.7 us -> 73.2 us (level)
  no operation moved by 1% of the time
where the time goes in v8:
time: 73.2 us; the launch traced here: 73 us
  blocking collectives  42.7 us (58%)
  Pallas kernels  21.9 us (30%)
  starting transfers between devices  5.05 us (7%)
  waiting for transfers between devices  1.97 us (3%)
    all_to_all x1, blocking collectives, local(): lax.all_to_all(spread(probes, spectrum, devices), axes, split_axis=0, con...  24.2 us
    all_to_all x1, blocking collectives, local(): lax.all_to_all(moved, axes, split_axis=0, concat_axis=0, tiled=True)  18.5 us
    pallas_call x1, Pallas kernels, group_factors(): pl.pallas_call(group_kernel, out_shape=[jax.ShapeDtypeStruct(shape, jnp.f...  9.4 us
    pallas_call x1, Pallas kernels, leaf_factor(): pl.pallas_call(leaf_kernel, out_shape=[jax.ShapeDtypeStruct(shape, jnp.fl...  7.97 us
    ppermute x3, starting transfers between devices, partner(): return lax.ppermute(value, axis, pairs)  5.05 us
    pallas_call x1, Pallas kernels, circulant(): pl.pallas_call(circulant_kernel(devices, split, width // devices, tiles -...  2.32 us
    pallas_call x1, Pallas kernels, spread(): pl.pallas_call(spread_kernel(per_dev, extra), out_shape=jax.ShapeDtypeStr...  2.22 us
    ppermute x3, waiting for transfers between devices, partner(): return lax.ppermute(value, axis, pairs)  1.97 us
  transfers between devices with their start and end apart: 3, of which 1 were waited for; matrix products, arithmetic and copies ran while one was open for 0% of the time, Pallas kernels for 11%

profile of v8, /device:TPU:0, one launch (start us, length us, event | category | flops | bytes accessed | tf_op | source)
XLA Modules:
  0.0 73.0 jit_solution(17407298196015552718)
XLA Ops:
  0.6 2.2 %spread.1 = f32[256,640]{1,0:T(8,128)} custom-call(f32[512,256]{1,0:T(8,128)} %probes_ref.1, f32[1,512]{1,0:T(1,128)} %spectrum_ref.1), custom_call_target="tpu_custom_call" | custom-call | tf_op jit(solution)/shard_map/spread/pallas_call | solution.py:98
  2.8 0.0 copy-start
  2.8 0.0 copy-start.1
  2.9 0.0 copy-start.2
  2.9 0.0 copy-start.3
  2.9 0.0 copy-start.4
  2.9 24.2 %all_to_all.22 = f32[32,8,640]{2,1,0:T(8,128)S(1)} all-to-all(f32[32,8,640]{2,1,0:T(8,128)} %bitcast.10), channel_id=1, replica_groups=mesh['row'=8,'col'=4] {'row','col'}, dimensions={0} | all-to-all | bytes 1310720 | tf_op jit(solution)/shard_map/all_to_all | solution.py:430
  27.1 0.0 copy-done
  27.1 0.0 copy-done.1
  27.1 0.0 copy-done.2
  27.1 0.0 copy-done.3
  27.1 0.0 copy-done.4
  27.1 2.3 %circulant.1 = f32[256,512]{1,0:T(8,128)S(1)} custom-call(f32[256,640]{1,0:T(8,128)S(1)} %bitcast.8, bf16[2,256,256]{2,1,0:T(8,128)(2,1)S(1)} %copy-done, bf16[2,256,256]{2,1,0:T(8,128)(2,1)S(1)} %copy-done.1, bf16[2,256,256]{2,1,0:T(8,128)(2,1)S(1)} %copy-done.2, bf16[2,256,256]{2,1,0:T(8,128)(2,1)S(1)} %copy-done.3, f32[2,128,128]{2,1,0:T(8,128)S(1)} %copy-done.4), custom_call_target="tpu_custom_call" | custom-call | tf_op jit(solution)/shard_map/circulant/pallas_call | solution.py:187
  29.5 18.5 %all_to_all.23 = f32[32,8,512]{2,1,0:T(8,128)S(1)} all-to-all(f32[32,8,512]{2,1,0:T(8,128)S(1)} %bitcast.9), channel_id=1, replica_groups=mesh['row'=8,'col'=4] {'row','col'}, dimensions={0} | all-to-all | bytes 1048576 | tf_op jit(solution)/shard_map/all_to_all | solution.py:434
  47.9 0.6 convolution_multiply_fusion
  48.6 2.6 %collective-permute-start = (f32[264,128]{1,0:T(8,128)S(1)}, f32[264,128]{1,0:T(8,128)S(1)}, u32[]{:S(2)}, u32[]{:S(2)}) collective-permute-start(f32[264,128]{1,0:T(8,128)S(1)} %pad_maximum_fusion.packed_ref.leaf_ref), channel_id=1, source_target_pairs={{0,1},{1,0},{2,3},{3,2},{4,5},{5,4},{6,7},{7,6},{8,9},{9,8},{10,11... | collective-permute-start | bytes 405512 | tf_op jit(solution)/shard_map/ppermute | solution.py:17
  51.2 0.8 %collective-permute-start.1 = (f32[264,128]{1,0:T(8,128)S(1)}, f32[264,128]{1,0:T(8,128)S(1)}, u32[]{:S(2)}, u32[]{:S(2)}) collective-permute-start(f32[264,128]{1,0:T(8,128)S(1)} %pad_maximum_fusion.packed_ref.leaf_ref), channel_id=1, source_target_pairs={{0,2},{1,3},{2,0},{3,1},{4,6},{5,7},{6,4},{7,5},{8,10},{9,11},{10,... | collective-permute-start | bytes 405512 | tf_op jit(solution)/shard_map/ppermute | solution.py:17
  52.1 1.6 %collective-permute-start.2 = (f32[264,128]{1,0:T(8,128)S(1)}, f32[264,128]{1,0:T(8,128)S(1)}, u32[]{:S(2)}, u32[]{:S(2)}) collective-permute-start(f32[264,128]{1,0:T(8,128)S(1)} %pad_maximum_fusion.packed_ref.leaf_ref), channel_id=1, source_target_pairs={{0,3},{1,2},{2,1},{3,0},{4,7},{5,6},{6,5},{7,4},{8,11},{9,10},{10,... | collective-permute-start | bytes 405512 | tf_op jit(solution)/shard_map/ppermute | solution.py:17
  53.7 8.0 %leaf.1 = (f32[512,256]{1,0:T(8,128)}, f32[256,256]{1,0:T(8,128)S(1)}) custom-call(f32[256,512]{1,0:T(8,128)S(1)} %bitcast.7, f32[264,128]{1,0:T(8,128)S(1)} %pad_maximum_fusion.packed_ref.leaf_ref), custom_call_target="tpu_custom_call" | custom-call | tf_op jit(solution)/shard_map/leaf/pallas_call | solution.py:404
  61.6 0.0 collective-permute-done.near_ref
  61.6 2.0 %collective-permute-done.1.far_ref = f32[264,128]{1,0:T(8,128)S(1)} collective-permute-done((f32[264,128]{1,0:T(8,128)S(1)}, f32[264,128]{1,0:T(8,128)S(1)}, u32[]{:S(2)}, u32[]{:S(2)}) %collective-permute-start.1) | collective-permute-done | bytes 135200 | tf_op jit(solution)/shard_map/ppermute | solution.py:17
  63.6 0.0 collective-permute-done.2.last_ref
  63.6 9.4 %group.1 = (f32[256,256]{1,0:T(8,128)}, f32[128,256]{1,0:T(8,128)}, f32[64,256]{1,0:T(8,128)}) custom-call(s32[1]{0:T(128)} %bitcast.4.place_ref, f32[264,128]{1,0:T(8,128)S(1)} %pad_maximum_fusion.packed_ref.leaf_ref, f32[264,128]{1,0:T(8,128)S(1)} %collective-permute-done.near_ref, f32[264,128]{1,0:T(8,128)S(1)} %collective-permute-done.1.far_ref, ...), custom_call_target="tpu_custom_call" | custom-call | tf_op jit(solution)/shard_map/group/pallas_call | solution.py:416
  (3 shorter events, 0.1 us)
Async XLA Ops:
  2.8 24.3 %copy-start = (bf16[2,256,256]{2,1,0:T(8,128)(2,1)S(1)}, bf16[2,256,256]{2,1,0:T(8,128)(2,1)}, u32[]{:S(2)}) copy-start(bf16[2,256,256]{2,1,0:T(8,128)(2,1)} %constant.18.clone.first_ref) | copy-start | bytes 786436
  2.8 24.3 %copy-start.1 = (bf16[2,256,256]{2,1,0:T(8,128)(2,1)S(1)}, bf16[2,256,256]{2,1,0:T(8,128)(2,1)}, u32[]{:S(2)}) copy-start(bf16[2,256,256]{2,1,0:T(8,128)(2,1)} %constant.19.clone.first_t_ref) | copy-start | bytes 786436
  2.9 24.3 %copy-start.2 = (bf16[2,256,256]{2,1,0:T(8,128)(2,1)S(1)}, bf16[2,256,256]{2,1,0:T(8,128)(2,1)}, u32[]{:S(2)}) copy-start(bf16[2,256,256]{2,1,0:T(8,128)(2,1)} %constant.20.clone.second_ref) | copy-start | bytes 786436
  2.9 24.3 %copy-start.3 = (bf16[2,256,256]{2,1,0:T(8,128)(2,1)S(1)}, bf16[2,256,256]{2,1,0:T(8,128)(2,1)}, u32[]{:S(2)}) copy-start(bf16[2,256,256]{2,1,0:T(8,128)(2,1)} %constant.21.clone.second_t_ref) | copy-start | bytes 786436
  2.9 24.3 %copy-start.4 = (f32[2,128,128]{2,1,0:T(8,128)S(1)}, f32[2,128,128]{2,1,0:T(8,128)}, u32[]{:S(2)}) copy-start(f32[2,128,128]{2,1,0:T(8,128)} %constant.22.clone.turn_ref) | copy-start | bytes 393220
  48.6 13.0 %collective-permute-start = (f32[264,128]{1,0:T(8,128)S(1)}, f32[264,128]{1,0:T(8,128)S(1)}, u32[]{:S(2)}, u32[]{:S(2)}) collective-permute-start(f32[264,128]{1,0:T(8,128)S(1)} %pad_maximum_fusion.packed_ref.leaf_ref), channel_id=1, source_target_pairs={{0,1},{1,0},{2,3},{3,2},{4,5},{5,4},{6,7},{7,6},{8,9},{9,8},{10,11... | collective-permute-start | bytes 405512 | tf_op jit(solution)/shard_map/ppermute | solution.py:17
  51.2 12.4 %collective-permute-start.1 = (f32[264,128]{1,0:T(8,128)S(1)}, f32[264,128]{1,0:T(8,128)S(1)}, u32[]{:S(2)}, u32[]{:S(2)}) collective-permute-start(f32[264,128]{1,0:T(8,128)S(1)} %pad_maximum_fusion.packed_ref.leaf_ref), channel_id=1, source_target_pairs={{0,2},{1,3},{2,0},{3,1},{4,6},{5,7},{6,4},{7,5},{8,10},{9,11},{10,... | collective-permute-start | bytes 405512 | tf_op jit(solution)/shard_map/ppermute | solution.py:17
  52.1 11.6 %collective-permute-start.2 = (f32[264,128]{1,0:T(8,128)S(1)}, f32[264,128]{1,0:T(8,128)S(1)}, u32[]{:S(2)}, u32[]{:S(2)}) collective-permute-start(f32[264,128]{1,0:T(8,128)S(1)} %pad_maximum_fusion.packed_ref.leaf_ref), channel_id=1, source_target_pairs={{0,3},{1,2},{2,1},{3,0},{4,7},{5,6},{6,5},{7,4},{8,11},{9,10},{10,... | collective-permute-start | bytes 405512 | tf_op jit(solution)/shard_map/ppermute | solution.py:17

commit v9 on v8

--- a/solution.py
+++ b/solution.py
@@ -39,6 +39,17 @@
 def product(left, right):
     def dot(i, j):
         return jnp.dot(left[i], right[j], preferred_element_type=jnp.float32)
+
+    return dot(0, 0) + (dot(0, 1) + dot(1, 0))
+
+
+def product_transpose(left, right):
+    left, right = split2(left), split2(right)
+
+    def dot(i, j):
+        return lax.dot_general(
+            left[i], right[j], (((1,), (1,)), ((), ())), preferred_element_type=jnp.float32
+        )
 
     return dot(0, 0) + (dot(0, 1) + dot(1, 0))
 
@@ -383,12 +394,12 @@
     eliminate(tile_ref, done_ref, 2, width)
     upper_ref[0], pair_inverse = factors(done_ref, 0, width)
     upper_ref[1], group_inverse = factors(done_ref, width, width)
-    leaf_transfer_ref[...] = times_transpose(leaf_upper_ref[...], pair_inverse)
+    leaf_transfer_ref[...] = product_transpose(leaf_upper_ref[...], pair_inverse)
     half = width // 2
     quarter = width // 4
     place = place_ref[0]
     pair_upper = upper_ref[0, pl.ds(pl.multiple_of(place % 2 * half, half), half), :]
-    pair_transfer_ref[...] = times_transpose(pair_upper, group_inverse)
+    pair_transfer_ref[...] = product_transpose(pair_upper, group_inverse)
     group_factor_ref[...] = upper_ref[
         1, pl.ds(pl.multiple_of(place % 4 * quarter, quarter), quarter), :
     ]

time: 73.2 us -> 73 us (level)
  no operation moved by 1% of the time
where the time goes in v9:
time: 73 us; the launch traced here: 72.8 us
  blocking collectives  42.7 us (58%)
  Pallas kernels  21.7 us (30%)
  starting transfers between devices  5.05 us (7%)
  waiting for transfers between devices  1.97 us (3%)
    all_to_all x1, blocking collectives, local(): lax.all_to_all(spread(probes, spectrum, devices), axes, split_axis=0, con...  24.2 us
    all_to_all x1, blocking collectives, local(): lax.all_to_all(moved, axes, split_axis=0, concat_axis=0, tiled=True)  18.5 us
    pallas_call x1, Pallas kernels, group_factors(): pl.pallas_call(group_kernel, out_shape=[jax.ShapeDtypeStruct(shape, jnp.f...  9.18 us
    pallas_call x1, Pallas kernels, leaf_factor(): pl.pallas_call(leaf_kernel, out_shape=[jax.ShapeDtypeStruct(shape, jnp.fl...  7.97 us
    ppermute x3, starting transfers between devices, partner(): return lax.ppermute(value, axis, pairs)  5.05 us
    pallas_call x1, Pallas kernels, circulant(): pl.pallas_call(circulant_kernel(devices, split, width // devices, tiles -...  2.32 us
    pallas_call x1, Pallas kernels, spread(): pl.pallas_call(spread_kernel(per_dev, extra), out_shape=jax.ShapeDtypeStr...  2.22 us
    ppermute x3, waiting for transfers between devices, partner(): return lax.ppermute(value, axis, pairs)  1.97 us
  transfers between devices with their start and end apart: 3, of which 1 were waited for; matrix products, arithmetic and copies ran while one was open for 0% of the time, Pallas kernels for 11%

profile of v9, /device:TPU:0, one launch (start us, length us, event | category | flops | bytes accessed | tf_op | source)
XLA Modules:
  0.0 72.8 jit_solution(5375079265586764583)
XLA Ops:
  0.6 2.2 %spread.1 = f32[256,640]{1,0:T(8,128)} custom-call(f32[512,256]{1,0:T(8,128)} %probes_ref.1, f32[1,512]{1,0:T(1,128)} %spectrum_ref.1), custom_call_target="tpu_custom_call" | custom-call | tf_op jit(solution)/shard_map/spread/pallas_call | solution.py:109
  2.8 0.0 copy-start
  2.8 0.0 copy-start.1
  2.9 0.0 copy-start.2
  2.9 0.0 copy-start.3
  2.9 0.0 copy-start.4
  2.9 24.2 %all_to_all.22 = f32[32,8,640]{2,1,0:T(8,128)S(1)} all-to-all(f32[32,8,640]{2,1,0:T(8,128)} %bitcast.10), channel_id=1, replica_groups=mesh['row'=8,'col'=4] {'row','col'}, dimensions={0} | all-to-all | bytes 1310720 | tf_op jit(solution)/shard_map/all_to_all | solution.py:441
  27.1 0.0 copy-done
  27.1 0.0 copy-done.1
  27.1 0.0 copy-done.2
  27.1 0.0 copy-done.3
  27.1 0.0 copy-done.4
  27.1 2.3 %circulant.1 = f32[256,512]{1,0:T(8,128)S(1)} custom-call(f32[256,640]{1,0:T(8,128)S(1)} %bitcast.8, bf16[2,256,256]{2,1,0:T(8,128)(2,1)S(1)} %copy-done, bf16[2,256,256]{2,1,0:T(8,128)(2,1)S(1)} %copy-done.1, bf16[2,256,256]{2,1,0:T(8,128)(2,1)S(1)} %copy-done.2, bf16[2,256,256]{2,1,0:T(8,128)(2,1)S(1)} %copy-done.3, f32[2,128,128]{2,1,0:T(8,128)S(1)} %copy-done.4), custom_call_target="tpu_custom_call" | custom-call | tf_op jit(solution)/shard_map/circulant/pallas_call | solution.py:198
  29.5 18.5 %all_to_all.23 = f32[32,8,512]{2,1,0:T(8,128)S(1)} all-to-all(f32[32,8,512]{2,1,0:T(8,128)S(1)} %bitcast.9), channel_id=1, replica_groups=mesh['row'=8,'col'=4] {'row','col'}, dimensions={0} | all-to-all | bytes 1048576 | tf_op jit(solution)/shard_map/all_to_all | solution.py:445
  47.9 0.6 convolution_multiply_fusion
  48.6 2.6 %collective-permute-start = (f32[264,128]{1,0:T(8,128)S(1)}, f32[264,128]{1,0:T(8,128)S(1)}, u32[]{:S(2)}, u32[]{:S(2)}) collective-permute-start(f32[264,128]{1,0:T(8,128)S(1)} %pad_maximum_fusion.packed_ref.leaf_ref), channel_id=1, source_target_pairs={{0,1},{1,0},{2,3},{3,2},{4,5},{5,4},{6,7},{7,6},{8,9},{9,8},{10,11... | collective-permute-start | bytes 405512 | tf_op jit(solution)/shard_map/ppermute | solution.py:17
  51.2 0.8 %collective-permute-start.1 = (f32[264,128]{1,0:T(8,128)S(1)}, f32[264,128]{1,0:T(8,128)S(1)}, u32[]{:S(2)}, u32[]{:S(2)}) collective-permute-start(f32[264,128]{1,0:T(8,128)S(1)} %pad_maximum_fusion.packed_ref.leaf_ref), channel_id=1, source_target_pairs={{0,2},{1,3},{2,0},{3,1},{4,6},{5,7},{6,4},{7,5},{8,10},{9,11},{10,... | collective-permute-start | bytes 405512 | tf_op jit(solution)/shard_map/ppermute | solution.py:17
  52.1 1.6 %collective-permute-start.2 = (f32[264,128]{1,0:T(8,128)S(1)}, f32[264,128]{1,0:T(8,128)S(1)}, u32[]{:S(2)}, u32[]{:S(2)}) collective-permute-start(f32[264,128]{1,0:T(8,128)S(1)} %pad_maximum_fusion.packed_ref.leaf_ref), channel_id=1, source_target_pairs={{0,3},{1,2},{2,1},{3,0},{4,7},{5,6},{6,5},{7,4},{8,11},{9,10},{10,... | collective-permute-start | bytes 405512 | tf_op jit(solution)/shard_map/ppermute | solution.py:17
  53.7 8.0 %leaf.1 = (f32[512,256]{1,0:T(8,128)}, f32[256,256]{1,0:T(8,128)S(1)}) custom-call(f32[256,512]{1,0:T(8,128)S(1)} %bitcast.7, f32[264,128]{1,0:T(8,128)S(1)} %pad_maximum_fusion.packed_ref.leaf_ref), custom_call_target="tpu_custom_call" | custom-call | tf_op jit(solution)/shard_map/leaf/pallas_call | solution.py:415
  61.6 0.0 collective-permute-done.near_ref
  61.6 2.0 %collective-permute-done.1.far_ref = f32[264,128]{1,0:T(8,128)S(1)} collective-permute-done((f32[264,128]{1,0:T(8,128)S(1)}, f32[264,128]{1,0:T(8,128)S(1)}, u32[]{:S(2)}, u32[]{:S(2)}) %collective-permute-start.1) | collective-permute-done | bytes 135200 | tf_op jit(solution)/shard_map/ppermute | solution.py:17
  63.6 0.0 collective-permute-done.2.last_ref
  63.6 9.2 %group.1 = (f32[256,256]{1,0:T(8,128)}, f32[128,256]{1,0:T(8,128)}, f32[64,256]{1,0:T(8,128)}) custom-call(s32[1]{0:T(128)} %bitcast.4.place_ref, f32[264,128]{1,0:T(8,128)S(1)} %pad_maximum_fusion.packed_ref.leaf_ref, f32[264,128]{1,0:T(8,128)S(1)} %collective-permute-done.near_ref, f32[264,128]{1,0:T(8,128)S(1)} %collective-permute-done.1.far_ref, ...), custom_call_target="tpu_custom_call" | custom-call | tf_op jit(solution)/shard_map/group/pallas_call | solution.py:427
  (3 shorter events, 0.1 us)
Async XLA Ops:
  2.8 24.3 %copy-start = (bf16[2,256,256]{2,1,0:T(8,128)(2,1)S(1)}, bf16[2,256,256]{2,1,0:T(8,128)(2,1)}, u32[]{:S(2)}) copy-start(bf16[2,256,256]{2,1,0:T(8,128)(2,1)} %constant.18.clone.first_ref) | copy-start | bytes 786436
  2.8 24.3 %copy-start.1 = (bf16[2,256,256]{2,1,0:T(8,128)(2,1)S(1)}, bf16[2,256,256]{2,1,0:T(8,128)(2,1)}, u32[]{:S(2)}) copy-start(bf16[2,256,256]{2,1,0:T(8,128)(2,1)} %constant.19.clone.first_t_ref) | copy-start | bytes 786436
  2.9 24.3 %copy-start.2 = (bf16[2,256,256]{2,1,0:T(8,128)(2,1)S(1)}, bf16[2,256,256]{2,1,0:T(8,128)(2,1)}, u32[]{:S(2)}) copy-start(bf16[2,256,256]{2,1,0:T(8,128)(2,1)} %constant.20.clone.second_ref) | copy-start | bytes 786436
  2.9 24.3 %copy-start.3 = (bf16[2,256,256]{2,1,0:T(8,128)(2,1)S(1)}, bf16[2,256,256]{2,1,0:T(8,128)(2,1)}, u32[]{:S(2)}) copy-start(bf16[2,256,256]{2,1,0:T(8,128)(2,1)} %constant.21.clone.second_t_ref) | copy-start | bytes 786436
  2.9 24.3 %copy-start.4 = (f32[2,128,128]{2,1,0:T(8,128)S(1)}, f32[2,128,128]{2,1,0:T(8,128)}, u32[]{:S(2)}) copy-start(f32[2,128,128]{2,1,0:T(8,128)} %constant.22.clone.turn_ref) | copy-start | bytes 393220
  48.6 13.0 %collective-permute-start = (f32[264,128]{1,0:T(8,128)S(1)}, f32[264,128]{1,0:T(8,128)S(1)}, u32[]{:S(2)}, u32[]{:S(2)}) collective-permute-start(f32[264,128]{1,0:T(8,128)S(1)} %pad_maximum_fusion.packed_ref.leaf_ref), channel_id=1, source_target_pairs={{0,1},{1,0},{2,3},{3,2},{4,5},{5,4},{6,7},{7,6},{8,9},{9,8},{10,11... | collective-permute-start | bytes 405512 | tf_op jit(solution)/shard_map/ppermute | solution.py:17
  51.2 12.4 %collective-permute-start.1 = (f32[264,128]{1,0:T(8,128)S(1)}, f32[264,128]{1,0:T(8,128)S(1)}, u32[]{:S(2)}, u32[]{:S(2)}) collective-permute-start(f32[264,128]{1,0:T(8,128)S(1)} %pad_maximum_fusion.packed_ref.leaf_ref), channel_id=1, source_target_pairs={{0,2},{1,3},{2,0},{3,1},{4,6},{5,7},{6,4},{7,5},{8,10},{9,11},{10,... | collective-permute-start | bytes 405512 | tf_op jit(solution)/shard_map/ppermute | solution.py:17
  52.1 11.6 %collective-permute-start.2 = (f32[264,128]{1,0:T(8,128)S(1)}, f32[264,128]{1,0:T(8,128)S(1)}, u32[]{:S(2)}, u32[]{:S(2)}) collective-permute-start(f32[264,128]{1,0:T(8,128)S(1)} %pad_maximum_fusion.packed_ref.leaf_ref), channel_id=1, source_target_pairs={{0,3},{1,2},{2,1},{3,0},{4,7},{5,6},{6,5},{7,4},{8,11},{9,10},{10,... | collective-permute-start | bytes 405512 | tf_op jit(solution)/shard_map/ppermute | solution.py:17

commit v10 on v9

--- a/solution.py
+++ b/solution.py
@@ -376,9 +376,9 @@
 def group_kernel(
     place_ref,
     leaf_ref,
+    last_ref,
+    far_ref,
     near_ref,
-    far_ref,
-    last_ref,
     leaf_upper_ref,
     leaf_transfer_ref,
     pair_transfer_ref,
@@ -432,7 +432,7 @@
         scratch_shapes=scratch(2, width) + [pltpu.VMEM((2, width, width), jnp.float32)],
         compiler_params=pltpu.CompilerParams(vmem_limit_bytes=24 << 20),
         name="group",
-    )(place, leaf, near, far, last, leaf_upper)
+    )(place, leaf, last, far, near, leaf_upper)
 
 
 def local(probes, spectrum):
@@ -444,7 +444,7 @@
     moved = circulant(columns, probes.shape[0], devices)
     sample_t = lax.all_to_all(moved, axes, split_axis=0, concat_axis=0, tiled=True)
     leaf = packed_gram(sample_t)
-    far, last, near = (partner(leaf, "col", mask) for mask in (2, 3, 1))
+    last, far, near = (partner(leaf, "col", mask) for mask in (3, 2, 1))
     leaf_basis, leaf_upper = leaf_factor(sample_t, leaf)
     place = lax.axis_index("col").reshape(1).astype(jnp.int32)
     return (leaf_basis, *group_factors(place, leaf, near, far, last, leaf_upper))

time: 73 us -> 73.6 us (level)
  waiting for transfers between devices: 1.97 us -> 3.14 us
    ppermute x3, waiting for transfers between devices: 1.97 us -> 3.14 us  [partner(): return lax.ppermute(value, axis, pairs)]
where the time goes in v10:
time: 73.6 us; the launch traced here: 73.4 us
  blocking collectives  42.7 us (58%)
  Pallas kernels  21.7 us (29%)
  starting transfers between devices  4.45 us (6%)
  waiting for transfers between devices  3.14 us (4%)
    all_to_all x1, blocking collectives, local(): lax.all_to_all(spread(probes, spectrum, devices), axes, split_axis=0, con...  24.2 us
    all_to_all x1, blocking collectives, local(): lax.all_to_all(moved, axes, split_axis=0, concat_axis=0, tiled=True)  18.5 us
    pallas_call x1, Pallas kernels, group_factors(): pl.pallas_call(group_kernel, out_shape=[jax.ShapeDtypeStruct(shape, jnp.f...  9.17 us
    pallas_call x1, Pallas kernels, leaf_factor(): pl.pallas_call(leaf_kernel, out_shape=[jax.ShapeDtypeStruct(shape, jnp.fl...  7.97 us
    ppermute x3, starting transfers between devices, partner(): return lax.ppermute(value, axis, pairs)  4.45 us
    ppermute x3, waiting for transfers between devices, partner(): return lax.ppermute(value, axis, pairs)  3.14 us
    pallas_call x1, Pallas kernels, circulant(): pl.pallas_call(circulant_kernel(devices, split, width // devices, tiles -...  2.32 us
    pallas_call x1, Pallas kernels, spread(): pl.pallas_call(spread_kernel(per_dev, extra), out_shape=jax.ShapeDtypeStr...  2.22 us
  transfers between devices with their start and end apart: 3, of which 1 were waited for; matrix products, arithmetic and copies ran while one was open for 0% of the time, Pallas kernels for 11%

profile of v10, /device:TPU:0, one launch (start us, length us, event | category | flops | bytes accessed | tf_op | source)
XLA Modules:
  0.0 73.4 jit_solution(16806352399071891521)
XLA Ops:
  0.6 2.2 %spread.1 = f32[256,640]{1,0:T(8,128)} custom-call(f32[512,256]{1,0:T(8,128)} %probes_ref.1, f32[1,512]{1,0:T(1,128)} %spectrum_ref.1), custom_call_target="tpu_custom_call" | custom-call | tf_op jit(solution)/shard_map/spread/pallas_call | solution.py:109
  2.8 0.0 copy-start
  2.8 0.0 copy-start.1
  2.9 0.0 copy-start.2
  2.9 0.0 copy-start.3
  2.9 0.0 copy-start.4
  2.9 24.2 %all_to_all.22 = f32[32,8,640]{2,1,0:T(8,128)S(1)} all-to-all(f32[32,8,640]{2,1,0:T(8,128)} %bitcast.10), channel_id=1, replica_groups=mesh['row'=8,'col'=4] {'row','col'}, dimensions={0} | all-to-all | bytes 1310720 | tf_op jit(solution)/shard_map/all_to_all | solution.py:441
  27.1 0.0 copy-done
  27.1 0.0 copy-done.1
  27.1 0.0 copy-done.2
  27.1 0.0 copy-done.3
  27.1 0.0 copy-done.4
  27.1 2.3 %circulant.1 = f32[256,512]{1,0:T(8,128)S(1)} custom-call(f32[256,640]{1,0:T(8,128)S(1)} %bitcast.8, bf16[2,256,256]{2,1,0:T(8,128)(2,1)S(1)} %copy-done, bf16[2,256,256]{2,1,0:T(8,128)(2,1)S(1)} %copy-done.1, bf16[2,256,256]{2,1,0:T(8,128)(2,1)S(1)} %copy-done.2, bf16[2,256,256]{2,1,0:T(8,128)(2,1)S(1)} %copy-done.3, f32[2,128,128]{2,1,0:T(8,128)S(1)} %copy-done.4), custom_call_target="tpu_custom_call" | custom-call | tf_op jit(solution)/shard_map/circulant/pallas_call | solution.py:198
  29.5 18.5 %all_to_all.23 = f32[32,8,512]{2,1,0:T(8,128)S(1)} all-to-all(f32[32,8,512]{2,1,0:T(8,128)S(1)} %bitcast.9), channel_id=1, replica_groups=mesh['row'=8,'col'=4] {'row','col'}, dimensions={0} | all-to-all | bytes 1048576 | tf_op jit(solution)/shard_map/all_to_all | solution.py:445
  47.9 0.6 convolution_multiply_fusion
  48.6 2.9 %collective-permute-start = (f32[264,128]{1,0:T(8,128)S(1)}, f32[264,128]{1,0:T(8,128)S(1)}, u32[]{:S(2)}, u32[]{:S(2)}) collective-permute-start(f32[264,128]{1,0:T(8,128)S(1)} %pad_maximum_fusion.packed_ref.leaf_ref), channel_id=1, source_target_pairs={{0,3},{1,2},{2,1},{3,0},{4,7},{5,6},{6,5},{7,4},{8,11},{9,10},{10,... | collective-permute-start | bytes 405512 | tf_op jit(solution)/shard_map/ppermute | solution.py:17
  51.5 1.2 %collective-permute-start.1 = (f32[264,128]{1,0:T(8,128)S(1)}, f32[264,128]{1,0:T(8,128)S(1)}, u32[]{:S(2)}, u32[]{:S(2)}) collective-permute-start(f32[264,128]{1,0:T(8,128)S(1)} %pad_maximum_fusion.packed_ref.leaf_ref), channel_id=1, source_target_pairs={{0,2},{1,3},{2,0},{3,1},{4,6},{5,7},{6,4},{7,5},{8,10},{9,11},{10,... | collective-permute-start | bytes 405512 | tf_op jit(solution)/shard_map/ppermute | solution.py:17
  52.7 0.4 collective-permute-start.2
  53.1 8.0 %leaf.1 = (f32[512,256]{1,0:T(8,128)}, f32[256,256]{1,0:T(8,128)S(1)}) custom-call(f32[256,512]{1,0:T(8,128)S(1)} %bitcast.7, f32[264,128]{1,0:T(8,128)S(1)} %pad_maximum_fusion.packed_ref.leaf_ref), custom_call_target="tpu_custom_call" | custom-call | tf_op jit(solution)/shard_map/leaf/pallas_call | solution.py:415
  61.0 0.0 collective-permute-done.last_ref
  61.1 3.1 %collective-permute-done.1.far_ref = f32[264,128]{1,0:T(8,128)S(1)} collective-permute-done((f32[264,128]{1,0:T(8,128)S(1)}, f32[264,128]{1,0:T(8,128)S(1)}, u32[]{:S(2)}, u32[]{:S(2)}) %collective-permute-start.1) | collective-permute-done | bytes 135200 | tf_op jit(solution)/shard_map/ppermute | solution.py:17
  64.2 0.0 collective-permute-done.2.near_ref
  64.2 9.2 %group.1 = (f32[256,256]{1,0:T(8,128)}, f32[128,256]{1,0:T(8,128)}, f32[64,256]{1,0:T(8,128)}) custom-call(s32[1]{0:T(128)} %bitcast.4.place_ref, f32[264,128]{1,0:T(8,128)S(1)} %pad_maximum_fusion.packed_ref.leaf_ref, f32[264,128]{1,0:T(8,128)S(1)} %collective-permute-done.last_ref, f32[264,128]{1,0:T(8,128)S(1)} %collective-permute-done.1.far_ref, ...), custom_call_target="tpu_custom_call" | custom-call | tf_op jit(solution)/shard_map/group/pallas_call | solution.py:427
  (3 shorter events, 0.1 us)
Async XLA Ops:
  2.8 24.3 %copy-start = (bf16[2,256,256]{2,1,0:T(8,128)(2,1)S(1)}, bf16[2,256,256]{2,1,0:T(8,128)(2,1)}, u32[]{:S(2)}) copy-start(bf16[2,256,256]{2,1,0:T(8,128)(2,1)} %constant.18.clone.first_ref) | copy-start | bytes 786436
  2.8 24.3 %copy-start.1 = (bf16[2,256,256]{2,1,0:T(8,128)(2,1)S(1)}, bf16[2,256,256]{2,1,0:T(8,128)(2,1)}, u32[]{:S(2)}) copy-start(bf16[2,256,256]{2,1,0:T(8,128)(2,1)} %constant.19.clone.first_t_ref) | copy-start | bytes 786436
  2.9 24.3 %copy-start.2 = (bf16[2,256,256]{2,1,0:T(8,128)(2,1)S(1)}, bf16[2,256,256]{2,1,0:T(8,128)(2,1)}, u32[]{:S(2)}) copy-start(bf16[2,256,256]{2,1,0:T(8,128)(2,1)} %constant.20.clone.second_ref) | copy-start | bytes 786436
  2.9 24.3 %copy-start.3 = (bf16[2,256,256]{2,1,0:T(8,128)(2,1)S(1)}, bf16[2,256,256]{2,1,0:T(8,128)(2,1)}, u32[]{:S(2)}) copy-start(bf16[2,256,256]{2,1,0:T(8,128)(2,1)} %constant.21.clone.second_t_ref) | copy-start | bytes 786436
  2.9 24.3 %copy-start.4 = (f32[2,128,128]{2,1,0:T(8,128)S(1)}, f32[2,128,128]{2,1,0:T(8,128)}, u32[]{:S(2)}) copy-start(f32[2,128,128]{2,1,0:T(8,128)} %constant.22.clone.turn_ref) | copy-start | bytes 393220
  48.6 12.4 %collective-permute-start = (f32[264,128]{1,0:T(8,128)S(1)}, f32[264,128]{1,0:T(8,128)S(1)}, u32[]{:S(2)}, u32[]{:S(2)}) collective-permute-start(f32[264,128]{1,0:T(8,128)S(1)} %pad_maximum_fusion.packed_ref.leaf_ref), channel_id=1, source_target_pairs={{0,3},{1,2},{2,1},{3,0},{4,7},{5,6},{6,5},{7,4},{8,11},{9,10},{10,... | collective-permute-start | bytes 405512 | tf_op jit(solution)/shard_map/ppermute | solution.py:17
  51.5 12.7 %collective-permute-start.1 = (f32[264,128]{1,0:T(8,128)S(1)}, f32[264,128]{1,0:T(8,128)S(1)}, u32[]{:S(2)}, u32[]{:S(2)}) collective-permute-start(f32[264,128]{1,0:T(8,128)S(1)} %pad_maximum_fusion.packed_ref.leaf_ref), channel_id=1, source_target_pairs={{0,2},{1,3},{2,0},{3,1},{4,6},{5,7},{6,4},{7,5},{8,10},{9,11},{10,... | collective-permute-start | bytes 405512 | tf_op jit(solution)/shard_map/ppermute | solution.py:17
  52.7 11.5 %collective-permute-start.2 = (f32[264,128]{1,0:T(8,128)S(1)}, f32[264,128]{1,0:T(8,128)S(1)}, u32[]{:S(2)}, u32[]{:S(2)}) collective-permute-start(f32[264,128]{1,0:T(8,128)S(1)} %pad_maximum_fusion.packed_ref.leaf_ref), channel_id=1, source_target_pairs={{0,1},{1,0},{2,3},{3,2},{4,5},{5,4},{6,7},{7,6},{8,9},{9,8},{10,11... | collective-permute-start | bytes 405512 | tf_op jit(solution)/shard_map/ppermute | solution.py:17
